TPU v7x, 512 devices: a whole 4x4x16 slice. The times are simulated.
512 devices in a mesh: ctx: 64 (over y_hi, z, core), head: 8 (over x, y_lo).
Axes of the slice: x: 4, y: 4 (y_hi: 2, y_lo: 2; y = y_hi * 2 + y_lo), z: 16, core: 2. Of those that a mesh axis runs over, the one named last changes fastest.
Arguments:
- clean_latents: bfloat16 [128, 4, 8, 128], P('ctx'), may hold values from -6 to 6
- noise: bfloat16 [128, 4, 8, 128], P('ctx'), may hold values from -6 to 6
- timesteps: int32 [128], P('ctx'), may hold values from 0 to 999
- span_order: int32 [128], P('ctx'), may hold values from 0 to 127, as said below
- valid_frames: int32 [128], P('ctx'), may hold values from 1 to 4
- embed_weight: bfloat16 [256, 6144], P(None, 'head'), may hold values from -0.375 to 0.375
- position: bfloat16 [8192, 6144], P('ctx'), may hold values from -6 to 6
- norm_gain: bfloat16 [6144], replicated, may hold values from 0.099609375 to 1.8984375
- query_weight: bfloat16 [6144, 3072], P('ctx', 'head'), as said below
- kv_weight: bfloat16 [6144, 2048], P('ctx', 'head'), as said below
Outputs:
- attended: bfloat16 [8192, 3072], P('ctx', 'head')
Inputs may be any that keep to these rules, and one draw needn't show every extreme that they name: `span_order`: span slots 2d and 2d + 1 hold spans p and 127 - p for some p, in either order; each span number stands once. `query_weight`: entries scale with the fan-in 6144. `kv_weight`: entries scale with the fan-in 6144.
All inputs are finite; a program needn't handle non-finite values.
Results may differ from a plain program's by a relative error of at most 0.012.
The roundings to bfloat16 on the way count: a program that leaves them out, or rounds other values in their place, can miss the bound.
Values may be sent and summed in bfloat16 or wider, within the bound.
No kernel may reach another device: no remote copies, remote signals or barrier semaphores. Data moves between devices by JAX's collectives and lax.ppermute only.
A program may use at most 64 MiB of HBM per device.

v0:
```python
import math

import jax
import jax.numpy as jnp
from jax import lax
from jax.sharding import PartitionSpec as P

HD = 128
CH = 16


eps_norm = 1e-06
masked_low = -1e30


def make_patches(latents):
    slots, frames, height, flat = latents.shape
    width = flat // CH
    grid = latents.reshape(slots, frames, height, width, CH)
    padded = jnp.pad(grid, ((0, 0), (0, 0), (1, 1), (1, 1), (0, 0)))
    half_rows = height // 2
    half_cols = width // 2
    split = padded.reshape(slots, frames, half_rows + 1, 2, half_cols + 1, 2, CH)
    offsets_list = []
    for row_off in range(4):
        for col_off in range(4):
            offsets_list.append(
                split[
                    :,
                    :,
                    row_off // 2 : row_off // 2 + half_rows,
                    row_off % 2,
                    col_off // 2 : col_off // 2 + half_cols,
                    col_off % 2,
                    :,
                ]
            )
    stacked = jnp.stack(offsets_list, axis=4)
    return stacked.reshape(slots * frames * half_rows * half_cols, 16 * CH)


def rms_normalize(values, gain):
    wide = values.astype(jnp.float32)
    factor = lax.rsqrt(jnp.mean(wide * wide, axis=-1, keepdims=True) + eps_norm)
    return (wide * factor * gain.astype(jnp.float32)).astype(jnp.bfloat16)


def attend(carry, query_heads, kv_block, allowed):
    largest, total, summed = carry
    local_heads = query_heads.shape[1]
    blocks = kv_block.reshape(kv_block.shape[0], local_heads, 2, HD)
    scores = jnp.einsum(
        "tkgd,nkd->tkgn", query_heads, blocks[:, :, 0], preferred_element_type=jnp.float32
    ) * HD ** (-0.5)
    mask = allowed[:, None, None, :]
    lowered = jnp.where(mask, scores, masked_low)
    new_largest = jnp.maximum(largest, jnp.max(lowered, axis=-1))
    raw = jnp.where(mask, jnp.exp(lowered - new_largest[..., None]), 0.0)
    factor = jnp.exp(largest - new_largest)
    total = total * factor + jnp.sum(raw, axis=-1)
    summed = summed * factor[..., None] + jnp.einsum(
        "tkgn,nkd->tkgd",
        raw.astype(jnp.bfloat16),
        blocks[:, :, 1],
        preferred_element_type=jnp.float32,
    )
    return (new_largest, total, summed)


def expand_rows(values, span_rows):
    return (values[:, None] + jnp.zeros((1, span_rows), jnp.int32)).reshape(
        values.shape[0] * span_rows
    )


def add_position(projected, position_rows, tokens):
    cols = projected.shape[1]
    doubled = projected.reshape(2, tokens, cols) + position_rows.astype(jnp.float32)[None]
    return doubled.reshape(2 * tokens, cols).astype(jnp.bfloat16)


def on_device(
    clean_latents,
    noise,
    timesteps,
    span_order,
    valid_frames,
    embed_weight,
    position,
    norm_gain,
    query_weight,
    kv_weight,
):
    slots = clean_latents.shape[0]
    frames = clean_latents.shape[1]
    frame_rows = clean_latents.shape[2] // 2 * (clean_latents.shape[3] // (2 * CH))
    span_rows = frames * frame_rows
    tokens = slots * span_rows
    level = ((timesteps.astype(jnp.float32) + 1.0) / 1000.0)[:, None, None, None]
    noisy_latents = (
        (1.0 - level) * clean_latents.astype(jnp.float32) + level * noise.astype(jnp.float32)
    ).astype(jnp.bfloat16)
    patches = jnp.concatenate([make_patches(noisy_latents), make_patches(clean_latents)], axis=0)
    col_count = embed_weight.shape[1]
    col_start = lax.axis_index("head") * col_count
    position_cols = lax.dynamic_slice_in_dim(position, col_start, col_count, 1)
    projected = jnp.dot(patches, embed_weight, preferred_element_type=jnp.float32)
    partial_cols = add_position(projected, position_cols, tokens)
    embedded = lax.all_gather(partial_cols, "head", axis=1, tiled=True)
    normed = rms_normalize(embedded, norm_gain)
    normed_noisy = normed[:tokens]
    query_cols = query_weight.shape[1]
    kv_cols = kv_weight.shape[1]
    local_heads = kv_cols // (2 * HD)
    group_size = query_cols // (local_heads * HD)
    row_ids = jnp.arange(tokens, dtype=jnp.int32)
    query_slot = row_ids // span_rows
    query_frame = row_ids % span_rows // frame_rows
    query_span = expand_rows(span_order, span_rows)
    query_valid = expand_rows(valid_frames, span_rows)
    query_live = query_frame < query_valid

    def fold_block(carry, query_heads, kv_piece, order_piece, valid_piece):
        rows = kv_piece.shape[0]
        key_span = expand_rows(order_piece, span_rows)
        key_valid = expand_rows(valid_piece, span_rows)
        key_frame = jnp.arange(rows, dtype=jnp.int32) % span_rows // frame_rows
        allowed = (key_span[None, :] < query_span[:, None]) & (key_frame < key_valid)[None, :]
        return attend(carry, query_heads, kv_piece, allowed)

    start_carry = (
        jnp.full((tokens, local_heads, group_size), masked_low, jnp.float32),
        jnp.zeros((tokens, local_heads, group_size), jnp.float32),
        jnp.zeros((tokens, local_heads, group_size, HD), jnp.float32),
    )
    own_allowed = (query_slot[:, None] == query_slot[None, :]) & query_live[None, :]
    columns = normed_noisy
    query_sum = jnp.dot(
        columns,
        lax.all_gather(query_weight, "ctx", axis=0, tiled=True),
        preferred_element_type=jnp.float32,
    )
    columns = normed
    kv_sum = jnp.dot(
        columns,
        lax.all_gather(kv_weight, "ctx", axis=0, tiled=True),
        preferred_element_type=jnp.float32,
    )
    query_heads = query_sum.astype(jnp.bfloat16).reshape(tokens, local_heads, group_size, HD)
    keys_values = kv_sum.astype(jnp.bfloat16)
    carry = attend(start_carry, query_heads, keys_values[:tokens], own_allowed)
    piece = (
        lax.all_gather(keys_values[tokens:], "ctx", axis=0, tiled=True),
        lax.all_gather(span_order, "ctx", axis=0, tiled=True),
        lax.all_gather(valid_frames, "ctx", axis=0, tiled=True),
    )
    kv_all = piece[0]
    order_all = piece[1]
    valid_all = piece[2]
    all_spans = order_all.shape[0]
    block_spans = math.gcd(all_spans, max(1, 1024 // span_rows))
    block_count = all_spans // block_spans
    kv_blocks = kv_all.reshape(block_count, block_spans * span_rows, kv_cols)
    order_blocks = order_all.reshape(block_count, block_spans)
    valid_blocks = valid_all.reshape(block_count, block_spans)

    def scan_step(state, piece):
        return (fold_block(state, query_heads, piece[0], piece[1], piece[2]), None)

    result, unused = lax.scan(scan_step, carry, (kv_blocks, order_blocks, valid_blocks))
    carry = result
    largest, total, summed = carry
    result = summed / total[..., None]
    result = jnp.where(query_live[:, None, None, None], result, 0.0)
    return result.reshape(tokens, query_cols).astype(jnp.bfloat16)


def solution(mesh):
    return jax.shard_map(
        on_device,
        mesh=mesh,
        in_specs=(
            P("ctx", None, None, None),
            P("ctx", None, None, None),
            P("ctx"),
            P("ctx"),
            P("ctx"),
            P(None, "head"),
            P("ctx", None),
            P(),
            P("ctx", "head"),
            P("ctx", "head"),
        ),
        out_specs=P("ctx", "head"),
        check_vma=False,
    )
```

profile of v0, /device:TPU:1, one launch (start us, length us, event | category | flops | bytes accessed | tf_op | source)
XLA Modules:
  0.0 587.3 jit_solution(14975481105577285705)
XLA Ops:
  6.6 0.9 reshape.412
  8.1 0.3 copy.86
  8.4 0.5 reshape.414
  9.8 0.3 copy.68
  10.1 0.5 reshape.411
  10.6 1.0 dynamic-slice_convert_fusion
  11.6 1.0 fusion.27
  12.7 0.7 all-gather.7.cloned.1.call-update
  13.5 0.7 all-gather.9.cloned.1.call-update
  14.2 0.6 convert_element_type.58
  14.8 81.0 %all-gather.5.cloned.1.call-done = bf16[256,6144]{1,0:T(8,128)(2,1)} async-done(((bf16[256,768]{1,0:T(8,128)(2,1)}), bf16[256,6144]{1,0:T(8,128)(2,1)}) %all-gather.5.cloned.1.call-update) | async-done | bytes 3145744 | tf_op jit(solution)/shard_map/all_gather | solution.py:109
  95.8 2.7 fusion.22
  98.7 1.8 fusion.24
  100.5 148.0 %all-gather.7.cloned.1.call-done = bf16[6144,256]{1,0:T(8,128)(2,1)} async-done(((bf16[96,256]{1,0:T(8,128)(2,1)}), bf16[6144,256]{1,0:T(8,128)(2,1)}) %all-gather.7.cloned.1.call-update) | async-done | bytes 3145744 | tf_op jit(solution)/shard_map/all_gather | solution.py:146
  248.5 3.2 convolution_convert_fusion
  251.7 0.7 fusion.50
  252.6 1.3 dynamic-slice
  254.5 0.5 jit_remainder_.8.clone.1
  255.0 1.3 dynamic-update-slice.1
  256.5 17.4 %all-reduce.4 = (s32[128]{0:T(128)S(1)}, s32[128]{0:T(128)S(1)}) all-reduce(s32[128]{0:T(128)S(1)} %dynamic-update-slice, s32[128]{0:T(128)} %dynamic-update-slice.1), channel_id=1, replica_groups=mesh['ctx'=64,'head'=8] {'ctx'}, use_global_device_ids=true, to_apply=%add.2 | all-reduce | flops 256 | bytes 2048
  273.9 0.7 reshape.420
  274.6 0.7 reshape.421
  275.3 0.5 copy-done.5
  275.9 123.5 %all-gather.9.cloned.1.call-done = bf16[6144,384]{1,0:T(8,128)(2,1)} async-done(((bf16[96,384]{1,0:T(8,128)(2,1)}), bf16[6144,384]{1,0:T(8,128)(2,1)}) %all-gather.9.cloned.1.call-update) | async-done | bytes 4718608 | tf_op jit(solution)/shard_map/all_gather | solution.py:140
  399.4 4.0 fusion.31
  403.4 1.0 copy.88
  404.5 1.0 fusion.51
  405.6 0.9 fusion.30
  406.5 138.1 %all-gather.11.cloned.1.call-done = bf16[8192,256]{0,1:T(8,128)(2,1)} async-done(((bf16[128,256]{0,1:T(8,128)(2,1)}), bf16[8192,256]{0,1:T(8,128)(2,1)}) %all-gather.11.cloned.1.call-update) | async-done | bytes 4194320 | tf_op jit(solution)/shard_map/all_gather | solution.py:153
  544.6 4.8 copy.132
  549.4 30.5 %while.17 = (s32[]{:T(128)}, f32[128,1,3]{0,2,1:T(4,128)S(1)}, f32[128,1,3]{0,2,1:T(4,128)S(1)}, f32[128,1,3,128]{0,3,2,1:T(8,128)S(1)}, s32[8,16]{1,0:T(8,128)}...) while((s32[]{:T(128)}, f32[128,1,3]{0,2,1:T(4,128)S(1)}, ...), condition=%wide.region_6.7_spmd.clone, body=%wide.region_3.6_spmd.clone.sunk | while | flops 205249664 | bytes 7370237 | solution.py:170
  549.4 1.1 constant_dynamic-slice_fusion.4
  550.6 0.7 fusion.65
  551.9 0.4 fusion.67
  552.7 0.4 fusion.70
  553.2 1.1 constant_dynamic-slice_fusion.4
  554.4 0.7 fusion.65
  555.8 0.4 fusion.67
  556.5 0.4 fusion.70
  557.0 1.1 constant_dynamic-slice_fusion.4
  558.2 0.7 fusion.65
  559.6 0.4 fusion.67
  560.4 0.4 fusion.70
  560.8 1.1 constant_dynamic-slice_fusion.4
  562.1 0.7 fusion.65
  563.4 0.4 fusion.67
  564.2 0.4 fusion.70
  564.6 1.1 constant_dynamic-slice_fusion.4
  565.9 0.7 fusion.65
  567.2 0.4 fusion.67
  568.0 0.4 fusion.70
  568.5 1.1 constant_dynamic-slice_fusion.4
  569.7 0.7 fusion.65
  571.0 0.4 fusion.67
  571.8 0.4 fusion.70
  572.3 1.1 constant_dynamic-slice_fusion.4
  573.5 0.7 fusion.65
  574.9 0.4 fusion.67
  575.7 0.4 fusion.70
  576.1 1.1 constant_dynamic-slice_fusion.4
  577.3 0.7 fusion.65
  578.7 0.4 fusion.67
  579.5 0.4 fusion.70
  580.0 0.8 copy.94
  (176 shorter events, 11.4 us)
Async XLA Ops:
  6.5 5.1 copy-start
  6.5 2.4 copy-start.2
  6.5 2.4 copy-start.7
  6.5 2.4 copy-start.3
  6.5 89.3 %all-gather.5.cloned.1.call-start = ((), (), s32[]{:S(2)}) async-start(), calls=%async_computation | async-start | bytes 3538944 | tf_op jit(solution)/shard_map/all_gather | solution.py:109
  9.5 4.7 copy-start.4
  12.7 235.8 %all-gather.7.cloned.1.call-start = ((), (), s32[]{:S(2)}) async-start(), calls=%async_computation.1 | async-start | bytes 3194880 | tf_op jit(solution)/shard_map/all_gather | solution.py:146
  13.4 386.0 %all-gather.9.cloned.1.call-start = ((), (), s32[]{:S(2)}) async-start(), calls=%async_computation.2 | async-start | bytes 4792320 | tf_op jit(solution)/shard_map/all_gather | solution.py:140
  14.2 530.4 %all-gather.11.cloned.1.call-start = ((), (), s32[]{:S(2)}) async-start(), calls=%async_computation.3 | async-start | bytes 4259840 | tf_op jit(solution)/shard_map/all_gather | solution.py:153
  95.8 2.8 copy-start.1
  100.5 151.9 %copy-start.8 = (s32[2]{0:T(128)S(1)}, s32[2]{0:T(128)}, u32[]{:S(2)}) copy-start(s32[2]{0:T(128)} %param.16) | copy-start | bytes 28
  100.5 155.8 %copy-start.9 = (s32[2]{0:T(128)S(1)}, s32[2]{0:T(128)}, u32[]{:S(2)}) copy-start(s32[2]{0:T(128)} %param.15) | copy-start | bytes 28
  275.3 0.5 copy-start.5
  544.6 4.8 copy-start.10
  549.4 30.6 %copy-start.6 = (pred[128]{0:T(512)(128)(4,1)S(1)}, pred[128]{0:T(512)(128)(4,1)}, u32[]{:S(2)}) copy-start(pred[128]{0:T(512)(128)(4,1)} %copy-done.5) | copy-start | bytes 388
Sparse Core Ops, SparseCore 0:
  12.8 82.9 all-gather.4
  99.1 149.3 all-gather.6
  251.8 147.5 all-gather.8
  402.2 142.2 all-gather.10
where the time goes:
time: 588 us; the launch traced here: 587 us
  waiting for transfers between devices  492 us (84%)
  local copies, waits for them, and re-layouts  34.2 us (6%)
  blocking collectives  17.4 us (3%)
  matrix products  17.1 us (3%)
  between operations  14.2 us (2%)
  other arithmetic  11.9 us (2%)
    all_gather x1, waiting for transfers between devices, on_device(): lax.all_gather(kv_weight, 'ctx', axis=0, tiled=True)  148 us
    all_gather x1, waiting for transfers between devices, on_device(): lax.all_gather(keys_values[tokens:], 'ctx', axis=0, tiled=True)  138 us
    all_gather x1, waiting for transfers between devices, on_device(): lax.all_gather(query_weight, 'ctx', axis=0, tiled=True)  123 us
    all_gather x1, waiting for transfers between devices, on_device(): embedded = lax.all_gather(partial_cols, 'head', axis=1, tiled=True)  81 us
    unnamed x1, blocking collectives  17.4 us
  transfers between devices with their start and end apart: 4, of which 4 were waited for; matrix products, arithmetic and copies ran while one was open for 4% of the time, Pallas kernels for 0%

commit v1 on v0

v1 whole, which is shorter than its diff:
```python
import math

import jax
import jax.numpy as jnp
from jax import lax
from jax.experimental import pallas as pl
from jax.experimental.pallas import tpu as pltpu
from jax.sharding import Mesh, PartitionSpec as P

HD = 128
CH = 16


eps_norm = 1e-06
masked_low = -1e30


def make_patches(latents):
    slots, frames, height, flat = latents.shape
    width = flat // CH
    grid = latents.reshape(slots, frames, height, width, CH)
    padded = jnp.pad(grid, ((0, 0), (0, 0), (1, 1), (1, 1), (0, 0)))
    half_rows = height // 2
    half_cols = width // 2
    split = padded.reshape(slots, frames, half_rows + 1, 2, half_cols + 1, 2, CH)
    offsets_list = []
    for row_off in range(4):
        for col_off in range(4):
            offsets_list.append(
                split[
                    :,
                    :,
                    row_off // 2 : row_off // 2 + half_rows,
                    row_off % 2,
                    col_off // 2 : col_off // 2 + half_cols,
                    col_off % 2,
                    :,
                ]
            )
    stacked = jnp.stack(offsets_list, axis=4)
    return stacked.reshape(slots * frames * half_rows * half_cols, 16 * CH)


def rms_normalize(values, gain):
    wide = values.astype(jnp.float32)
    factor = lax.rsqrt(jnp.mean(wide * wide, axis=-1, keepdims=True) + eps_norm)
    return (wide * factor * gain.astype(jnp.float32)).astype(jnp.bfloat16)


CTX = ("yh", "z", "core")
HEAD = ("x", "yl")
meta_rows = 16
score_factor = HD ** (-0.5) * math.log2(math.e)
key_chunk = 1024


def attention_kernel(valid_ref, q_ref, own_ref, kv_ref, bias_ref, out_ref):
    tokens = q_ref.shape[0]
    group = q_ref.shape[1] // HD
    span_rows = tokens // 2
    frame_rows = span_rows // 4
    q = jnp.concatenate([q_ref[:, g * HD : (g + 1) * HD] for g in range(group)], axis=0)

    def scores_of(keys, bias):
        s = lax.dot_general(q, keys, (((1,), (1,)), ((), ())), preferred_element_type=jnp.float32)
        s = s.reshape(group, tokens, keys.shape[0]) * score_factor + bias[None]
        return s.reshape(group * tokens, keys.shape[0])

    row = lax.broadcasted_iota(jnp.int32, (tokens, tokens), 0)
    col = lax.broadcasted_iota(jnp.int32, (tokens, tokens), 1)
    valid_col = jnp.where(col < span_rows, valid_ref[0], valid_ref[1])
    same = (row < span_rows) == (col < span_rows)
    live_col = lax.rem(col, span_rows) < valid_col * frame_rows
    own_bias = jnp.where(same & live_col, 0.0, masked_low)
    s = scores_of(own_ref[:, :HD], own_bias)
    largest = jnp.max(s, axis=1, keepdims=True)
    raw = jnp.exp2(s - largest)
    total = jnp.sum(raw, axis=1, keepdims=True)
    summed = jnp.dot(raw.astype(jnp.bfloat16), own_ref[:, HD:], preferred_element_type=jnp.float32)
    first = lax.broadcasted_iota(jnp.int32, (tokens, key_chunk), 0) < span_rows
    for start in range(0, kv_ref.shape[0], key_chunk):
        keys = kv_ref[start : start + key_chunk, :HD]
        values = kv_ref[start : start + key_chunk, HD:]
        bias = jnp.where(
            first,
            bias_ref[0:1, start : start + key_chunk],
            bias_ref[1:2, start : start + key_chunk],
        )
        s = scores_of(keys, bias)
        new_largest = jnp.maximum(largest, jnp.max(s, axis=1, keepdims=True))
        raw = jnp.exp2(s - new_largest)
        factor = jnp.exp2(largest - new_largest)
        total = total * factor + jnp.sum(raw, axis=1, keepdims=True)
        summed = summed * factor + jnp.dot(
            raw.astype(jnp.bfloat16), values, preferred_element_type=jnp.float32
        )
        largest = new_largest
    result = summed / total
    token = lax.broadcasted_iota(jnp.int32, (tokens, HD), 0)
    valid_row = jnp.where(token < span_rows, valid_ref[0], valid_ref[1])
    live_row = lax.rem(token, span_rows) < valid_row * frame_rows
    for g in range(group):
        piece = result[g * tokens : (g + 1) * tokens]
        out_ref[:, g * HD : (g + 1) * HD] = jnp.where(live_row, piece, 0.0).astype(jnp.bfloat16)


def attention(valid, q, own, kv_all, bias):
    vmem = pl.BlockSpec(memory_space=pltpu.VMEM)
    return pl.pallas_call(
        attention_kernel,
        out_shape=jax.ShapeDtypeStruct(q.shape, jnp.bfloat16),
        in_specs=[pl.BlockSpec(memory_space=pltpu.SMEM), vmem, vmem, vmem, vmem],
        out_specs=vmem,
        compiler_params=pltpu.CompilerParams(vmem_limit_bytes=40 * 1024 * 1024),
    )(valid, q, own, kv_all, bias)


def add_position(projected, position_rows, tokens):
    cols = projected.shape[1]
    doubled = projected.reshape(2, tokens, cols) + position_rows.astype(jnp.float32)[None]
    return doubled.reshape(2 * tokens, cols).astype(jnp.bfloat16)


def on_device(
    clean_latents,
    noise,
    timesteps,
    span_order,
    valid_frames,
    embed_weight,
    position,
    norm_gain,
    query_weight,
    kv_weight,
):
    slots, frames, height, flat = clean_latents.shape
    frame_rows = height // 2 * (flat // (2 * CH))
    span_rows = frames * frame_rows
    tokens = slots * span_rows
    core = lax.axis_index("core")
    half = embed_weight.shape[0] // 2
    own_embed = lax.all_gather(
        lax.dynamic_slice_in_dim(embed_weight, core * half, half, 0), HEAD, axis=1, tiled=True
    )
    rows, kv_cols = kv_weight.shape
    meta = jnp.concatenate([span_order, valid_frames]).astype(jnp.float16)
    meta_block = jnp.pad(meta[None, :], ((0, meta_rows - 1), (0, kv_cols - 2 * slots)))
    kv_shard = jnp.concatenate([kv_weight.astype(jnp.float16), meta_block], axis=0)
    kv_pair = lax.all_gather(kv_shard, "yh", axis=0, tiled=True)
    kv_gathered = lax.all_gather(kv_pair, ("z", "core"), axis=0, tiled=True)
    kv_gathered = kv_gathered.reshape(-1, 2, rows + meta_rows, kv_cols)
    kv_full = kv_gathered[:, :, :rows].swapaxes(0, 1).astype(jnp.bfloat16).reshape(-1, kv_cols)
    meta_all = kv_gathered[:, :, rows, : 2 * slots].astype(jnp.float32).astype(jnp.int32)
    q_pair = lax.all_gather(query_weight, "yh", axis=0, tiled=True)
    q_gathered = lax.all_gather(q_pair, ("z", "core"), axis=0, tiled=True)
    q_gathered = q_gathered.reshape(-1, 2, rows, query_weight.shape[1])

    other_embed = lax.ppermute(own_embed, "core", [(0, 1), (1, 0)])
    level = ((timesteps.astype(jnp.float32) + 1.0) / 1000.0)[:, None, None, None]
    noisy_latents = (
        (1.0 - level) * clean_latents.astype(jnp.float32) + level * noise.astype(jnp.float32)
    ).astype(jnp.bfloat16)
    patches = make_patches(jnp.concatenate([noisy_latents, clean_latents], axis=0))
    own_patches = lax.dynamic_slice_in_dim(patches, core * half, half, 1)
    other_patches = lax.dynamic_slice_in_dim(patches, (1 - core) * half, half, 1)
    projected = jnp.dot(
        own_patches, own_embed, preferred_element_type=jnp.float32
    ) + jnp.dot(other_patches, other_embed, preferred_element_type=jnp.float32)
    embedded = add_position(projected, position, tokens)
    normed = rms_normalize(embedded, norm_gain)
    keys_values = jnp.dot(normed, kv_full, preferred_element_type=jnp.float32).astype(jnp.bfloat16)

    clean_pair = lax.all_gather(keys_values[tokens:].astype(jnp.float16), "yh", axis=0, tiled=True)
    kv_all = lax.all_gather(clean_pair, ("z", "core"), axis=0, tiled=True).astype(jnp.bfloat16)

    key_order = meta_all[:, :, :slots].reshape(-1)
    key_valid = meta_all[:, :, slots:].reshape(-1)
    frame = jnp.arange(span_rows, dtype=jnp.int32) // frame_rows
    live = (frame[None, :] < key_valid[:, None])[None]
    earlier = (key_order[None, :] < span_order[:, None])[:, :, None]
    bias = jnp.where(live & earlier, 0.0, masked_low).reshape(slots, -1)

    pairs = q_gathered.shape[0]
    normed_noisy = normed[:tokens].reshape(tokens, 2, pairs * rows)
    queries = jnp.dot(
        normed_noisy[:, 0], q_gathered[:, 0].reshape(pairs * rows, -1), preferred_element_type=jnp.float32
    ) + jnp.dot(
        normed_noisy[:, 1], q_gathered[:, 1].reshape(pairs * rows, -1), preferred_element_type=jnp.float32
    )
    return attention(
        valid_frames, queries.astype(jnp.bfloat16), keys_values[:tokens], kv_all, bias
    )


def solution(mesh):
    fine = Mesh(mesh.devices.reshape(2, 16, 2, 4, 2), CTX + HEAD)
    return jax.shard_map(
        on_device,
        mesh=fine,
        in_specs=(
            P(CTX, None, None, None),
            P(CTX, None, None, None),
            P(CTX),
            P(CTX),
            P(CTX),
            P(None, HEAD),
            P(CTX, None),
            P(),
            P(CTX, HEAD),
            P(CTX, HEAD),
        ),
        out_specs=P(CTX, HEAD),
        check_vma=False,
    )
```

time: 588 us -> 183 us (0.31)
  waiting for transfers between devices: 492 us -> 0.92 us
  blocking collectives: 17.4 us -> 123 us
  local copies, waits for them, and re-layouts: 34.2 us -> 22.5 us
  matrix products: 17.1 us -> 6.26 us
  Pallas kernels: 0 us -> 6.71 us
    all_gather x4 -> x2, waiting for transfers between devices: 490 us -> 0.02 us  [the longest x1 0.02 us: on_device(): lax.all_gather(lax.dynamic_slice_in_dim(embed_weight, core * half, half,...]
    all_gather x0 -> x5, blocking collectives: none -> 123 us  [the longest x1 51.6 us: on_device(): kv_gathered = lax.all_gather(kv_pair, ('z', 'core'), axis=0, tiled=True)]
    unnamed x1 -> x0, blocking collectives: 17.4 us -> none
    dot_general x21 -> x5, matrix products: 17.1 us -> 6.26 us  [the longest x1 2.5 us: on_device(): jnp.dot(own_patches, own_embed, preferred_element_type=jnp.float32)]
    dynamic_slice x8 -> x1, local copies, waits for them, and re-layouts: 8.64 us -> 0.7 us  [on_device(): lax.dynamic_slice_in_dim(embed_weight, core * half, half, 0)]
    add x33 -> x0, local copies, waits for them, and re-layouts: 7.3 us -> none  [expand_rows(): values[:, None] + jnp.zeros((1, span_rows), jnp.int32)]
    slice x1 -> x4, local copies, waits for them, and re-layouts: 0.68 us -> 7.93 us  [the longest x1 3.61 us: on_device(): normed_noisy[:, 1]]
    pallas_call x0 -> x1, Pallas kernels: none -> 6.71 us  [attention(): pl.pallas_call(attention_kernel, out_shape=jax.ShapeDtypeStruct(q.shape,...]
  transfers between devices with their start and end apart: 4 -> 3, of which waited for: 4 -> 1; matrix products, arithmetic and copies ran while one was open for 4% -> 15% of each run, Pallas kernels for 0% -> 0%
where the time goes in v1:
time: 183 us; the launch traced here: 182 us
  blocking collectives  123 us (67%)
  local copies, waits for them, and re-layouts  22.5 us (12%)
  between operations  13.8 us (8%)
  other arithmetic  6.99 us (4%)
  Pallas kernels  6.71 us (4%)
  matrix products  6.26 us (3%)
  starting transfers between devices  2.1 us (1%)
    all_gather x1, blocking collectives, on_device(): kv_gathered = lax.all_gather(kv_pair, ('z', 'core'), axis=0, tiled=True)  51.6 us
    all_gather x1, blocking collectives, on_device(): lax.all_gather(clean_pair, ('z', 'core'), axis=0, tiled=True)  51 us
    all_gather x1, blocking collectives, on_device(): q_pair = lax.all_gather(query_weight, 'yh', axis=0, tiled=True)  7.99 us
    all_gather x1, blocking collectives, on_device(): lax.all_gather(keys_values[tokens:].astype(jnp.float16), 'yh', axis=0, ti...  7.03 us
    pallas_call x1, Pallas kernels, attention(): pl.pallas_call(attention_kernel, out_shape=jax.ShapeDtypeStruct(q.shape,...  6.71 us
    all_gather x1, blocking collectives, on_device(): kv_pair = lax.all_gather(kv_shard, 'yh', axis=0, tiled=True)  5.21 us
    unnamed x35, local copies, waits for them, and re-layouts  4.14 us
    reshape x1, local copies, waits for them, and re-layouts, on_device(): normed_noisy = normed[:tokens].reshape(tokens, 2, pairs * rows)  4.06 us
  transfers between devices with their start and end apart: 3, of which 1 were waited for; matrix products, arithmetic and copies ran while one was open for 15% of the time, Pallas kernels for 0%

profile of v1, /device:TPU:1, one launch (start us, length us, event | category | flops | bytes accessed | tf_op | source)
XLA Modules:
  0.0 182.1 jit_solution(13542485930356248812)
XLA Ops:
  6.5 0.0 copy-start
  6.5 0.0 all-gather.5.cloned.1.call-start
  6.5 1.0 copy-done
  7.5 0.7 constant_dynamic-slice_fusion
  8.2 0.0 all-gather.5.cloned.1.call-update
  8.3 0.0 all-gather.7.cloned.1.call-start
  8.3 8.0 %all_gather.22 = bf16[192,384]{1,0:T(8,128)(2,1)} all-gather(bf16[96,384]{1,0:T(8,128)(2,1)} %param.18), channel_id=1, replica_groups=mesh['yh'=2,'z'=16,'core'=2,'x'=4,'yl'=2] {'yh'}, dimensions={0}, use_global_device_ids=true | all-gather | bytes 221184 | tf_op jit(solution)/shard_map/all_gather | solution.py:154
  16.3 0.0 all-gather.7.cloned.1.call-update
  16.3 0.7 broadcast_subtract_fusion
  17.0 0.8 add_convert_fusion
  17.8 0.7 pad_maximum_fusion.1
  18.5 0.2 reshape.144
  18.7 0.2 copy.49
  18.9 0.0 copy-start.8
  19.0 0.0 copy-start.7
  19.0 0.0 copy-start.2
  19.0 0.0 copy-start.9
  19.0 0.2 pad.8
  19.8 0.7 copy.66
  20.5 1.0 reshape.146
  21.5 0.0 copy-done.8
  21.5 0.0 copy-done.7
  21.5 0.0 copy-done.2
  21.6 0.0 copy-done.9
  21.6 0.1 fusion.33
  21.7 5.2 %all_gather.24 = f16[224,256]{1,0:T(8,128)(2,1)S(1)} all-gather(f16[112,256]{1,0:T(8,128)(2,1)S(1)} %pad_maximum_fusion), channel_id=1, replica_groups=mesh['yh'=2,'z'=16,'core'=2,'x'=4,'yl'=2] {'yh'}, dimensions={0}, use_global_device_ids=true | all-gather | bytes 172032 | tf_op jit(solution)/shard_map/all_gather | solution.py:149
  26.9 51.6 %all-gather.8 = f16[7168,256]{1,0:T(8,128)(2,1)S(1)} all-gather(f16[224,256]{1,0:T(8,128)(2,1)S(1)} %all_gather.24), channel_id=1, replica_groups=mesh['yh'=2,'z'=16,'core'=2,'x'=4,'yl'=2] {'z','core'}, dimensions={0}, use_global_device_ids=true | all-gather | bytes 3784704 | tf_op jit(solution)/shard_map/all_gather | solution.py:150
  78.4 0.7 fusion.5
  79.2 1.9 %copy.69 = bf16[2,32,96,256]{3,2,1,0:T(8,128)(2,1)} copy(bf16[2,32,96,256]{3,2,0,1:T(8,128)(2,1)S(1)} %fusion.5) | data formatting | bytes 6291456 | tf_op jit(solution)/shard_map/convert_element_type | solution.py:152
  81.1 0.1 fusion.38
  81.2 0.2 lt.53
  81.3 0.1 lt.54
  81.4 0.1 lt.55
  81.5 0.1 lt.52
  81.6 0.1 lt.57
  81.8 0.1 broadcast_compare_fusion
  81.8 0.1 and.32
  81.9 0.1 and.33
  82.1 0.0 all-gather.5.cloned.1.call-done
  82.1 2.1 %collective-permute-start = (bf16[128,6144]{1,0:T(8,128)(2,1)}, bf16[128,6144]{1,0:T(8,128)(2,1)S(1)}, u32[]{:S(2)}, u32[]{:S(2)}) collective-permute-start(bf16[128,6144]{1,0:T(8,128)(2,1)} %all-gather.5.cloned.1.call-done), channel_id=1, source_target_pairs={{0,8},{8,0},{1,9},{9,1},{2,10},{10,2},{3,11},{11,3},{4,12},{12,4},... | collective-permute-start | bytes 4718600 | tf_op jit(solution)/shard_map/ppermute | solution.py:158
  84.2 0.1 and_select_fusion.bias_ref
  84.2 0.0 copy-start.6
  84.3 2.5 %fusion.25 = f32[256,6144]{1,0:T(8,128)S(1)} fusion(bf16[128,6144]{1,0:T(8,128)(2,1)} %all-gather.5.cloned.1.call-done, bf16[256,256]{1,0:T(8,128)(2,1)S(1)} %reshape.146, s32[]{:T(128)S(6)} %select_n.21), kind=kOutput, calls=%fused_computation.51 | convolution fusion | flops 402653184 | bytes 7929860 | tf_op jit(solution)/shard_map/dot_general | solution.py:166
  86.8 0.9 collective-permute-done
  87.6 0.0 copy-done.6
  87.6 0.7 add.55
  88.4 1.6 fusion.2
  89.9 0.9 fusion.4
  90.8 0.0 copy-start.5
  90.9 1.3 slice.124
  92.1 1.2 copy-done.5
  93.3 1.0 convolution_convert_fusion
  94.3 7.0 %all_gather.26 = f16[256,256]{1,0:T(8,128)(2,1)S(1)} all-gather(f16[128,256]{1,0:T(8,128)(2,1)S(1)} %get-tuple-element.9), channel_id=1, replica_groups=mesh['yh'=2,'z'=16,'core'=2,'x'=4,'yl'=2] {'yh'}, dimensions={0}, use_global_device_ids=true | all-gather | bytes 196608 | tf_op jit(solution)/shard_map/all_gather | solution.py:173
  101.4 51.0 %all-gather.9 = f16[8192,256]{1,0:T(8,128)(2,1)S(1)} all-gather(f16[256,256]{1,0:T(8,128)(2,1)S(1)} %all_gather.26), channel_id=1, replica_groups=mesh['yh'=2,'z'=16,'core'=2,'x'=4,'yl'=2] {'z','core'}, dimensions={0}, use_global_device_ids=true | all-gather | bytes 4325376 | tf_op jit(solution)/shard_map/all_gather | solution.py:174
  152.4 2.8 %convert_element_type.85.kv_ref = bf16[8192,256]{1,0:T(8,128)(2,1)} convert(f16[8192,256]{1,0:T(8,128)(2,1)S(1)} %all-gather.9) | non-fusion elementwise | flops 2097152 | bytes 8388608 | tf_op jit(solution)/shard_map/convert_element_type | solution.py:174
  155.2 4.1 %reshape.147 = bf16[128,2,3072]{2,1,0:T(2,128)(2,1)S(1)} reshape(bf16[128,6144]{1,0:T(8,128)(2,1)} %slice.124) | data formatting | bytes 3145728 | tf_op jit(solution)/shard_map/reshape | solution.py:184
  159.3 3.6 %fusion.37 = (bf16[128,1,3072]{2,1,0:T(2,128)(2,1)}, bf16[128,1,3072]{2,1,0:T(2,128)(2,1)}) fusion(bf16[128,2,3072]{2,1,0:T(2,128)(2,1)S(1)} %reshape.147), kind=kLoop, calls=%fused_computation.80 | loop fusion | bytes 3145728 | tf_op jit(solution)/shard_map/slice | solution.py:188
  162.9 3.0 %fusion.36 = (bf16[32,1,96,384]{3,2,1,0:T(8,128)(2,1)S(1)}, bf16[32,1,96,384]{3,2,1,0:T(8,128)(2,1)S(1)}) fusion(bf16[32,2,96,384]{3,2,1,0:T(8,128)(2,1)} %bitcast.145), kind=kLoop, calls=%fused_computation.79 | loop fusion | bytes 9437184 | tf_op jit(solution)/shard_map/slice | solution.py:188
  165.9 0.0 copy-start.3
  165.9 0.6 fusion.7
  166.5 0.8 copy-done.3
  167.3 0.6 fusion.6.q_ref
  167.9 0.6 copy-done.1
  168.5 6.7 %shard_map.100 = bf16[128,384]{1,0:T(8,128)(2,1)} custom-call(s32[2]{0:T(128)S(1)} %copy-done.2, bf16[128,384]{1,0:T(8,128)(2,1)S(1)} %fusion.6.q_ref, bf16[128,256]{1,0:T(8,128)(2,1)S(1)} %get-tuple-element.10.own_ref, bf16[8192,256]{1,0:T(8,128)(2,1)S(1)} %copy-done.1, f32[2,8192]{1,0:T(2,128)S(1)} %and_select_fusion.bias_ref), custom_call_target="tpu_custom_call" | custom-call | tf_op jit(solution)/shard_map/pallas_call | solution.py:109
  (30 shorter events, 0.7 us)
Async XLA Ops:
  6.5 1.0 copy-start
  6.5 75.6 %all-gather.5.cloned.1.call-start = ((), (), s32[]{:S(2)}) async-start(), calls=%async_computation | async-start | bytes 1769472 | tf_op jit(solution)/shard_map/all_gather | solution.py:142
  8.3 154.6 %all-gather.7.cloned.1.call-start = ((), (), s32[]{:S(2)}) async-start(), calls=%async_computation.1 | async-start | bytes 4866048 | tf_op jit(solution)/shard_map/all_gather | solution.py:155
  18.9 2.5 %copy-start.8 = (bf16[6144]{0:T(1024)(128)(2,1)S(1)}, bf16[6144]{0:T(1024)(128)(2,1)}, u32[]{:S(2)}) copy-start(bf16[6144]{0:T(1024)(128)(2,1)} %param.17) | copy-start | bytes 36868
  19.0 2.6 %copy-start.7 = (bf16[96,256]{1,0:T(8,128)(2,1)S(1)}, bf16[96,256]{1,0:T(8,128)(2,1)}, u32[]{:S(2)}) copy-start(bf16[96,256]{1,0:T(8,128)(2,1)} %param.19) | copy-start | bytes 147460
  19.0 2.6 %copy-start.2 = (s32[2]{0:T(128)S(1)}, s32[2]{0:T(128)}, u32[]{:S(2)}) copy-start(s32[2]{0:T(128)} %valid_ref.1) | copy-start | bytes 28
  19.0 2.6 %copy-start.9 = (s32[2]{0:T(128)S(1)}, s32[2]{0:T(128)}, u32[]{:S(2)}) copy-start(s32[2]{0:T(128)} %param.13) | copy-start | bytes 28
  82.1 5.5 %collective-permute-start = (bf16[128,6144]{1,0:T(8,128)(2,1)}, bf16[128,6144]{1,0:T(8,128)(2,1)S(1)}, u32[]{:S(2)}, u32[]{:S(2)}) collective-permute-start(bf16[128,6144]{1,0:T(8,128)(2,1)} %all-gather.5.cloned.1.call-done), channel_id=1, source_target_pairs={{0,8},{8,0},{1,9},{9,1},{2,10},{10,2},{3,11},{11,3},{4,12},{12,4},... | collective-permute-start | bytes 4718600 | tf_op jit(solution)/shard_map/ppermute | solution.py:158
  84.2 3.4 %copy-start.6 = (bf16[128,6144]{1,0:T(8,128)(2,1)S(1)}, bf16[128,6144]{1,0:T(8,128)(2,1)}, u32[]{:S(2)}) copy-start(bf16[128,6144]{1,0:T(8,128)(2,1)} %param.16) | copy-start | bytes 4718596
  90.8 2.5 %copy-start.5 = (bf16[2,32,96,256]{3,2,1,0:T(8,128)(2,1)S(1)}, bf16[2,32,96,256]{3,2,1,0:T(8,128)(2,1)}, u32[]{:S(2)}) copy-start(bf16[2,32,96,256]{3,2,1,0:T(8,128)(2,1)} %copy.69) | copy-start | bytes 9437188
  162.9 3.0 %copy-start.4 = (bf16[128,1,3072]{2,1,0:T(2,128)(2,1)S(1)}, bf16[128,1,3072]{2,1,0:T(2,128)(2,1)}, u32[]{:S(2)}) copy-start(bf16[128,1,3072]{2,1,0:T(2,128)(2,1)} %get-tuple-element.8) | copy-start | bytes 2359300
  165.9 1.4 copy-start.3
  165.9 2.7 %copy-start.1 = (bf16[8192,256]{1,0:T(8,128)(2,1)S(1)}, bf16[8192,256]{1,0:T(8,128)(2,1)}, u32[]{:S(2)}) copy-start(bf16[8192,256]{1,0:T(8,128)(2,1)} %convert_element_type.85.kv_ref) | copy-start | bytes 12582916
Sparse Core Ops, SparseCore 0:
  9.4 53.1 all-gather.4
  64.7 81.6 all-gather.6

commit v2 on v1

--- a/solution.py
+++ b/solution.py
@@ -15,30 +15,54 @@
 masked_low = -1e30
 
 
-def make_patches(latents):
-    slots, frames, height, flat = latents.shape
-    width = flat // CH
-    grid = latents.reshape(slots, frames, height, width, CH)
-    padded = jnp.pad(grid, ((0, 0), (0, 0), (1, 1), (1, 1), (0, 0)))
-    half_rows = height // 2
-    half_cols = width // 2
-    split = padded.reshape(slots, frames, half_rows + 1, 2, half_cols + 1, 2, CH)
-    offsets_list = []
-    for row_off in range(4):
-        for col_off in range(4):
-            offsets_list.append(
-                split[
-                    :,
-                    :,
-                    row_off // 2 : row_off // 2 + half_rows,
-                    row_off % 2,
-                    col_off // 2 : col_off // 2 + half_cols,
-                    col_off % 2,
-                    :,
-                ]
+def patch_kernel(core_ref, time_ref, clean_ref, noise_ref, own_ref, other_ref):
+    rows, lanes = clean_ref.shape
+    row = lax.broadcasted_iota(jnp.int32, (rows, lanes), 0)
+    steps = jnp.where(row < rows // 2, time_ref[0], time_ref[1])
+    level = (steps.astype(jnp.float32) + 1.0) / 1000.0
+    clean = clean_ref[...]
+    noisy = (
+        (1.0 - level) * clean.astype(jnp.float32) + level * noise_ref[...].astype(jnp.float32)
+    ).astype(jnp.bfloat16)
+    latents = jnp.concatenate([noisy, clean], axis=0)
+    count = 2 * rows
+    source = lax.broadcasted_iota(jnp.int32, (lanes, 256), 0)
+    target = lax.broadcasted_iota(jnp.int32, (lanes, 256), 1)
+    token = lax.broadcasted_iota(jnp.int32, (256, 4 * count), 0)
+    place = lax.broadcasted_iota(jnp.int32, (256, 4 * count), 1)
+    result = jnp.zeros((256, 256), jnp.float32)
+    for kernel_row in range(4):
+        shifted = []
+        for token_col in range(4):
+            wanted = (target & 63) + (32 * token_col - 16)
+            pick = (source == wanted) & ((target >> 6) == kernel_row)
+            pick = jnp.where(pick, 1.0, 0.0).astype(jnp.bfloat16)
+            shifted.append(
+                jnp.dot(latents, pick, preferred_element_type=jnp.float32).astype(jnp.bfloat16)
             )
-    stacked = jnp.stack(offsets_list, axis=4)
-    return stacked.reshape(slots * frames * half_rows * half_cols, 16 * CH)
+        latent_row = 2 * ((token >> 2) & 3) - 1 + kernel_row
+        wanted = (token & 3) * count + (token >> 4) * 8 + latent_row
+        pick = (place == wanted) & (latent_row >= 0) & (latent_row < 8)
+        pick = jnp.where(pick, 1.0, 0.0).astype(jnp.bfloat16)
+        result += jnp.dot(pick, jnp.concatenate(shifted, axis=0), preferred_element_type=jnp.float32)
+    patches = result.astype(jnp.bfloat16)
+    half = patches.shape[1] // 2
+    upper = core_ref[0] == 1
+    own_ref[...] = jnp.where(upper, patches[:, half:], patches[:, :half])
+    other_ref[...] = jnp.where(upper, patches[:, :half], patches[:, half:])
+
+
+def make_patches(core, timesteps, clean_latents, noise):
+    flat = clean_latents.shape[-1]
+    smem = pl.BlockSpec(memory_space=pltpu.SMEM)
+    vmem = pl.BlockSpec(memory_space=pltpu.VMEM)
+    shape = jax.ShapeDtypeStruct((256, 128), jnp.bfloat16)
+    return pl.pallas_call(
+        patch_kernel,
+        out_shape=(shape, shape),
+        in_specs=[smem, smem, vmem, vmem],
+        out_specs=(vmem, vmem),
+    )(core[None], timesteps, clean_latents.reshape(-1, flat), noise.reshape(-1, flat))
 
 
 def rms_normalize(values, gain):
@@ -111,7 +135,7 @@
         out_shape=jax.ShapeDtypeStruct(q.shape, jnp.bfloat16),
         in_specs=[pl.BlockSpec(memory_space=pltpu.SMEM), vmem, vmem, vmem, vmem],
         out_specs=vmem,
-        compiler_params=pltpu.CompilerParams(vmem_limit_bytes=40 * 1024 * 1024),
+        compiler_params=pltpu.CompilerParams(vmem_limit_bytes=24 * 1024 * 1024),
     )(valid, q, own, kv_all, bias)
 
 
@@ -143,26 +167,22 @@
         lax.dynamic_slice_in_dim(embed_weight, core * half, half, 0), HEAD, axis=1, tiled=True
     )
     rows, kv_cols = kv_weight.shape
+    q_cols = query_weight.shape[1]
+    weights = jnp.concatenate([query_weight, kv_weight], axis=1).astype(jnp.float16)
     meta = jnp.concatenate([span_order, valid_frames]).astype(jnp.float16)
-    meta_block = jnp.pad(meta[None, :], ((0, meta_rows - 1), (0, kv_cols - 2 * slots)))
-    kv_shard = jnp.concatenate([kv_weight.astype(jnp.float16), meta_block], axis=0)
-    kv_pair = lax.all_gather(kv_shard, "yh", axis=0, tiled=True)
-    kv_gathered = lax.all_gather(kv_pair, ("z", "core"), axis=0, tiled=True)
-    kv_gathered = kv_gathered.reshape(-1, 2, rows + meta_rows, kv_cols)
-    kv_full = kv_gathered[:, :, :rows].swapaxes(0, 1).astype(jnp.bfloat16).reshape(-1, kv_cols)
-    meta_all = kv_gathered[:, :, rows, : 2 * slots].astype(jnp.float32).astype(jnp.int32)
-    q_pair = lax.all_gather(query_weight, "yh", axis=0, tiled=True)
-    q_gathered = lax.all_gather(q_pair, ("z", "core"), axis=0, tiled=True)
-    q_gathered = q_gathered.reshape(-1, 2, rows, query_weight.shape[1])
+    meta_block = jnp.pad(meta[None, :], ((0, meta_rows - 1), (q_cols, kv_cols - 2 * slots)))
+    weights_pair = lax.all_gather(jnp.concatenate([weights, meta_block], axis=0), "yh", axis=0)
+    kv_gathered = lax.all_gather(
+        weights_pair[:, :, q_cols:], ("z", "core"), axis=1, tiled=True
+    ).reshape(-1, rows + meta_rows, kv_cols)
+    kv_full = kv_gathered[:, :rows].astype(jnp.bfloat16).reshape(-1, kv_cols)
+    meta_all = kv_gathered[:, rows, : 2 * slots].astype(jnp.float32).astype(jnp.int32)
+    q_full = lax.all_gather(
+        weights_pair[:, :rows, :q_cols].astype(jnp.bfloat16), ("z", "core"), axis=1, tiled=True
+    ).reshape(-1, q_cols)
 
     other_embed = lax.ppermute(own_embed, "core", [(0, 1), (1, 0)])
-    level = ((timesteps.astype(jnp.float32) + 1.0) / 1000.0)[:, None, None, None]
-    noisy_latents = (
-        (1.0 - level) * clean_latents.astype(jnp.float32) + level * noise.astype(jnp.float32)
-    ).astype(jnp.bfloat16)
-    patches = make_patches(jnp.concatenate([noisy_latents, clean_latents], axis=0))
-    own_patches = lax.dynamic_slice_in_dim(patches, core * half, half, 1)
-    other_patches = lax.dynamic_slice_in_dim(patches, (1 - core) * half, half, 1)
+    own_patches, other_patches = make_patches(core, timesteps, clean_latents, noise)
     projected = jnp.dot(
         own_patches, own_embed, preferred_element_type=jnp.float32
     ) + jnp.dot(other_patches, other_embed, preferred_element_type=jnp.float32)
@@ -170,23 +190,21 @@
     normed = rms_normalize(embedded, norm_gain)
     keys_values = jnp.dot(normed, kv_full, preferred_element_type=jnp.float32).astype(jnp.bfloat16)
 
-    clean_pair = lax.all_gather(keys_values[tokens:].astype(jnp.float16), "yh", axis=0, tiled=True)
-    kv_all = lax.all_gather(clean_pair, ("z", "core"), axis=0, tiled=True).astype(jnp.bfloat16)
-
-    key_order = meta_all[:, :, :slots].reshape(-1)
-    key_valid = meta_all[:, :, slots:].reshape(-1)
+    clean_pair = lax.all_gather(keys_values[tokens:].astype(jnp.float16), "yh", axis=0)
+    kv_all = (
+        lax.all_gather(clean_pair, ("z", "core"), axis=1, tiled=True)
+        .reshape(-1, kv_cols)
+        .astype(jnp.bfloat16)
+    )
+
+    key_order = meta_all[:, :slots].reshape(-1)
+    key_valid = meta_all[:, slots:].reshape(-1)
     frame = jnp.arange(span_rows, dtype=jnp.int32) // frame_rows
     live = (frame[None, :] < key_valid[:, None])[None]
     earlier = (key_order[None, :] < span_order[:, None])[:, :, None]
     bias = jnp.where(live & earlier, 0.0, masked_low).reshape(slots, -1)
 
-    pairs = q_gathered.shape[0]
-    normed_noisy = normed[:tokens].reshape(tokens, 2, pairs * rows)
-    queries = jnp.dot(
-        normed_noisy[:, 0], q_gathered[:, 0].reshape(pairs * rows, -1), preferred_element_type=jnp.float32
-    ) + jnp.dot(
-        normed_noisy[:, 1], q_gathered[:, 1].reshape(pairs * rows, -1), preferred_element_type=jnp.float32
-    )
+    queries = jnp.dot(normed[:tokens], q_full, preferred_element_type=jnp.float32)
     return attention(
         valid_frames, queries.astype(jnp.bfloat16), keys_values[:tokens], kv_all, bias
     )

time: 183 us -> 169 us (0.923)
  local copies, waits for them, and re-layouts: 22.5 us -> 6.36 us
  blocking collectives: 123 us -> 117 us
  other arithmetic: 6.99 us -> 10.8 us
  matrix products: 6.26 us -> 8.93 us
  Pallas kernels: 6.71 us -> 8.85 us
    slice x4 -> x2, local copies, waits for them, and re-layouts: 7.93 us -> 0.1 us  [the longest x1 0.07 us: on_device(): key_valid = meta_all[:, slots:].reshape(-1)]
    all_gather x5 -> x4, blocking collectives: 123 us -> 117 us  [the longest x1 54.6 us: on_device(): lax.all_gather(clean_pair, ('z', 'core'), axis=1, tiled=True)]
    reshape x4 -> x0, local copies, waits for them, and re-layouts: 5.49 us -> none  [the longest x1 4.06 us: on_device(): normed_noisy = normed[:tokens].reshape(tokens, 2, pairs * rows)]
    convert_element_type x5, other arithmetic: 4.4 us -> 8.92 us  [the longest x1 4.4 us: on_device(): kv_full = kv_gathered[:, :rows].astype(jnp.bfloat16).reshape(-1, kv_cols)]
    dot_general x2 -> x1, matrix products: 1.24 us -> 3.95 us  [on_device(): jnp.dot(normed[:tokens], q_full, preferred_element_type=jnp.float32)]
    pallas_call x0 -> x1, Pallas kernels: none -> 2.38 us  [make_patches(): pl.pallas_call(patch_kernel, out_shape=(shape, shape), in_specs=[smem, sm...]
    convert_element_type x1 -> x0, local copies, waits for them, and re-layouts: 1.87 us -> none  [on_device(): kv_gathered[:, :, :rows].swapaxes(0, 1).astype(jnp.bfloat16)]
    unnamed x35 -> x22, local copies, waits for them, and re-layouts: 4.14 us -> 4.11 us
  transfers between devices with their start and end apart: 3 -> 3, of which waited for: 1 -> 1; matrix products, arithmetic and copies ran while one was open for 15% -> 10% of each run, Pallas kernels for 0% -> 1%
where the time goes in v2:
time: 169 us
  blocking collectives  117 us (69%)
  between operations  13.6 us (8%)
  other arithmetic  10.8 us (6%)
  matrix products  8.93 us (5%)
  Pallas kernels  8.85 us (5%)
  local copies, waits for them, and re-layouts  6.36 us (4%)
  starting transfers between devices  2.09 us (1%)
    all_gather x1, blocking collectives, on_device(): lax.all_gather(clean_pair, ('z', 'core'), axis=1, tiled=True)  54.6 us
    all_gather x1, blocking collectives, on_device(): lax.all_gather(weights_pair[:, :, q_cols:], ('z', 'core'), axis=1, tiled=...  50.2 us
    all_gather x1, blocking collectives, on_device(): lax.all_gather(jnp.concatenate([weights, meta_block], axis=0), 'yh', axis=0)  6.89 us
    pallas_call x1, Pallas kernels, attention(): pl.pallas_call(attention_kernel, out_shape=jax.ShapeDtypeStruct(q.shape,...  6.48 us
    all_gather x1, blocking collectives, on_device(): lax.all_gather(keys_values[tokens:].astype(jnp.float16), 'yh', axis=0)  5.34 us
    convert_element_type x1, other arithmetic, on_device(): kv_full = kv_gathered[:, :rows].astype(jnp.bfloat16).reshape(-1, kv_cols)  4.4 us
    unnamed x22, local copies, waits for them, and re-layouts  4.11 us
    dot_general x1, matrix products, on_device(): jnp.dot(normed[:tokens], q_full, preferred_element_type=jnp.float32)  3.95 us
  transfers between devices with their start and end apart: 3, of which 1 were waited for; matrix products, arithmetic and copies ran while one was open for 10% of the time, Pallas kernels for 1%

profile of v2, /device:TPU:1, one launch (start us, length us, event | category | flops | bytes accessed | tf_op | source)
XLA Modules:
  0.0 168.6 jit_solution(5463568343294529453)
XLA Ops:
  6.5 0.0 copy-start
  6.5 0.0 copy-start.9
  6.5 0.0 all-gather.7.cloned.1.call-start
  6.5 1.0 copy-done
  7.5 0.7 constant_dynamic-slice_fusion
  8.2 0.0 copy-start.10
  8.2 0.0 all-gather.7.cloned.1.call-update
  8.2 0.0 all-gather.9.cloned.1.call-start
  8.3 0.7 convert_bitcast_fusion
  9.0 0.1 fusion.16
  9.1 0.9 maximum_convert_fusion
  10.0 6.9 %all-gather = f16[224,640]{1,0:T(8,128)(2,1)S(1)} all-gather(f16[112,640]{1,0:T(8,128)(2,1)S(1)} %pad_maximum_fusion), channel_id=2, replica_groups=mesh['yh'=2,'z'=16,'core'=2,'x'=4,'yl'=2] {'yh'}, dimensions={0}, use_global_device_ids=true | all-gather | bytes 430080 | tf_op jit(solution)/shard_map/all_gather | solution.py:174
  16.9 0.7 slice_convert_fusion.1
  17.6 0.0 all-gather.9.cloned.1.call-update
  17.7 50.2 %all-gather.10 = f16[2,3584,256]{2,1,0:T(8,128)(2,1)S(1)} all-gather(f16[2,112,256]{2,1,0:T(8,128)(2,1)S(1)} %slice.38), channel_id=1, replica_groups=mesh['yh'=2,'z'=16,'core'=2,'x'=4,'yl'=2] {'z','core'}, dimensions={1}, use_global_device_ids=true | all-gather | bytes 3784704 | tf_op jit(solution)/shard_map/all_gather | solution.py:175
  67.9 0.0 copy-done.9
  67.9 0.0 copy-start.3
  67.9 1.9 %copy-done.3 = f16[2,3584,256]{2,1,0:T(8,128)(2,1)} copy-done((f16[2,3584,256]{2,1,0:T(8,128)(2,1)}, f16[2,3584,256]{2,1,0:T(8,128)(2,1)S(1)}, u32[]{:S(2)}) %copy-start.3) | copy-done | bytes 3670040
  69.9 0.1 fusion.18
  70.0 0.1 lt.48
  70.1 0.1 lt.49
  70.2 0.1 lt.50
  70.3 0.1 lt.47
  70.4 0.1 lt.52
  70.5 0.0 copy-done.10
  70.5 0.1 broadcast_compare_fusion
  70.6 0.1 and.32
  70.7 0.1 and.33
  70.8 2.4 %shard_map.100 = (bf16[256,128]{1,0:T(8,128)(2,1)}, bf16[256,128]{1,0:T(8,128)(2,1)}) custom-call(s32[1]{0:T(128)} %bitcast.core_ref, s32[2]{0:T(128)} %time_ref.1, bf16[64,128]{1,0:T(8,128)(2,1)} %bitcast.34, bf16[64,128]{1,0:T(8,128)(2,1)} %bitcast.35), custom_call_target="tpu_custom_call" | custom-call | tf_op jit(solution)/shard_map/pallas_call | solution.py:60
  73.2 0.0 copy-start.8
  73.2 4.4 %slice_convert_fusion = bf16[64,96,256]{2,1,0:T(8,128)(2,1)} fusion(f16[64,112,256]{2,1,0:T(8,128)(2,1)} %bitcast.27), kind=kLoop, calls=%fused_computation.8 | loop fusion | flops 1572864 | bytes 6291456 | tf_op jit(solution)/shard_map/convert_element_type | solution.py:178
  77.6 0.0 all-gather.7.cloned.1.call-done
  77.6 2.0 %collective-permute-start = (bf16[128,6144]{1,0:T(8,128)(2,1)}, bf16[128,6144]{1,0:T(8,128)(2,1)S(1)}, u32[]{:S(2)}, u32[]{:S(2)}) collective-permute-start(bf16[128,6144]{1,0:T(8,128)(2,1)} %all-gather.7.cloned.1.call-done), channel_id=1, source_target_pairs={{0,8},{8,0},{1,9},{9,1},{2,10},{10,2},{3,11},{11,3},{4,12},{12,4},... | collective-permute-start | bytes 4718600 | tf_op jit(solution)/shard_map/ppermute | solution.py:184
  79.7 0.1 and_select_fusion.bias_ref
  79.7 0.0 copy-done.8
  79.7 0.0 copy-start.6
  79.8 2.5 %fusion.19 = f32[256,6144]{1,0:T(8,128)S(1)} fusion(bf16[256,128]{1,0:T(8,128)(2,1)S(1)} %copy-done.8, bf16[128,6144]{1,0:T(8,128)(2,1)} %all-gather.7.cloned.1.call-done), kind=kOutput, calls=%fused_computation.40 | convolution fusion | flops 402653184 | bytes 7929856 | tf_op jit(solution)/shard_map/dot_general | solution.py:186
  82.3 0.9 collective-permute-done
  83.1 0.0 copy-done.6
  83.1 0.0 copy-start.7
  83.1 0.7 add.37
  83.8 0.1 copy-done.7
  84.0 1.5 fusion.2
  85.5 0.0 copy-start.5
  85.5 0.9 fusion.4
  86.4 0.0 copy-start.4
  86.4 1.0 copy-done.5
  87.4 1.0 convolution_convert_fusion
  88.4 0.0 copy-done.4
  88.4 5.3 %all-gather.1 = f16[256,256]{1,0:T(8,128)(2,1)S(1)} all-gather(f16[128,256]{1,0:T(8,128)(2,1)S(1)} %get-tuple-element.9), channel_id=3, replica_groups=mesh['yh'=2,'z'=16,'core'=2,'x'=4,'yl'=2] {'yh'}, dimensions={0}, use_global_device_ids=true | all-gather | bytes 196608 | tf_op jit(solution)/shard_map/all_gather | solution.py:193
  93.8 54.6 %all-gather.11 = f16[2,4096,256]{2,1,0:T(8,128)(2,1)S(1)} all-gather(f16[2,128,256]{2,1,0:T(8,128)(2,1)S(1)} %bitcast.32), channel_id=1, replica_groups=mesh['yh'=2,'z'=16,'core'=2,'x'=4,'yl'=2] {'z','core'}, dimensions={1}, use_global_device_ids=true | all-gather | bytes 4325376 | tf_op jit(solution)/shard_map/all_gather | solution.py:195
  148.4 2.9 %convert_element_type.69 = bf16[2,4096,256]{2,1,0:T(8,128)(2,1)} convert(f16[2,4096,256]{2,1,0:T(8,128)(2,1)S(1)} %all-gather.11) | non-fusion elementwise | flops 2097152 | bytes 8388608 | tf_op jit(solution)/shard_map/convert_element_type | solution.py:197
  151.3 0.0 all-gather.9.cloned.1.call-done
  151.3 0.0 copy-start.1
  151.3 0.0 copy-start.2
  151.3 3.9 %fusion.7.q_ref = bf16[128,384]{1,0:T(8,128)(2,1)S(1)} fusion(bf16[6144,384]{1,0:T(8,128)(2,1)} %bitcast.28, bf16[256,6144]{1,0:T(8,128)(2,1)} %copy-done.4), kind=kOutput, calls=%fused_computation.12 | convolution fusion | flops 604028928 | bytes 6389760 | tf_op jit(solution)/shard_map/dot_general | solution.py:207
  155.2 0.1 copy-done.1
  155.3 0.0 copy-done.2
  155.3 6.5 %shard_map.101 = bf16[128,384]{1,0:T(8,128)(2,1)} custom-call(s32[2]{0:T(128)S(1)} %copy-done.2, bf16[128,384]{1,0:T(8,128)(2,1)S(1)} %fusion.7.q_ref, bf16[128,256]{1,0:T(8,128)(2,1)S(1)} %get-tuple-element.10.own_ref, bf16[8192,256]{1,0:T(8,128)(2,1)S(1)} %bitcast.24, f32[2,8192]{1,0:T(2,128)S(1)} %and_select_fusion.bias_ref), custom_call_target="tpu_custom_call" | custom-call | tf_op jit(solution)/shard_map/pallas_call | solution.py:133
  (9 shorter events, 0.1 us)
Async XLA Ops:
  6.5 1.0 copy-start
  6.5 61.4 %copy-start.9 = (bf16[6144]{0:T(1024)(128)(2,1)S(1)}, bf16[6144]{0:T(1024)(128)(2,1)}, u32[]{:S(2)}) copy-start(bf16[6144]{0:T(1024)(128)(2,1)} %param.17) | copy-start | bytes 36868
  6.5 71.1 %all-gather.7.cloned.1.call-start = ((), (), s32[]{:S(2)}) async-start(), calls=%async_computation | async-start | bytes 1769472 | tf_op jit(solution)/shard_map/all_gather | solution.py:166
  8.2 62.3 %copy-start.10 = (s32[2]{0:T(128)S(1)}, s32[2]{0:T(128)}, u32[]{:S(2)}) copy-start(s32[2]{0:T(128)} %param.13) | copy-start | bytes 28
  8.2 143.0 %all-gather.9.cloned.1.call-start = ((), (), s32[]{:S(2)}) async-start(), calls=%async_computation.1 | async-start | bytes 4866048 | tf_op jit(solution)/shard_map/all_gather | solution.py:180
  67.9 1.9 %copy-start.3 = (f16[2,3584,256]{2,1,0:T(8,128)(2,1)}, f16[2,3584,256]{2,1,0:T(8,128)(2,1)S(1)}, u32[]{:S(2)}) copy-start(f16[2,3584,256]{2,1,0:T(8,128)(2,1)S(1)} %all-gather.10) | copy-start | bytes 11010052
  73.2 6.5 %copy-start.8 = (bf16[256,128]{1,0:T(8,128)(2,1)S(1)}, bf16[256,128]{1,0:T(8,128)(2,1)}, u32[]{:S(2)}) copy-start(bf16[256,128]{1,0:T(8,128)(2,1)} %get-tuple-element.7) | copy-start | bytes 196612
  77.6 5.5 %collective-permute-start = (bf16[128,6144]{1,0:T(8,128)(2,1)}, bf16[128,6144]{1,0:T(8,128)(2,1)S(1)}, u32[]{:S(2)}, u32[]{:S(2)}) collective-permute-start(bf16[128,6144]{1,0:T(8,128)(2,1)} %all-gather.7.cloned.1.call-done), channel_id=1, source_target_pairs={{0,8},{8,0},{1,9},{9,1},{2,10},{10,2},{3,11},{11,3},{4,12},{12,4},... | collective-permute-start | bytes 4718600 | tf_op jit(solution)/shard_map/ppermute | solution.py:184
  79.7 3.4 %copy-start.6 = (bf16[128,6144]{1,0:T(8,128)(2,1)S(1)}, bf16[128,6144]{1,0:T(8,128)(2,1)}, u32[]{:S(2)}) copy-start(bf16[128,6144]{1,0:T(8,128)(2,1)} %param.16) | copy-start | bytes 4718596
  83.1 0.8 copy-start.7
  85.5 1.9 %copy-start.5 = (bf16[64,96,256]{2,1,0:T(8,128)(2,1)S(1)}, bf16[64,96,256]{2,1,0:T(8,128)(2,1)}, u32[]{:S(2)}) copy-start(bf16[64,96,256]{2,1,0:T(8,128)(2,1)} %slice_convert_fusion) | copy-start | bytes 9437188
  86.4 2.0 %copy-start.4 = (bf16[256,6144]{1,0:T(8,128)(2,1)}, bf16[256,6144]{1,0:T(8,128)(2,1)S(1)}, u32[]{:S(2)}) copy-start(bf16[256,6144]{1,0:T(8,128)(2,1)S(1)} %fusion.4) | copy-start | bytes 9437188
  151.3 4.0 %copy-start.1 = (bf16[2,4096,256]{2,1,0:T(8,128)(2,1)S(1)}, bf16[2,4096,256]{2,1,0:T(8,128)(2,1)}, u32[]{:S(2)}) copy-start(bf16[2,4096,256]{2,1,0:T(8,128)(2,1)} %convert_element_type.69) | copy-start | bytes 12582916
  151.3 4.0 %copy-start.2 = (s32[2]{0:T(128)S(1)}, s32[2]{0:T(128)}, u32[]{:S(2)}) copy-start(s32[2]{0:T(128)} %valid_ref.1) | copy-start | bytes 28
Sparse Core Ops, SparseCore 0:
  9.4 54.0 all-gather.6
  65.7 80.7 all-gather.8

commit v3 on v2

--- a/solution.py
+++ b/solution.py
@@ -15,7 +15,12 @@
 masked_low = -1e30
 
 
-def patch_kernel(core_ref, time_ref, clean_ref, noise_ref, own_ref, other_ref):
+def in_hbm(array):
+    return pltpu.with_memory_space_constraint(array, pltpu.HBM)
+
+
+def patch_kernel(core_ref, time_ref, clean_ref, noise_ref, after_ref, own_ref, other_ref):
+    del after_ref
     rows, lanes = clean_ref.shape
     row = lax.broadcasted_iota(jnp.int32, (rows, lanes), 0)
     steps = jnp.where(row < rows // 2, time_ref[0], time_ref[1])
@@ -52,7 +57,7 @@
     other_ref[...] = jnp.where(upper, patches[:, :half], patches[:, half:])
 
 
-def make_patches(core, timesteps, clean_latents, noise):
+def make_patches(core, timesteps, clean_latents, noise, after):
     flat = clean_latents.shape[-1]
     smem = pl.BlockSpec(memory_space=pltpu.SMEM)
     vmem = pl.BlockSpec(memory_space=pltpu.VMEM)
@@ -60,15 +65,10 @@
     return pl.pallas_call(
         patch_kernel,
         out_shape=(shape, shape),
-        in_specs=[smem, smem, vmem, vmem],
+        in_specs=[smem, smem, vmem, vmem, pl.BlockSpec(memory_space=pltpu.HBM)],
         out_specs=(vmem, vmem),
-    )(core[None], timesteps, clean_latents.reshape(-1, flat), noise.reshape(-1, flat))
-
-
-def rms_normalize(values, gain):
-    wide = values.astype(jnp.float32)
-    factor = lax.rsqrt(jnp.mean(wide * wide, axis=-1, keepdims=True) + eps_norm)
-    return (wide * factor * gain.astype(jnp.float32)).astype(jnp.bfloat16)
+        compiler_params=pltpu.CompilerParams(vmem_limit_bytes=8 * 1024 * 1024),
+    )(core[None], timesteps, clean_latents.reshape(-1, flat), noise.reshape(-1, flat), in_hbm(after))
 
 
 CTX = ("yh", "z", "core")
@@ -76,14 +76,53 @@
 meta_rows = 16
 score_factor = HD ** (-0.5) * math.log2(math.e)
 key_chunk = 1024
-
-
-def attention_kernel(valid_ref, q_ref, own_ref, kv_ref, bias_ref, out_ref):
-    tokens = q_ref.shape[0]
-    group = q_ref.shape[1] // HD
+column_chunk = 768
+weight_pieces = 6
+embed_pieces = 4
+
+
+def attention_kernel(
+    valid_ref,
+    normed_ref,
+    weight_ref,
+    own_ref,
+    kv_first_ref,
+    kv_second_ref,
+    bias_ref,
+    out_ref,
+    normed_buffer,
+    buffer_ref,
+    normed_sems,
+    sems,
+):
+    tokens, width = normed_ref.shape
+    group = weight_ref.shape[1] // HD
+    depth = width // weight_pieces
+    copies = []
+    for piece in range(weight_pieces):
+        rows = pl.ds(piece * depth, depth)
+        copies.append(
+            (
+                pltpu.make_async_copy(
+                    normed_ref.at[:, rows], normed_buffer.at[:, rows], normed_sems.at[piece]
+                ),
+                pltpu.make_async_copy(weight_ref.at[rows], buffer_ref.at[rows], sems.at[piece]),
+            )
+        )
+        for copy in copies[-1]:
+            copy.start()
     span_rows = tokens // 2
     frame_rows = span_rows // 4
-    q = jnp.concatenate([q_ref[:, g * HD : (g + 1) * HD] for g in range(group)], axis=0)
+    queries = jnp.zeros((tokens, weight_ref.shape[1]), jnp.float32)
+    for piece in range(weight_pieces):
+        for copy in copies[piece]:
+            copy.wait()
+        span = slice(piece * depth, (piece + 1) * depth)
+        queries += jnp.dot(
+            normed_buffer[:, span], buffer_ref[span, :], preferred_element_type=jnp.float32
+        )
+    queries = queries.astype(jnp.bfloat16)
+    q = jnp.concatenate([queries[:, g * HD : (g + 1) * HD] for g in range(group)], axis=0)
 
     def scores_of(keys, bias):
         s = lax.dot_general(q, keys, (((1,), (1,)), ((), ())), preferred_element_type=jnp.float32)
@@ -102,9 +141,12 @@
     total = jnp.sum(raw, axis=1, keepdims=True)
     summed = jnp.dot(raw.astype(jnp.bfloat16), own_ref[:, HD:], preferred_element_type=jnp.float32)
     first = lax.broadcasted_iota(jnp.int32, (tokens, key_chunk), 0) < span_rows
-    for start in range(0, kv_ref.shape[0], key_chunk):
-        keys = kv_ref[start : start + key_chunk, :HD]
-        values = kv_ref[start : start + key_chunk, HD:]
+    key_rows = kv_first_ref.shape[0]
+    for start in range(0, 2 * key_rows, key_chunk):
+        kv_ref = kv_first_ref if start < key_rows else kv_second_ref
+        inside = start % key_rows
+        keys = kv_ref[inside : inside + key_chunk, :HD]
+        values = kv_ref[inside : inside + key_chunk, HD:]
         bias = jnp.where(
             first,
             bias_ref[0:1, start : start + key_chunk],
@@ -128,21 +170,130 @@
         out_ref[:, g * HD : (g + 1) * HD] = jnp.where(live_row, piece, 0.0).astype(jnp.bfloat16)
 
 
-def attention(valid, q, own, kv_all, bias):
+def attention(valid, normed, weight, own, kv_first, kv_second, bias):
     vmem = pl.BlockSpec(memory_space=pltpu.VMEM)
+    hbm = pl.BlockSpec(memory_space=pltpu.HBM)
     return pl.pallas_call(
         attention_kernel,
-        out_shape=jax.ShapeDtypeStruct(q.shape, jnp.bfloat16),
-        in_specs=[pl.BlockSpec(memory_space=pltpu.SMEM), vmem, vmem, vmem, vmem],
+        out_shape=jax.ShapeDtypeStruct((normed.shape[0], weight.shape[1]), jnp.bfloat16),
+        in_specs=[
+            pl.BlockSpec(memory_space=pltpu.SMEM),
+            hbm,
+            hbm,
+            vmem,
+            vmem,
+            vmem,
+            vmem,
+        ],
         out_specs=vmem,
+        scratch_shapes=[
+            pltpu.VMEM(normed.shape, jnp.bfloat16),
+            pltpu.VMEM(weight.shape, jnp.bfloat16),
+            pltpu.SemaphoreType.DMA((weight_pieces,)),
+            pltpu.SemaphoreType.DMA((weight_pieces,)),
+        ],
+        compiler_params=pltpu.CompilerParams(vmem_limit_bytes=20 * 1024 * 1024),
+    )(valid, in_hbm(normed), in_hbm(weight), own, kv_first, kv_second, bias)
+
+
+def embed_kernel(
+    own_patch_ref,
+    other_patch_ref,
+    own_embed_ref,
+    other_embed_ref,
+    position_ref,
+    gain_ref,
+    weight_ref,
+    normed_ref,
+    noisy_ref,
+    clean_ref,
+    embedded_ref,
+    own_buffer,
+    position_buffer,
+    sems,
+    out_sems,
+):
+    tokens, width = position_ref.shape
+    piece_cols = width // embed_pieces
+    copies = []
+    for piece in range(embed_pieces):
+        cols = pl.ds(piece * piece_cols, piece_cols)
+        for index, (source, buffer) in enumerate(
+            (
+                (own_embed_ref, own_buffer),
+                (position_ref, position_buffer),
+            )
+        ):
+            copies.append(
+                pltpu.make_async_copy(source.at[:, cols], buffer.at[:, cols], sems.at[index, piece])
+            )
+            copies[-1].start()
+    patches = jnp.concatenate([own_patch_ref[...], other_patch_ref[...]], axis=1)
+    squares = jnp.zeros((2 * tokens, 1), jnp.float32)
+    for start in range(0, width, column_chunk):
+        cols = slice(start, start + column_chunk)
+        if start % piece_cols == 0:
+            first = 2 * (start // piece_cols)
+            for copy in copies[first : first + 2]:
+                copy.wait()
+        embed = jnp.concatenate([own_buffer[:, cols], other_embed_ref[:, cols]], axis=0)
+        projected = jnp.dot(patches, embed, preferred_element_type=jnp.float32)
+        place = position_buffer[:, cols].astype(jnp.float32)
+        embedded = (projected + jnp.concatenate([place, place], axis=0)).astype(jnp.bfloat16)
+        embedded_ref[:, cols] = embedded
+        wide = embedded.astype(jnp.float32)
+        squares += jnp.sum(wide * wide, axis=1, keepdims=True)
+    factor = lax.rsqrt(squares / width + eps_norm)
+    summed = jnp.zeros((2 * tokens, weight_ref.shape[1]), jnp.float32)
+    stores = []
+    for start in range(0, width, column_chunk):
+        cols = slice(start, start + column_chunk)
+        wide = embedded_ref[:, cols].astype(jnp.float32)
+        normed = (wide * factor * gain_ref[:, cols].astype(jnp.float32)).astype(jnp.bfloat16)
+        embedded_ref[:tokens, cols] = normed[:tokens]
+        if (start + column_chunk) % piece_cols == 0:
+            piece = start // piece_cols
+            done = pl.ds(piece * piece_cols, piece_cols)
+            stores.append(
+                pltpu.make_async_copy(
+                    embedded_ref.at[:tokens, done], normed_ref.at[:, done], out_sems.at[piece]
+                )
+            )
+            stores[-1].start()
+        summed += jnp.dot(normed, weight_ref[cols, :], preferred_element_type=jnp.float32)
+    noisy_ref[...] = summed[:tokens].astype(jnp.bfloat16)
+    clean_ref[...] = summed[tokens:].astype(jnp.bfloat16)
+    for store in stores:
+        store.wait()
+
+
+def embed_tokens(own_patches, other_patches, own_embed, other_embed, position, gain, weight):
+    tokens, width = position.shape
+    vmem = pl.BlockSpec(memory_space=pltpu.VMEM)
+    hbm = pl.BlockSpec(memory_space=pltpu.HBM)
+    kv_shape = jax.ShapeDtypeStruct((tokens, weight.shape[1]), jnp.bfloat16)
+    return pl.pallas_call(
+        embed_kernel,
+        out_shape=(jax.ShapeDtypeStruct((tokens, width), jnp.bfloat16), kv_shape, kv_shape),
+        in_specs=[vmem, vmem, hbm, vmem, hbm, vmem, vmem],
+        out_specs=(hbm, vmem, vmem),
+        scratch_shapes=[
+            pltpu.VMEM((2 * tokens, width), jnp.bfloat16),
+            pltpu.VMEM(own_embed.shape, jnp.bfloat16),
+            pltpu.VMEM(position.shape, jnp.bfloat16),
+            pltpu.SemaphoreType.DMA((2, embed_pieces)),
+            pltpu.SemaphoreType.DMA((embed_pieces,)),
+        ],
         compiler_params=pltpu.CompilerParams(vmem_limit_bytes=24 * 1024 * 1024),
-    )(valid, q, own, kv_all, bias)
-
-
-def add_position(projected, position_rows, tokens):
-    cols = projected.shape[1]
-    doubled = projected.reshape(2, tokens, cols) + position_rows.astype(jnp.float32)[None]
-    return doubled.reshape(2 * tokens, cols).astype(jnp.bfloat16)
+    )(
+        own_patches,
+        other_patches,
+        in_hbm(own_embed),
+        other_embed,
+        in_hbm(position),
+        gain[None],
+        weight,
+    )
 
 
 def on_device(
@@ -182,20 +333,15 @@
     ).reshape(-1, q_cols)
 
     other_embed = lax.ppermute(own_embed, "core", [(0, 1), (1, 0)])
-    own_patches, other_patches = make_patches(core, timesteps, clean_latents, noise)
-    projected = jnp.dot(
-        own_patches, own_embed, preferred_element_type=jnp.float32
-    ) + jnp.dot(other_patches, other_embed, preferred_element_type=jnp.float32)
-    embedded = add_position(projected, position, tokens)
-    normed = rms_normalize(embedded, norm_gain)
-    keys_values = jnp.dot(normed, kv_full, preferred_element_type=jnp.float32).astype(jnp.bfloat16)
-
-    clean_pair = lax.all_gather(keys_values[tokens:].astype(jnp.float16), "yh", axis=0)
-    kv_all = (
-        lax.all_gather(clean_pair, ("z", "core"), axis=1, tiled=True)
-        .reshape(-1, kv_cols)
-        .astype(jnp.bfloat16)
+    own_patches, other_patches = make_patches(core, timesteps, clean_latents, noise, own_embed)
+    normed_noisy, noisy_kv, clean_kv = embed_tokens(
+        own_patches, other_patches, own_embed, other_embed, position, norm_gain, kv_full
     )
+
+    clean_pair = lax.all_gather(clean_kv.astype(jnp.float16), "yh", axis=0)
+    clean_all = lax.all_gather(clean_pair, ("z", "core"), axis=1, tiled=True)
+    kv_first = clean_all[0].astype(jnp.bfloat16)
+    kv_second = clean_all[1].astype(jnp.bfloat16)
 
     key_order = meta_all[:, :slots].reshape(-1)
     key_valid = meta_all[:, slots:].reshape(-1)
@@ -204,10 +350,7 @@
     earlier = (key_order[None, :] < span_order[:, None])[:, :, None]
     bias = jnp.where(live & earlier, 0.0, masked_low).reshape(slots, -1)
 
-    queries = jnp.dot(normed[:tokens], q_full, preferred_element_type=jnp.float32)
-    return attention(
-        valid_frames, queries.astype(jnp.bfloat16), keys_values[:tokens], kv_all, bias
-    )
+    return attention(valid_frames, normed_noisy, q_full, noisy_kv, kv_first, kv_second, bias)
 
 
 def solution(mesh):

time: 169 us -> 170 us (level)
  matrix products: 8.93 us -> 0 us
  Pallas kernels: 8.85 us -> 17.5 us
  local copies, waits for them, and re-layouts: 6.36 us -> 10.5 us
  blocking collectives: 117 us -> 115 us
    pallas_call x1 -> x2, Pallas kernels: 6.48 us -> 16 us  [the longest x1 9.62 us: attention(): pl.pallas_call(attention_kernel, out_shape=jax.ShapeDtypeStruct((normed.s...]
    dot_general x4 -> x0, matrix products: 8.93 us -> none  [the longest x1 3.95 us: on_device(): jnp.dot(normed[:tokens], q_full, preferred_element_type=jnp.float32)]
    unnamed x22 -> x28, local copies, waits for them, and re-layouts: 4.11 us -> 7.78 us
    all_gather x2, blocking collectives: 60 us -> 58 us  [the longest x1 52.7 us: on_device(): clean_all = lax.all_gather(clean_pair, ('z', 'core'), axis=1, tiled=True)]
    convert_element_type x1, other arithmetic: 4.4 us -> 2.69 us  [on_device(): kv_full = kv_gathered[:, :rows].astype(jnp.bfloat16).reshape(-1, kv_cols)]
    convert_element_type x4 -> x2, other arithmetic: 3.79 us -> 2.24 us  [the longest x1 2.22 us: on_device(): kv_second = clean_all[1].astype(jnp.bfloat16)]
  transfers between devices with their start and end apart: 3 -> 3, of which waited for: 1 -> 0; matrix products, arithmetic and copies ran while one was open for 10% -> 7% of each run, Pallas kernels for 1% -> 5%
where the time goes in v3:
time: 170 us; the launch traced here: 168 us
  blocking collectives  115 us (68%)
  Pallas kernels  17.5 us (10%)
  between operations  13.6 us (8%)
  local copies, waits for them, and re-layouts  10.5 us (6%)
  other arithmetic  9.48 us (6%)
  starting transfers between devices  2.1 us (1%)
    all_gather x1, blocking collectives, on_device(): clean_all = lax.all_gather(clean_pair, ('z', 'core'), axis=1, tiled=True)  52.7 us
    all_gather x1, blocking collectives, on_device(): lax.all_gather(weights_pair[:, :, q_cols:], ('z', 'core'), axis=1, tiled=...  50.3 us
    pallas_call x1, Pallas kernels, attention(): pl.pallas_call(attention_kernel, out_shape=jax.ShapeDtypeStruct((normed.s...  9.62 us
    unnamed x28, local copies, waits for them, and re-layouts  7.78 us
    all_gather x1, blocking collectives, on_device(): lax.all_gather(jnp.concatenate([weights, meta_block], axis=0), 'yh', axis=0)  6.89 us
    pallas_call x1, Pallas kernels, embed_tokens(): pl.pallas_call(embed_kernel, out_shape=(jax.ShapeDtypeStruct((tokens, wid...  6.4 us
    all_gather x1, blocking collectives, on_device(): clean_pair = lax.all_gather(clean_kv.astype(jnp.float16), 'yh', axis=0)  5.3 us
  transfers between devices with their start and end apart: 3, of which 0 were waited for; matrix products, arithmetic and copies ran while one was open for 7% of the time, Pallas kernels for 5%

profile of v3, /device:TPU:1, one launch (start us, length us, event | category | flops | bytes accessed | tf_op | source)
XLA Modules:
  0.0 168.5 jit_solution(17177517518279244759)
XLA Ops:
  6.5 0.0 copy-start
  6.5 0.0 copy-start.12
  6.5 0.0 all-gather.7.cloned.1.call-start
  6.5 1.0 copy-done
  7.5 0.7 constant_dynamic-slice_fusion
  8.2 0.0 all-gather.7.cloned.1.call-update
  8.2 0.0 all-gather.9.cloned.1.call-start
  8.3 0.7 convert_bitcast_fusion
  9.0 0.1 fusion.8
  9.0 0.9 maximum_convert_fusion
  10.0 6.9 %all-gather = f16[224,640]{1,0:T(8,128)(2,1)S(1)} all-gather(f16[112,640]{1,0:T(8,128)(2,1)S(1)} %pad_maximum_fusion), channel_id=2, replica_groups=mesh['yh'=2,'z'=16,'core'=2,'x'=4,'yl'=2] {'yh'}, dimensions={0}, use_global_device_ids=true | all-gather | bytes 430080 | tf_op jit(solution)/shard_map/all_gather | solution.py:325
  16.9 0.7 slice_convert_fusion.3
  17.6 0.0 all-gather.9.cloned.1.call-update
  17.7 0.0 copy-done.12
  17.7 0.6 broadcast_in_dim.20.gain_ref
  18.3 0.0 copy-start.13
  18.3 50.3 %all-gather.10 = f16[2,3584,256]{2,1,0:T(8,128)(2,1)S(1)} all-gather(f16[2,112,256]{2,1,0:T(8,128)(2,1)S(1)} %slice.32), channel_id=1, replica_groups=mesh['yh'=2,'z'=16,'core'=2,'x'=4,'yl'=2] {'z','core'}, dimensions={1}, use_global_device_ids=true | all-gather | bytes 3784704 | tf_op jit(solution)/shard_map/all_gather | solution.py:326
  68.6 0.0 copy-start.11
  68.6 1.9 %copy-done.11 = f16[2,3584,256]{2,1,0:T(8,128)(2,1)} copy-done((f16[2,3584,256]{2,1,0:T(8,128)(2,1)}, f16[2,3584,256]{2,1,0:T(8,128)(2,1)S(1)}, u32[]{:S(2)}) %copy-start.11) | copy-done | bytes 3670040
  70.5 0.1 fusion.10
  70.6 0.1 lt.48
  70.7 0.1 lt.49
  70.8 0.1 lt.50
  70.9 0.1 lt.47
  71.0 0.1 lt.52
  71.1 0.0 copy-done.13
  71.1 0.1 broadcast_compare_fusion
  71.2 0.1 and.32
  71.3 0.7 and.33
  72.1 0.6 lt.51
  72.7 0.0 copy-start.7
  72.7 2.7 %slice_convert_fusion = bf16[64,96,256]{2,1,0:T(8,128)(2,1)S(1)} fusion(f16[64,112,256]{2,1,0:T(8,128)(2,1)} %bitcast.23), kind=kLoop, calls=%fused_computation | loop fusion | flops 1572864 | bytes 6291456 | tf_op jit(solution)/shard_map/convert_element_type | solution.py:329
  75.4 0.0 all-gather.7.cloned.1.call-done.after_ref.own_embed_ref
  75.4 2.1 %collective-permute-start = (bf16[128,6144]{1,0:T(8,128)(2,1)}, bf16[128,6144]{1,0:T(8,128)(2,1)S(1)}, u32[]{:S(2)}, u32[]{:S(2)}) collective-permute-start(bf16[128,6144]{1,0:T(8,128)(2,1)} %all-gather.7.cloned.1.call-done.after_ref.own_embed_ref), channel_id=1, source_target_pairs={{0,8},{8,0},{1,9},{9,1},{2,10},{10,2},{3,11},{11,3},{4,12},{12,4},... | collective-permute-start | bytes 4718600 | tf_op jit(solution)/shard_map/ppermute | solution.py:335
  77.5 1.4 and_select_fusion.bias_ref
  78.9 0.0 copy-done.7
  78.9 0.0 copy-start.8
  78.9 0.7 copy-done.8
  79.6 0.0 copy-start.10
  79.6 0.7 copy-done.10
  80.3 1.5 shard_map.100
  81.8 0.0 collective-permute-done.other_embed_ref
  81.8 0.0 copy-start.4
  81.8 0.7 copy-done.4
  82.6 6.4 %shard_map.101 = (bf16[128,6144]{1,0:T(8,128)(2,1)S(1)}, bf16[128,256]{1,0:T(8,128)(2,1)S(1)}, bf16[128,256]{1,0:T(8,128)(2,1)S(1)}) custom-call(bf16[256,128]{1,0:T(8,128)(2,1)S(1)} %get-tuple-element.10.own_patch_ref, bf16[256,128]{1,0:T(8,128)(2,1)S(1)} %get-tuple-element.11.other_patch_ref, ...), custom_call_target="tpu_custom_call" | custom-call | tf_op jit(solution)/shard_map/pallas_call | solution.py:275
  89.0 0.0 copy-start.2
  89.0 1.2 copy-done.2
  90.2 0.0 copy-start.5
  90.2 5.3 %all-gather.1 = f16[256,256]{1,0:T(8,128)(2,1)S(1)} all-gather(f16[128,256]{1,0:T(8,128)(2,1)S(1)} %convert_element_type.45), channel_id=3, replica_groups=mesh['yh'=2,'z'=16,'core'=2,'x'=4,'yl'=2] {'yh'}, dimensions={0}, use_global_device_ids=true | all-gather | bytes 196608 | tf_op jit(solution)/shard_map/all_gather | solution.py:341
  95.5 0.0 copy-done.5
  95.5 52.7 %all-gather.11 = f16[2,4096,256]{2,1,0:T(8,128)(2,1)S(1)} all-gather(f16[2,128,256]{2,1,0:T(8,128)(2,1)S(1)} %bitcast.27), channel_id=1, replica_groups=mesh['yh'=2,'z'=16,'core'=2,'x'=4,'yl'=2] {'z','core'}, dimensions={1}, use_global_device_ids=true | all-gather | bytes 4325376 | tf_op jit(solution)/shard_map/all_gather | solution.py:342
  148.2 0.0 copy-start.3
  148.2 0.0 copy-start.6
  148.2 0.0 copy-start.9
  148.2 2.2 %fusion = (bf16[4096,256]{1,0:T(8,128)(2,1)S(1)}, bf16[4096,256]{1,0:T(8,128)(2,1)}) fusion(f16[2,4096,256]{2,1,0:T(8,128)(2,1)S(1)} %all-gather.11), kind=kLoop, calls=%fused_computation.2 | loop fusion | flops 2097152 | bytes 8388608 | tf_op jit(solution)/shard_map/convert_element_type | solution.py:344
  150.4 0.0 all-gather.9.cloned.1.call-done
  150.4 0.0 copy-done.3
  150.4 0.0 copy-done.6
  150.4 0.0 copy-done.9
  150.4 0.0 copy-start.1
  150.4 1.6 copy-done.1
  152.0 9.6 %shard_map.102 = bf16[128,384]{1,0:T(8,128)(2,1)} custom-call(s32[2]{0:T(128)S(1)} %copy-done.9, bf16[128,6144]{1,0:T(8,128)(2,1)} %copy-done.2, bf16[6144,384]{1,0:T(8,128)(2,1)} %bitcast.24, bf16[128,256]{1,0:T(8,128)(2,1)S(1)} %copy-done.6, bf16[4096,256]{1,0:T(8,128)(2,1)S(1)} %copy-done.1, bf16[4096,256]{1,0:T(8,128)(2,1)S(1)} %get-tuple-element.15.kv_second_ref, ...), custom_call_target="tpu_custom_call" | custom-call | tf_op jit(solution)/shard_map/pallas_call | solution.py:176
  (6 shorter events, 0.1 us)
Async XLA Ops:
  6.5 1.0 copy-start
  6.5 11.1 %copy-start.12 = (bf16[6144]{0:T(1024)(128)(2,1)S(1)}, bf16[6144]{0:T(1024)(128)(2,1)}, u32[]{:S(2)}) copy-start(bf16[6144]{0:T(1024)(128)(2,1)} %param.17) | copy-start | bytes 36868
  6.5 68.8 %all-gather.7.cloned.1.call-start = ((), (), s32[]{:S(2)}) async-start(), calls=%async_computation | async-start | bytes 1769472 | tf_op jit(solution)/shard_map/all_gather | solution.py:317
  8.2 142.2 %all-gather.9.cloned.1.call-start = ((), (), s32[]{:S(2)}) async-start(), calls=%async_computation.1 | async-start | bytes 4866048 | tf_op jit(solution)/shard_map/all_gather | solution.py:331
  18.3 52.8 %copy-start.13 = (s32[2]{0:T(128)S(1)}, s32[2]{0:T(128)}, u32[]{:S(2)}) copy-start(s32[2]{0:T(128)} %param.13) | copy-start | bytes 28
  68.6 1.9 %copy-start.11 = (f16[2,3584,256]{2,1,0:T(8,128)(2,1)}, f16[2,3584,256]{2,1,0:T(8,128)(2,1)S(1)}, u32[]{:S(2)}) copy-start(f16[2,3584,256]{2,1,0:T(8,128)(2,1)S(1)} %all-gather.10) | copy-start | bytes 11010052
  72.7 6.2 %copy-start.7 = (bf16[2,4,8,128]{3,2,1,0:T(8,128)(2,1)S(1)}, bf16[2,4,8,128]{3,2,1,0:T(8,128)(2,1)}, u32[]{:S(2)}) copy-start(bf16[2,4,8,128]{3,2,1,0:T(8,128)(2,1)} %param.10) | copy-start | bytes 49156
  75.4 6.4 %collective-permute-start = (bf16[128,6144]{1,0:T(8,128)(2,1)}, bf16[128,6144]{1,0:T(8,128)(2,1)S(1)}, u32[]{:S(2)}, u32[]{:S(2)}) collective-permute-start(bf16[128,6144]{1,0:T(8,128)(2,1)} %all-gather.7.cloned.1.call-done.after_ref.own_embed_ref), channel_id=1, source_target_pairs={{0,8},{8,0},{1,9},{9,1},{2,10},{10,2},{3,11},{11,3},{4,12},{12,4},... | collective-permute-start | bytes 4718600 | tf_op jit(solution)/shard_map/ppermute | solution.py:335
  78.9 0.7 copy-start.8
  79.6 0.7 copy-start.10
  81.8 0.7 copy-start.4
  89.0 1.2 copy-start.2
  90.2 5.3 %copy-start.5 = (bf16[128,256]{1,0:T(8,128)(2,1)}, bf16[128,256]{1,0:T(8,128)(2,1)S(1)}, u32[]{:S(2)}) copy-start(bf16[128,256]{1,0:T(8,128)(2,1)S(1)} %get-tuple-element.13.own_ref) | copy-start | bytes 196612
  148.2 2.2 %copy-start.3 = (f32[2,8192]{1,0:T(2,128)S(1)}, f32[2,8192]{1,0:T(2,128)}, u32[]{:S(2)}) copy-start(f32[2,8192]{1,0:T(2,128)} %and_select_fusion.bias_ref) | copy-start | bytes 196612
  148.2 2.2 %copy-start.6 = (bf16[128,256]{1,0:T(8,128)(2,1)S(1)}, bf16[128,256]{1,0:T(8,128)(2,1)}, u32[]{:S(2)}) copy-start(bf16[128,256]{1,0:T(8,128)(2,1)} %copy-done.5) | copy-start | bytes 196612
  148.2 2.2 %copy-start.9 = (s32[2]{0:T(128)S(1)}, s32[2]{0:T(128)}, u32[]{:S(2)}) copy-start(s32[2]{0:T(128)} %valid_ref.1) | copy-start | bytes 28
  150.4 1.6 copy-start.1
Sparse Core Ops, SparseCore 0:
  9.4 54.0 all-gather.6
  65.6 81.5 all-gather.8

commit v4 on v3

--- a/solution.py
+++ b/solution.py
@@ -19,12 +19,22 @@
     return pltpu.with_memory_space_constraint(array, pltpu.HBM)
 
 
-def patch_kernel(core_ref, time_ref, clean_ref, noise_ref, after_ref, own_ref, other_ref):
+def patch_kernel(
+    scalar_ref, clean_hbm, noise_hbm, after_ref, own_ref, other_ref, clean_ref, noise_ref, sems
+):
     del after_ref
+    loads = [
+        pltpu.make_async_copy(clean_hbm, clean_ref, sems.at[0]),
+        pltpu.make_async_copy(noise_hbm, noise_ref, sems.at[1]),
+    ]
+    for load in loads:
+        load.start()
     rows, lanes = clean_ref.shape
     row = lax.broadcasted_iota(jnp.int32, (rows, lanes), 0)
-    steps = jnp.where(row < rows // 2, time_ref[0], time_ref[1])
+    steps = jnp.where(row < rows // 2, scalar_ref[1], scalar_ref[2])
     level = (steps.astype(jnp.float32) + 1.0) / 1000.0
+    for load in loads:
+        load.wait()
     clean = clean_ref[...]
     noisy = (
         (1.0 - level) * clean.astype(jnp.float32) + level * noise_ref[...].astype(jnp.float32)
@@ -52,23 +62,34 @@
         result += jnp.dot(pick, jnp.concatenate(shifted, axis=0), preferred_element_type=jnp.float32)
     patches = result.astype(jnp.bfloat16)
     half = patches.shape[1] // 2
-    upper = core_ref[0] == 1
+    upper = scalar_ref[0] == 1
     own_ref[...] = jnp.where(upper, patches[:, half:], patches[:, :half])
     other_ref[...] = jnp.where(upper, patches[:, :half], patches[:, half:])
 
 
-def make_patches(core, timesteps, clean_latents, noise, after):
+def make_patches(scalars, clean_latents, noise, after):
     flat = clean_latents.shape[-1]
-    smem = pl.BlockSpec(memory_space=pltpu.SMEM)
+    rows = clean_latents.size // flat
+    hbm = pl.BlockSpec(memory_space=pltpu.HBM)
     vmem = pl.BlockSpec(memory_space=pltpu.VMEM)
     shape = jax.ShapeDtypeStruct((256, 128), jnp.bfloat16)
     return pl.pallas_call(
         patch_kernel,
         out_shape=(shape, shape),
-        in_specs=[smem, smem, vmem, vmem, pl.BlockSpec(memory_space=pltpu.HBM)],
+        in_specs=[pl.BlockSpec(memory_space=pltpu.SMEM), hbm, hbm, hbm],
         out_specs=(vmem, vmem),
+        scratch_shapes=[
+            pltpu.VMEM((rows, flat), jnp.bfloat16),
+            pltpu.VMEM((rows, flat), jnp.bfloat16),
+            pltpu.SemaphoreType.DMA((2,)),
+        ],
         compiler_params=pltpu.CompilerParams(vmem_limit_bytes=8 * 1024 * 1024),
-    )(core[None], timesteps, clean_latents.reshape(-1, flat), noise.reshape(-1, flat), in_hbm(after))
+    )(
+        scalars,
+        in_hbm(clean_latents.reshape(rows, flat)),
+        in_hbm(noise.reshape(rows, flat)),
+        in_hbm(after),
+    )
 
 
 CTX = ("yh", "z", "core")
@@ -82,19 +103,22 @@
 
 
 def attention_kernel(
-    valid_ref,
+    scalar_ref,
     normed_ref,
     weight_ref,
     own_ref,
-    kv_first_ref,
-    kv_second_ref,
-    bias_ref,
+    kv_hbm,
+    meta_ref,
     out_ref,
     normed_buffer,
     buffer_ref,
+    kv_ref,
     normed_sems,
     sems,
+    kv_sems,
 ):
+    orders = (scalar_ref[3], scalar_ref[4])
+    valids = (scalar_ref[5], scalar_ref[6])
     tokens, width = normed_ref.shape
     group = weight_ref.shape[1] // HD
     depth = width // weight_pieces
@@ -113,6 +137,38 @@
             copy.start()
     span_rows = tokens // 2
     frame_rows = span_rows // 4
+    kv_copies = []
+    for piece in range(kv_ref.shape[0] // key_chunk):
+        rows = pl.ds(piece * key_chunk, key_chunk)
+        kv_copies.append(
+            pltpu.make_async_copy(kv_hbm.at[rows], kv_ref.at[rows], kv_sems.at[piece])
+        )
+        kv_copies[-1].start()
+    meta = meta_ref[...].astype(jnp.bfloat16)
+    blocks = meta.shape[0]
+    block_row = lax.broadcasted_iota(jnp.int32, (blocks, key_chunk), 0)
+    block_col = lax.broadcasted_iota(jnp.int32, (blocks, key_chunk), 1)
+    key_place = lax.broadcasted_iota(jnp.int32, (1, key_chunk), 1)
+    second = (key_place & span_rows) != 0
+    key_frame = ((key_place & (span_rows - 1)) // frame_rows).astype(jnp.float32)
+    biases = []
+    for piece in range(kv_ref.shape[0] // key_chunk):
+        pick = block_row == ((block_col + piece * key_chunk) // tokens)
+        spread = lax.dot_general(
+            meta,
+            jnp.where(pick, 1.0, 0.0).astype(jnp.bfloat16),
+            (((0,), (0,)), ((), ())),
+            preferred_element_type=jnp.float32,
+        )
+        key_order = jnp.where(second, spread[1:2], spread[0:1])
+        key_valid = jnp.where(second, spread[3:4], spread[2:3])
+        live = key_frame < key_valid
+        biases.append(
+            [
+                jnp.where(live & (key_order < order.astype(jnp.float32)), 0.0, masked_low)
+                for order in orders
+            ]
+        )
     queries = jnp.zeros((tokens, weight_ref.shape[1]), jnp.float32)
     for piece in range(weight_pieces):
         for copy in copies[piece]:
@@ -131,7 +187,7 @@
 
     row = lax.broadcasted_iota(jnp.int32, (tokens, tokens), 0)
     col = lax.broadcasted_iota(jnp.int32, (tokens, tokens), 1)
-    valid_col = jnp.where(col < span_rows, valid_ref[0], valid_ref[1])
+    valid_col = jnp.where(col < span_rows, valids[0], valids[1])
     same = (row < span_rows) == (col < span_rows)
     live_col = lax.rem(col, span_rows) < valid_col * frame_rows
     own_bias = jnp.where(same & live_col, 0.0, masked_low)
@@ -141,17 +197,11 @@
     total = jnp.sum(raw, axis=1, keepdims=True)
     summed = jnp.dot(raw.astype(jnp.bfloat16), own_ref[:, HD:], preferred_element_type=jnp.float32)
     first = lax.broadcasted_iota(jnp.int32, (tokens, key_chunk), 0) < span_rows
-    key_rows = kv_first_ref.shape[0]
-    for start in range(0, 2 * key_rows, key_chunk):
-        kv_ref = kv_first_ref if start < key_rows else kv_second_ref
-        inside = start % key_rows
-        keys = kv_ref[inside : inside + key_chunk, :HD]
-        values = kv_ref[inside : inside + key_chunk, HD:]
-        bias = jnp.where(
-            first,
-            bias_ref[0:1, start : start + key_chunk],
-            bias_ref[1:2, start : start + key_chunk],
-        )
+    for start in range(0, kv_ref.shape[0], key_chunk):
+        kv_copies[start // key_chunk].wait()
+        keys = kv_ref[start : start + key_chunk, :HD]
+        values = kv_ref[start : start + key_chunk, HD:]
+        bias = jnp.where(first, biases[start // key_chunk][0], biases[start // key_chunk][1])
         s = scores_of(keys, bias)
         new_largest = jnp.maximum(largest, jnp.max(s, axis=1, keepdims=True))
         raw = jnp.exp2(s - new_largest)
@@ -163,37 +213,32 @@
         largest = new_largest
     result = summed / total
     token = lax.broadcasted_iota(jnp.int32, (tokens, HD), 0)
-    valid_row = jnp.where(token < span_rows, valid_ref[0], valid_ref[1])
+    valid_row = jnp.where(token < span_rows, valids[0], valids[1])
     live_row = lax.rem(token, span_rows) < valid_row * frame_rows
     for g in range(group):
         piece = result[g * tokens : (g + 1) * tokens]
         out_ref[:, g * HD : (g + 1) * HD] = jnp.where(live_row, piece, 0.0).astype(jnp.bfloat16)
 
 
-def attention(valid, normed, weight, own, kv_first, kv_second, bias):
+def attention(scalars, normed, weight, own, kv_all, meta):
+    smem = pl.BlockSpec(memory_space=pltpu.SMEM)
     vmem = pl.BlockSpec(memory_space=pltpu.VMEM)
     hbm = pl.BlockSpec(memory_space=pltpu.HBM)
     return pl.pallas_call(
         attention_kernel,
         out_shape=jax.ShapeDtypeStruct((normed.shape[0], weight.shape[1]), jnp.bfloat16),
-        in_specs=[
-            pl.BlockSpec(memory_space=pltpu.SMEM),
-            hbm,
-            hbm,
-            vmem,
-            vmem,
-            vmem,
-            vmem,
-        ],
+        in_specs=[smem, hbm, hbm, vmem, hbm, vmem],
         out_specs=vmem,
         scratch_shapes=[
             pltpu.VMEM(normed.shape, jnp.bfloat16),
             pltpu.VMEM(weight.shape, jnp.bfloat16),
+            pltpu.VMEM(kv_all.shape, jnp.bfloat16),
             pltpu.SemaphoreType.DMA((weight_pieces,)),
             pltpu.SemaphoreType.DMA((weight_pieces,)),
+            pltpu.SemaphoreType.DMA((kv_all.shape[0] // key_chunk,)),
         ],
-        compiler_params=pltpu.CompilerParams(vmem_limit_bytes=20 * 1024 * 1024),
-    )(valid, in_hbm(normed), in_hbm(weight), own, kv_first, kv_second, bias)
+        compiler_params=pltpu.CompilerParams(vmem_limit_bytes=32 * 1024 * 1024),
+    )(scalars, in_hbm(normed), in_hbm(weight), own, in_hbm(kv_all), meta)
 
 
 def embed_kernel(
@@ -229,7 +274,7 @@
             )
             copies[-1].start()
     patches = jnp.concatenate([own_patch_ref[...], other_patch_ref[...]], axis=1)
-    squares = jnp.zeros((2 * tokens, 1), jnp.float32)
+    squares = jnp.zeros((2 * tokens, 128), jnp.float32)
     for start in range(0, width, column_chunk):
         cols = slice(start, start + column_chunk)
         if start % piece_cols == 0:
@@ -242,8 +287,9 @@
         embedded = (projected + jnp.concatenate([place, place], axis=0)).astype(jnp.bfloat16)
         embedded_ref[:, cols] = embedded
         wide = embedded.astype(jnp.float32)
-        squares += jnp.sum(wide * wide, axis=1, keepdims=True)
-    factor = lax.rsqrt(squares / width + eps_norm)
+        for lane in range(0, column_chunk, 128):
+            squares += wide[:, lane : lane + 128] * wide[:, lane : lane + 128]
+    factor = lax.rsqrt(jnp.sum(squares, axis=1, keepdims=True) / width + eps_norm)
     summed = jnp.zeros((2 * tokens, weight_ref.shape[1]), jnp.float32)
     stores = []
     for start in range(0, width, column_chunk):
@@ -274,7 +320,7 @@
     kv_shape = jax.ShapeDtypeStruct((tokens, weight.shape[1]), jnp.bfloat16)
     return pl.pallas_call(
         embed_kernel,
-        out_shape=(jax.ShapeDtypeStruct((tokens, width), jnp.bfloat16), kv_shape, kv_shape),
+        out_shape=(pltpu.HBM((tokens, width), jnp.bfloat16), kv_shape, kv_shape),
         in_specs=[vmem, vmem, hbm, vmem, hbm, vmem, vmem],
         out_specs=(hbm, vmem, vmem),
         scratch_shapes=[
@@ -308,12 +354,10 @@
     query_weight,
     kv_weight,
 ):
-    slots, frames, height, flat = clean_latents.shape
-    frame_rows = height // 2 * (flat // (2 * CH))
-    span_rows = frames * frame_rows
-    tokens = slots * span_rows
+    slots = clean_latents.shape[0]
     core = lax.axis_index("core")
     half = embed_weight.shape[0] // 2
+    scalars = in_hbm(jnp.concatenate([core[None], timesteps, span_order, valid_frames]))
     own_embed = lax.all_gather(
         lax.dynamic_slice_in_dim(embed_weight, core * half, half, 0), HEAD, axis=1, tiled=True
     )
@@ -326,31 +370,23 @@
     kv_gathered = lax.all_gather(
         weights_pair[:, :, q_cols:], ("z", "core"), axis=1, tiled=True
     ).reshape(-1, rows + meta_rows, kv_cols)
+    kv_gathered, own_embed = lax.optimization_barrier((kv_gathered, own_embed))
     kv_full = kv_gathered[:, :rows].astype(jnp.bfloat16).reshape(-1, kv_cols)
-    meta_all = kv_gathered[:, rows, : 2 * slots].astype(jnp.float32).astype(jnp.int32)
+    meta_all = jnp.sum(kv_gathered[:, rows:, : 2 * slots].astype(jnp.float32), axis=1)
     q_full = lax.all_gather(
         weights_pair[:, :rows, :q_cols].astype(jnp.bfloat16), ("z", "core"), axis=1, tiled=True
     ).reshape(-1, q_cols)
 
     other_embed = lax.ppermute(own_embed, "core", [(0, 1), (1, 0)])
-    own_patches, other_patches = make_patches(core, timesteps, clean_latents, noise, own_embed)
+    own_patches, other_patches = make_patches(scalars, clean_latents, noise, own_embed)
     normed_noisy, noisy_kv, clean_kv = embed_tokens(
         own_patches, other_patches, own_embed, other_embed, position, norm_gain, kv_full
     )
 
     clean_pair = lax.all_gather(clean_kv.astype(jnp.float16), "yh", axis=0)
     clean_all = lax.all_gather(clean_pair, ("z", "core"), axis=1, tiled=True)
-    kv_first = clean_all[0].astype(jnp.bfloat16)
-    kv_second = clean_all[1].astype(jnp.bfloat16)
-
-    key_order = meta_all[:, :slots].reshape(-1)
-    key_valid = meta_all[:, slots:].reshape(-1)
-    frame = jnp.arange(span_rows, dtype=jnp.int32) // frame_rows
-    live = (frame[None, :] < key_valid[:, None])[None]
-    earlier = (key_order[None, :] < span_order[:, None])[:, :, None]
-    bias = jnp.where(live & earlier, 0.0, masked_low).reshape(slots, -1)
-
-    return attention(valid_frames, normed_noisy, q_full, noisy_kv, kv_first, kv_second, bias)
+    kv_all = clean_all.astype(jnp.bfloat16).reshape(-1, kv_cols)
+    return attention(scalars, normed_noisy, q_full, noisy_kv, kv_all, meta_all)
 
 
 def solution(mesh):

time: 170 us -> 169 us (level)
  local copies, waits for them, and re-layouts: 10.5 us -> 1.7 us
  blocking collectives: 115 us -> 120 us
  Pallas kernels: 17.5 us -> 20.8 us
    unnamed x28 -> x10, local copies, waits for them, and re-layouts: 7.78 us -> 0.96 us
    all_gather x1, blocking collectives: 52.7 us -> 56.3 us  [on_device(): clean_all = lax.all_gather(clean_pair, ('z', 'core'), axis=1, tiled=True)]
    pallas_call x1, Pallas kernels: 9.62 us -> 12.7 us  [attention(): pl.pallas_call(attention_kernel, out_shape=jax.ShapeDtypeStruct((normed.s...]
  transfers between devices with their start and end apart: 3 -> 3, of which waited for: 0 -> 0; matrix products, arithmetic and copies ran while one was open for 7% -> 6% of each run, Pallas kernels for 5% -> 5%
where the time goes in v4:
time: 169 us; the launch traced here: 168 us
  blocking collectives  120 us (71%)
  Pallas kernels  20.8 us (12%)
  between operations  13.6 us (8%)
  other arithmetic  9.63 us (6%)
  starting transfers between devices  2.13 us (1%)
  local copies, waits for them, and re-layouts  1.7 us (1%)
    all_gather x1, blocking collectives, on_device(): clean_all = lax.all_gather(clean_pair, ('z', 'core'), axis=1, tiled=True)  56.3 us
    all_gather x1, blocking collectives, on_device(): lax.all_gather(weights_pair[:, :, q_cols:], ('z', 'core'), axis=1, tiled=...  51.3 us
    pallas_call x1, Pallas kernels, attention(): pl.pallas_call(attention_kernel, out_shape=jax.ShapeDtypeStruct((normed.s...  12.7 us
    all_gather x1, blocking collectives, on_device(): lax.all_gather(jnp.concatenate([weights, meta_block], axis=0), 'yh', axis=0)  6.89 us
    pallas_call x1, Pallas kernels, embed_tokens(): pl.pallas_call(embed_kernel, out_shape=(pltpu.HBM((tokens, width), jnp.bf...  5.7 us
    all_gather x1, blocking collectives, on_device(): clean_pair = lax.all_gather(clean_kv.astype(jnp.float16), 'yh', axis=0)  5.3 us
  transfers between devices with their start and end apart: 3, of which 0 were waited for; matrix products, arithmetic and copies ran while one was open for 6% of the time, Pallas kernels for 5%

profile of v4, /device:TPU:1, one launch (start us, length us, event | category | flops | bytes accessed | tf_op | source)
XLA Modules:
  0.0 167.6 jit_solution(16283430725492806356)
XLA Ops:
  6.5 0.0 copy-start
  6.5 0.0 copy-start.3
  6.5 0.0 copy-start.2
  6.5 0.0 copy-start.1
  6.5 0.0 copy-start.4
  6.5 0.0 all-gather.7.cloned.1.call-start
  6.6 0.9 copy-done
  7.5 0.7 constant_dynamic-slice_fusion
  8.2 0.0 all-gather.7.cloned.1.call-update
  8.3 0.0 all-gather.9.cloned.1.call-start
  8.3 0.7 convert_bitcast_fusion
  9.0 0.1 fusion.5
  9.1 0.9 maximum_convert_fusion
  10.1 6.9 %all-gather = f16[224,640]{1,0:T(8,128)(2,1)S(1)} all-gather(f16[112,640]{1,0:T(8,128)(2,1)S(1)} %pad_maximum_fusion), channel_id=2, replica_groups=mesh['yh'=2,'z'=16,'core'=2,'x'=4,'yl'=2] {'yh'}, dimensions={0}, use_global_device_ids=true | all-gather | bytes 430080 | tf_op jit(solution)/shard_map/all_gather | solution.py:369
  17.0 0.7 slice_convert_fusion.1
  17.6 0.0 all-gather.9.cloned.1.call-update
  17.7 51.3 %all-gather.10 = f16[2,3584,256]{2,1,0:T(8,128)(2,1)} all-gather(f16[2,112,256]{2,1,0:T(8,128)(2,1)S(1)} %slice.16), channel_id=1, replica_groups=mesh['yh'=2,'z'=16,'core'=2,'x'=4,'yl'=2] {'z','core'}, dimensions={1}, use_global_device_ids=true | all-gather | bytes 3784704 | tf_op jit(solution)/shard_map/all_gather | solution.py:370
  69.0 0.0 all-gather.7.cloned.1.call-done.after_ref.own_embed_ref
  69.0 2.0 %collective-permute-start = (bf16[128,6144]{1,0:T(8,128)(2,1)}, bf16[128,6144]{1,0:T(8,128)(2,1)S(1)}, u32[]{:S(2)}, u32[]{:S(2)}) collective-permute-start(bf16[128,6144]{1,0:T(8,128)(2,1)} %all-gather.7.cloned.1.call-done.after_ref.own_embed_ref), channel_id=1, source_target_pairs={{0,8},{8,0},{1,9},{9,1},{2,10},{10,2},{3,11},{11,3},{4,12},{12,4},... | collective-permute-start | bytes 4718600 | tf_op jit(solution)/shard_map/ppermute | solution.py:380
  71.0 0.0 copy-done.1
  71.1 0.0 copy-done.3
  71.1 0.0 copy-done.2
  71.1 0.0 copy-done.4
  71.1 0.6 pad_add_fusion.scalar_ref
  71.7 2.4 %shard_map.100 = (bf16[256,128]{1,0:T(8,128)(2,1)S(1)}, bf16[256,128]{1,0:T(8,128)(2,1)S(1)}) custom-call(s32[7]{0:T(128)} %pad_add_fusion.scalar_ref, bf16[64,128]{1,0:T(8,128)(2,1)} %bitcast.21, bf16[64,128]{1,0:T(8,128)(2,1)} %bitcast.22, bf16[128,6144]{1,0:T(8,128)(2,1)} %all-gather.7.cloned.1.call-done.after_ref.own_embed_ref), custom_call_target="tpu_custom_call" | custom-call | tf_op jit(solution)/shard_map/pallas_call | solution.py:76
  74.1 1.1 convert_reduce_fusion.meta_ref
  75.2 2.6 %slice_convert_fusion = bf16[64,96,256]{2,1,0:T(8,128)(2,1)S(1)} fusion(f16[64,112,256]{2,1,0:T(8,128)(2,1)} %bitcast.16), kind=kLoop, calls=%fused_computation | loop fusion | flops 1572864 | bytes 6291456 | tf_op jit(solution)/shard_map/convert_element_type | solution.py:374
  77.8 0.0 collective-permute-done.other_embed_ref
  77.9 5.7 %shard_map.101 = (bf16[128,6144]{1,0:T(8,128)(2,1)}, bf16[128,256]{1,0:T(8,128)(2,1)S(1)}, bf16[128,256]{1,0:T(8,128)(2,1)S(1)}) custom-call(bf16[256,128]{1,0:T(8,128)(2,1)S(1)} %get-tuple-element.13.own_patch_ref, bf16[256,128]{1,0:T(8,128)(2,1)S(1)} %get-tuple-element.14.other_patch_ref, ...), custom_call_target="tpu_custom_call" | custom-call | tf_op jit(solution)/shard_map/pallas_call | solution.py:321
  83.6 5.3 %all-gather.1 = f16[256,256]{1,0:T(8,128)(2,1)S(1)} all-gather(f16[128,256]{1,0:T(8,128)(2,1)S(1)} %convert_element_type.31), channel_id=3, replica_groups=mesh['yh'=2,'z'=16,'core'=2,'x'=4,'yl'=2] {'yh'}, dimensions={0}, use_global_device_ids=true | all-gather | bytes 196608 | tf_op jit(solution)/shard_map/all_gather | solution.py:386
  88.9 56.3 %all-gather.11 = f16[2,4096,256]{2,1,0:T(8,128)(2,1)S(1)} all-gather(f16[2,128,256]{2,1,0:T(8,128)(2,1)S(1)} %bitcast.20), channel_id=1, replica_groups=mesh['yh'=2,'z'=16,'core'=2,'x'=4,'yl'=2] {'z','core'}, dimensions={1}, use_global_device_ids=true | all-gather | bytes 4325376 | tf_op jit(solution)/shard_map/all_gather | solution.py:387
  145.2 2.9 %convert_element_type.32 = bf16[2,4096,256]{2,1,0:T(8,128)(2,1)} convert(f16[2,4096,256]{2,1,0:T(8,128)(2,1)S(1)} %all-gather.11) | non-fusion elementwise | flops 2097152 | bytes 8388608 | tf_op jit(solution)/shard_map/convert_element_type | solution.py:388
  148.1 0.0 all-gather.9.cloned.1.call-done
  148.1 12.7 %shard_map.102 = bf16[128,384]{1,0:T(8,128)(2,1)} custom-call(s32[7]{0:T(128)} %pad_add_fusion.scalar_ref, bf16[128,6144]{1,0:T(8,128)(2,1)} %get-tuple-element.16.normed_ref, bf16[6144,384]{1,0:T(8,128)(2,1)} %bitcast.17, bf16[128,256]{1,0:T(8,128)(2,1)S(1)} %get-tuple-element.17.own_ref, bf16[8192,256]{1,0:T(8,128)(2,1)} %bitcast.14, ...), custom_call_target="tpu_custom_call" | custom-call | tf_op jit(solution)/shard_map/pallas_call | solution.py:227
  (4 shorter events, 0.1 us)
Async XLA Ops:
  6.5 1.0 copy-start
  6.5 64.5 %copy-start.3 = (s32[2]{0:T(128)S(1)}, s32[2]{0:T(128)}, u32[]{:S(2)}) copy-start(s32[2]{0:T(128)} %param.13) | copy-start | bytes 28
  6.5 64.5 %copy-start.2 = (s32[2]{0:T(128)S(1)}, s32[2]{0:T(128)}, u32[]{:S(2)}) copy-start(s32[2]{0:T(128)} %param.14) | copy-start | bytes 28
  6.5 64.5 %copy-start.1 = (bf16[6144]{0:T(1024)(128)(2,1)S(1)}, bf16[6144]{0:T(1024)(128)(2,1)}, u32[]{:S(2)}) copy-start(bf16[6144]{0:T(1024)(128)(2,1)} %param.17) | copy-start | bytes 36868
  6.5 64.5 %copy-start.4 = (s32[2]{0:T(128)S(1)}, s32[2]{0:T(128)}, u32[]{:S(2)}) copy-start(s32[2]{0:T(128)} %param.12) | copy-start | bytes 28
  6.5 62.4 %all-gather.7.cloned.1.call-start = ((), (), s32[]{:S(2)}) async-start(), calls=%async_computation | async-start | bytes 1769472 | tf_op jit(solution)/shard_map/all_gather | solution.py:361
  8.3 139.8 %all-gather.9.cloned.1.call-start = ((), (), s32[]{:S(2)}) async-start(), calls=%async_computation.1 | async-start | bytes 4866048 | tf_op jit(solution)/shard_map/all_gather | solution.py:376
  69.0 8.9 %collective-permute-start = (bf16[128,6144]{1,0:T(8,128)(2,1)}, bf16[128,6144]{1,0:T(8,128)(2,1)S(1)}, u32[]{:S(2)}, u32[]{:S(2)}) collective-permute-start(bf16[128,6144]{1,0:T(8,128)(2,1)} %all-gather.7.cloned.1.call-done.after_ref.own_embed_ref), channel_id=1, source_target_pairs={{0,8},{8,0},{1,9},{9,1},{2,10},{10,2},{3,11},{11,3},{4,12},{12,4},... | collective-permute-start | bytes 4718600 | tf_op jit(solution)/shard_map/ppermute | solution.py:380
Sparse Core Ops, SparseCore 0:
  9.5 54.0 all-gather.6
  65.7 80.5 all-gather.8

commit v5 on v4

--- a/solution.py
+++ b/solution.py
@@ -94,54 +94,31 @@
 
 CTX = ("yh", "z", "core")
 HEAD = ("x", "yl")
-meta_rows = 16
+meta_rows = 8
 score_factor = HD ** (-0.5) * math.log2(math.e)
 key_chunk = 1024
 column_chunk = 768
-weight_pieces = 6
 embed_pieces = 4
 
 
 def attention_kernel(
-    scalar_ref,
-    normed_ref,
-    weight_ref,
-    own_ref,
-    kv_hbm,
-    meta_ref,
-    out_ref,
-    normed_buffer,
-    buffer_ref,
-    kv_ref,
-    normed_sems,
-    sems,
-    kv_sems,
+    scalar_ref, query_ref, own_ref, kv_hbm, meta_ref, out_ref, kv_ref, kv_sems
 ):
     orders = (scalar_ref[3], scalar_ref[4])
     valids = (scalar_ref[5], scalar_ref[6])
-    tokens, width = normed_ref.shape
-    group = weight_ref.shape[1] // HD
-    depth = width // weight_pieces
-    copies = []
-    for piece in range(weight_pieces):
-        rows = pl.ds(piece * depth, depth)
-        copies.append(
-            (
-                pltpu.make_async_copy(
-                    normed_ref.at[:, rows], normed_buffer.at[:, rows], normed_sems.at[piece]
-                ),
-                pltpu.make_async_copy(weight_ref.at[rows], buffer_ref.at[rows], sems.at[piece]),
-            )
-        )
-        for copy in copies[-1]:
-            copy.start()
+    tokens = query_ref.shape[0]
+    group = query_ref.shape[1] // HD
     span_rows = tokens // 2
     frame_rows = span_rows // 4
     kv_copies = []
-    for piece in range(kv_ref.shape[0] // key_chunk):
-        rows = pl.ds(piece * key_chunk, key_chunk)
+    chunk_blocks = key_chunk // tokens
+    chunks = kv_ref.shape[0] // chunk_blocks
+    for piece in range(chunks):
+        part = pl.ds(piece * chunk_blocks, chunk_blocks)
         kv_copies.append(
-            pltpu.make_async_copy(kv_hbm.at[rows], kv_ref.at[rows], kv_sems.at[piece])
+            pltpu.make_async_copy(
+                kv_hbm.at[part, pl.ds(0, tokens)], kv_ref.at[part], kv_sems.at[piece]
+            )
         )
         kv_copies[-1].start()
     meta = meta_ref[...].astype(jnp.bfloat16)
@@ -152,7 +129,7 @@
     second = (key_place & span_rows) != 0
     key_frame = ((key_place & (span_rows - 1)) // frame_rows).astype(jnp.float32)
     biases = []
-    for piece in range(kv_ref.shape[0] // key_chunk):
+    for piece in range(chunks):
         pick = block_row == ((block_col + piece * key_chunk) // tokens)
         spread = lax.dot_general(
             meta,
@@ -169,15 +146,7 @@
                 for order in orders
             ]
         )
-    queries = jnp.zeros((tokens, weight_ref.shape[1]), jnp.float32)
-    for piece in range(weight_pieces):
-        for copy in copies[piece]:
-            copy.wait()
-        span = slice(piece * depth, (piece + 1) * depth)
-        queries += jnp.dot(
-            normed_buffer[:, span], buffer_ref[span, :], preferred_element_type=jnp.float32
-        )
-    queries = queries.astype(jnp.bfloat16)
+    queries = query_ref[...]
     q = jnp.concatenate([queries[:, g * HD : (g + 1) * HD] for g in range(group)], axis=0)
 
     def scores_of(keys, bias):
@@ -197,11 +166,13 @@
     total = jnp.sum(raw, axis=1, keepdims=True)
     summed = jnp.dot(raw.astype(jnp.bfloat16), own_ref[:, HD:], preferred_element_type=jnp.float32)
     first = lax.broadcasted_iota(jnp.int32, (tokens, key_chunk), 0) < span_rows
-    for start in range(0, kv_ref.shape[0], key_chunk):
-        kv_copies[start // key_chunk].wait()
-        keys = kv_ref[start : start + key_chunk, :HD]
-        values = kv_ref[start : start + key_chunk, HD:]
-        bias = jnp.where(first, biases[start // key_chunk][0], biases[start // key_chunk][1])
+    for piece in range(chunks):
+        kv_copies[piece].wait()
+        block = kv_ref[piece * chunk_blocks : (piece + 1) * chunk_blocks]
+        block = block.reshape(key_chunk, 2 * HD)
+        keys = block[:, :HD]
+        values = block[:, HD:]
+        bias = jnp.where(first, biases[piece][0], biases[piece][1])
         s = scores_of(keys, bias)
         new_largest = jnp.maximum(largest, jnp.max(s, axis=1, keepdims=True))
         raw = jnp.exp2(s - new_largest)
@@ -220,25 +191,22 @@
         out_ref[:, g * HD : (g + 1) * HD] = jnp.where(live_row, piece, 0.0).astype(jnp.bfloat16)
 
 
-def attention(scalars, normed, weight, own, kv_all, meta):
-    smem = pl.BlockSpec(memory_space=pltpu.SMEM)
+def attention(scalars, queries, own, kv_all, meta):
     vmem = pl.BlockSpec(memory_space=pltpu.VMEM)
     hbm = pl.BlockSpec(memory_space=pltpu.HBM)
+    tokens = queries.shape[0]
+    blocks, unused, kv_cols = kv_all.shape
     return pl.pallas_call(
         attention_kernel,
-        out_shape=jax.ShapeDtypeStruct((normed.shape[0], weight.shape[1]), jnp.bfloat16),
-        in_specs=[smem, hbm, hbm, vmem, hbm, vmem],
+        out_shape=jax.ShapeDtypeStruct(queries.shape, jnp.bfloat16),
+        in_specs=[pl.BlockSpec(memory_space=pltpu.SMEM), vmem, vmem, hbm, vmem],
         out_specs=vmem,
         scratch_shapes=[
-            pltpu.VMEM(normed.shape, jnp.bfloat16),
-            pltpu.VMEM(weight.shape, jnp.bfloat16),
-            pltpu.VMEM(kv_all.shape, jnp.bfloat16),
-            pltpu.SemaphoreType.DMA((weight_pieces,)),
-            pltpu.SemaphoreType.DMA((weight_pieces,)),
-            pltpu.SemaphoreType.DMA((kv_all.shape[0] // key_chunk,)),
+            pltpu.VMEM((blocks, tokens, kv_cols), jnp.bfloat16),
+            pltpu.SemaphoreType.DMA((blocks * tokens // key_chunk,)),
         ],
-        compiler_params=pltpu.CompilerParams(vmem_limit_bytes=32 * 1024 * 1024),
-    )(scalars, in_hbm(normed), in_hbm(weight), own, in_hbm(kv_all), meta)
+        compiler_params=pltpu.CompilerParams(vmem_limit_bytes=28 * 1024 * 1024),
+    )(scalars, queries, own, in_hbm(kv_all), meta)
 
 
 def embed_kernel(
@@ -361,21 +329,14 @@
     own_embed = lax.all_gather(
         lax.dynamic_slice_in_dim(embed_weight, core * half, half, 0), HEAD, axis=1, tiled=True
     )
-    rows, kv_cols = kv_weight.shape
+    kv_cols = kv_weight.shape[1]
     q_cols = query_weight.shape[1]
     weights = jnp.concatenate([query_weight, kv_weight], axis=1).astype(jnp.float16)
-    meta = jnp.concatenate([span_order, valid_frames]).astype(jnp.float16)
-    meta_block = jnp.pad(meta[None, :], ((0, meta_rows - 1), (q_cols, kv_cols - 2 * slots)))
-    weights_pair = lax.all_gather(jnp.concatenate([weights, meta_block], axis=0), "yh", axis=0)
-    kv_gathered = lax.all_gather(
-        weights_pair[:, :, q_cols:], ("z", "core"), axis=1, tiled=True
-    ).reshape(-1, rows + meta_rows, kv_cols)
-    kv_gathered, own_embed = lax.optimization_barrier((kv_gathered, own_embed))
-    kv_full = kv_gathered[:, :rows].astype(jnp.bfloat16).reshape(-1, kv_cols)
-    meta_all = jnp.sum(kv_gathered[:, rows:, : 2 * slots].astype(jnp.float32), axis=1)
-    q_full = lax.all_gather(
-        weights_pair[:, :rows, :q_cols].astype(jnp.bfloat16), ("z", "core"), axis=1, tiled=True
-    ).reshape(-1, q_cols)
+    weights_pair = lax.all_gather(weights, "yh", axis=0)
+    gathered = lax.all_gather(weights_pair, ("z", "core"), axis=1, tiled=True)
+    gathered, own_embed = lax.optimization_barrier((gathered, own_embed))
+    gathered = gathered.reshape(-1, q_cols + kv_cols)
+    kv_full = gathered[:, q_cols:].astype(jnp.bfloat16)
 
     other_embed = lax.ppermute(own_embed, "core", [(0, 1), (1, 0)])
     own_patches, other_patches = make_patches(scalars, clean_latents, noise, own_embed)
@@ -383,10 +344,21 @@
         own_patches, other_patches, own_embed, other_embed, position, norm_gain, kv_full
     )
 
-    clean_pair = lax.all_gather(clean_kv.astype(jnp.float16), "yh", axis=0)
+    queries = jnp.dot(
+        normed_noisy,
+        gathered[:, :q_cols].astype(jnp.bfloat16),
+        preferred_element_type=jnp.float32,
+    ).astype(jnp.bfloat16)
+
+    tokens = clean_kv.shape[0]
+    meta = jnp.concatenate([span_order, valid_frames]).astype(jnp.float16)
+    meta_block = jnp.pad(meta[None, :], ((0, meta_rows - 1), (0, kv_cols - 2 * slots)))
+    clean = jnp.concatenate([clean_kv.astype(jnp.float16), meta_block], axis=0)
+    clean_pair = lax.all_gather(clean, "yh", axis=0)
     clean_all = lax.all_gather(clean_pair, ("z", "core"), axis=1, tiled=True)
-    kv_all = clean_all.astype(jnp.bfloat16).reshape(-1, kv_cols)
-    return attention(scalars, normed_noisy, q_full, noisy_kv, kv_all, meta_all)
+    clean_all = clean_all.reshape(-1, tokens + meta_rows, kv_cols)
+    meta_all = jnp.sum(clean_all[:, tokens:, : 2 * slots].astype(jnp.float32), axis=1)
+    return attention(scalars, queries, noisy_kv, clean_all.astype(jnp.bfloat16), meta_all)
 
 
 def solution(mesh):

time: 169 us -> 169 us (level)
  blocking collectives: 120 us -> 124 us
  Pallas kernels: 20.8 us -> 17.6 us
  other arithmetic: 9.63 us -> 7.82 us
    all_gather x3, blocking collectives: 63.5 us -> 79 us  [the longest x1 67 us: on_device(): gathered = lax.all_gather(weights_pair, ('z', 'core'), axis=1, tiled=True)]
    all_gather x1, blocking collectives: 56.3 us -> 45.1 us  [on_device(): clean_all = lax.all_gather(clean_pair, ('z', 'core'), axis=1, tiled=True)]
    pallas_call x1, Pallas kernels: 12.7 us -> 9.39 us  [attention(): pl.pallas_call(attention_kernel, out_shape=jax.ShapeDtypeStruct(queries.s...]
    convert_element_type x4 -> x3, other arithmetic: 6.21 us -> 5.35 us  [the longest x1 2.95 us: on_device(): clean_all.astype(jnp.bfloat16)]
  transfers between devices with their start and end apart: 3 -> 2, of which waited for: 0 -> 0; matrix products, arithmetic and copies ran while one was open for 6% -> 3% of each run, Pallas kernels for 5% -> 1%
where the time goes in v5:
time: 169 us
  blocking collectives  124 us (73%)
  Pallas kernels  17.6 us (10%)
  between operations  13.5 us (8%)
  other arithmetic  7.82 us (5%)
  local copies, waits for them, and re-layouts  2.43 us (1%)
  starting transfers between devices  2.04 us (1%)
    all_gather x1, blocking collectives, on_device(): gathered = lax.all_gather(weights_pair, ('z', 'core'), axis=1, tiled=True)  67 us
    all_gather x1, blocking collectives, on_device(): clean_all = lax.all_gather(clean_pair, ('z', 'core'), axis=1, tiled=True)  45.1 us
    pallas_call x1, Pallas kernels, attention(): pl.pallas_call(attention_kernel, out_shape=jax.ShapeDtypeStruct(queries.s...  9.39 us
    all_gather x1, blocking collectives, on_device(): weights_pair = lax.all_gather(weights, 'yh', axis=0)  6.67 us
    pallas_call x1, Pallas kernels, embed_tokens(): pl.pallas_call(embed_kernel, out_shape=(pltpu.HBM((tokens, width), jnp.bf...  5.82 us
    all_gather x1, blocking collectives, on_device(): clean_pair = lax.all_gather(clean, 'yh', axis=0)  5.34 us
  transfers between devices with their start and end apart: 2, of which 0 were waited for; matrix products, arithmetic and copies ran while one was open for 3% of the time, Pallas kernels for 1%

profile of v5, /device:TPU:1, one launch (start us, length us, event | category | flops | bytes accessed | tf_op | source)
XLA Modules:
  0.0 168.5 jit_solution(3958193026993464314)
XLA Ops:
  6.5 0.0 copy-start
  6.5 0.0 all-gather.5.cloned.1.call-start
  6.5 1.0 copy-done
  7.5 0.7 constant_dynamic-slice_fusion
  8.2 0.0 copy-start.1
  8.2 0.0 copy-start.2
  8.2 0.0 copy-start.3
  8.2 0.0 all-gather.5.cloned.1.call-update
  8.3 1.0 maximum_convert_fusion
  9.2 6.7 %all_gather.19 = f16[2,96,640]{2,1,0:T(8,128)(2,1)S(1)} all-gather(f16[1,96,640]{2,1,0:T(8,128)(2,1)S(1)} %maximum_convert_fusion), channel_id=1, replica_groups=mesh['yh'=2,'z'=16,'core'=2,'x'=4,'yl'=2] {'yh'}, dimensions={0}, use_global_device_ids=true | all-gather | bytes 368640 | tf_op jit(solution)/shard_map/all_gather | solution.py:335
  15.9 0.7 broadcast_in_dim.8.gain_ref
  16.6 0.7 convert_bitcast_fusion
  17.3 0.1 fusion.7
  17.4 67.0 %all-gather.6 = f16[2,3072,640]{2,1,0:T(8,128)(2,1)} all-gather(f16[2,96,640]{2,1,0:T(8,128)(2,1)S(1)} %all_gather.19), channel_id=1, replica_groups=mesh['yh'=2,'z'=16,'core'=2,'x'=4,'yl'=2] {'z','core'}, dimensions={1}, use_global_device_ids=true | all-gather | bytes 8110080 | tf_op jit(solution)/shard_map/all_gather | solution.py:336
  84.3 0.0 all-gather.5.cloned.1.call-done.after_ref.own_embed_ref
  84.3 2.0 %collective-permute-start = (bf16[128,6144]{1,0:T(8,128)(2,1)}, bf16[128,6144]{1,0:T(8,128)(2,1)S(1)}, u32[]{:S(2)}, u32[]{:S(2)}) collective-permute-start(bf16[128,6144]{1,0:T(8,128)(2,1)} %all-gather.5.cloned.1.call-done.after_ref.own_embed_ref), channel_id=1, source_target_pairs={{0,8},{8,0},{1,9},{9,1},{2,10},{10,2},{3,11},{11,3},{4,12},{12,4},... | collective-permute-start | bytes 4718600 | tf_op jit(solution)/shard_map/ppermute | solution.py:341
  86.4 0.0 copy-done.1
  86.4 0.0 copy-done.2
  86.4 0.0 copy-done.3
  86.4 0.7 pad_add_fusion.scalar_ref
  87.1 2.4 %shard_map.100 = (bf16[256,128]{1,0:T(8,128)(2,1)S(1)}, bf16[256,128]{1,0:T(8,128)(2,1)S(1)}) custom-call(s32[7]{0:T(128)} %pad_add_fusion.scalar_ref, bf16[64,128]{1,0:T(8,128)(2,1)} %bitcast.22, bf16[64,128]{1,0:T(8,128)(2,1)} %bitcast.23, bf16[128,6144]{1,0:T(8,128)(2,1)} %all-gather.5.cloned.1.call-done.after_ref.own_embed_ref), custom_call_target="tpu_custom_call" | custom-call | tf_op jit(solution)/shard_map/pallas_call | solution.py:76
  89.5 2.4 %slice_convert_fusion.2.weight_ref = bf16[6144,256]{1,0:T(8,128)(2,1)S(1)} fusion(f16[6144,640]{1,0:T(8,128)(2,1)} %bitcast.15), kind=kLoop, calls=%fused_computation.2 | loop fusion | flops 1572864 | bytes 6291456 | tf_op jit(solution)/shard_map/convert_element_type | solution.py:339
  91.9 0.0 collective-permute-done.other_embed_ref
  91.9 0.0 slice-start
  91.9 5.8 %shard_map.101 = (bf16[128,6144]{1,0:T(8,128)(2,1)}, bf16[128,256]{1,0:T(8,128)(2,1)S(1)}, bf16[128,256]{1,0:T(8,128)(2,1)S(1)}) custom-call(bf16[256,128]{1,0:T(8,128)(2,1)S(1)} %get-tuple-element.13.own_patch_ref, bf16[256,128]{1,0:T(8,128)(2,1)S(1)} %get-tuple-element.14.other_patch_ref, ...), custom_call_target="tpu_custom_call" | custom-call | tf_op jit(solution)/shard_map/pallas_call | solution.py:289
  97.8 5.3 %all-gather = f16[272,256]{1,0:T(8,128)(2,1)S(1)} all-gather(f16[136,256]{1,0:T(8,128)(2,1)S(1)} %pad_maximum_fusion), channel_id=2, replica_groups=mesh['yh'=2,'z'=16,'core'=2,'x'=4,'yl'=2] {'yh'}, dimensions={0}, use_global_device_ids=true | all-gather | bytes 208896 | tf_op jit(solution)/shard_map/all_gather | solution.py:357
  103.1 0.0 slice-start.1
  103.1 45.1 %all-gather.7 = f16[2,4352,256]{2,1,0:T(8,128)(2,1)S(1)} all-gather(f16[2,136,256]{2,1,0:T(8,128)(2,1)S(1)} %bitcast.19), channel_id=1, replica_groups=mesh['yh'=2,'z'=16,'core'=2,'x'=4,'yl'=2] {'z','core'}, dimensions={1}, use_global_device_ids=true | all-gather | bytes 4595712 | tf_op jit(solution)/shard_map/all_gather | solution.py:358
  148.2 0.0 copy-start.4
  148.2 2.9 %convert_element_type.43.kv_hbm = bf16[64,136,256]{2,1,0:T(8,128)(2,1)} convert(f16[64,136,256]{2,1,0:T(8,128)(2,1)S(1)} %bitcast.13) | non-fusion elementwise | flops 2228224 | bytes 8912896 | tf_op jit(solution)/shard_map/convert_element_type | solution.py:361
  151.2 0.1 convert_reduce_fusion.meta_ref
  151.3 0.0 slice-done
  151.3 0.0 slice-done.1
  151.3 0.0 copy-done.4
  151.3 1.0 fusion.1.query_ref
  152.3 9.4 %shard_map.102 = bf16[128,384]{1,0:T(8,128)(2,1)} custom-call(s32[7]{0:T(128)} %pad_add_fusion.scalar_ref, bf16[128,384]{1,0:T(8,128)(2,1)S(1)} %fusion.1.query_ref, bf16[128,256]{1,0:T(8,128)(2,1)S(1)} %get-tuple-element.17.own_ref, bf16[64,136,256]{2,1,0:T(8,128)(2,1)} %convert_element_type.43.kv_hbm, f32[64,4]{1,0:T(8,128)S(1)} %convert_reduce_fusion.meta_ref), custom_call_target="tpu_custom_call" | custom-call | tf_op jit(solution)/shard_map/pallas_call | solution.py:199
  (3 shorter events, 0.0 us)
Async XLA Ops:
  6.5 1.0 copy-start
  6.5 77.8 %all-gather.5.cloned.1.call-start = ((), (), s32[]{:S(2)}) async-start(), calls=%async_computation | async-start | bytes 1769472 | tf_op jit(solution)/shard_map/all_gather | solution.py:329
  8.2 78.2 %copy-start.1 = (s32[2]{0:T(128)S(1)}, s32[2]{0:T(128)}, u32[]{:S(2)}) copy-start(s32[2]{0:T(128)} %param.14) | copy-start | bytes 28
  8.2 78.2 %copy-start.2 = (s32[2]{0:T(128)S(1)}, s32[2]{0:T(128)}, u32[]{:S(2)}) copy-start(s32[2]{0:T(128)} %param.13) | copy-start | bytes 28
  8.2 78.2 %copy-start.3 = (s32[2]{0:T(128)S(1)}, s32[2]{0:T(128)}, u32[]{:S(2)}) copy-start(s32[2]{0:T(128)} %param.12) | copy-start | bytes 28
  84.3 7.5 %collective-permute-start = (bf16[128,6144]{1,0:T(8,128)(2,1)}, bf16[128,6144]{1,0:T(8,128)(2,1)S(1)}, u32[]{:S(2)}, u32[]{:S(2)}) collective-permute-start(bf16[128,6144]{1,0:T(8,128)(2,1)} %all-gather.5.cloned.1.call-done.after_ref.own_embed_ref), channel_id=1, source_target_pairs={{0,8},{8,0},{1,9},{9,1},{2,10},{10,2},{3,11},{11,3},{4,12},{12,4},... | collective-permute-start | bytes 4718600 | tf_op jit(solution)/shard_map/ppermute | solution.py:341
  91.9 59.4 %slice-start = ((s8[7864320]{0:T(1024)(128)(4,1)}), s8[4194304]{0:T(1024)(128)(4,1)S(1)}, s32[]{:S(2)}) async-start(s8[7864320]{0:T(1024)(128)(4,1)} %bitcast.16), calls=%async_computation.1 | async-start | bytes 8388608
  103.1 48.2 %slice-start.1 = ((s8[7864320]{0:T(1024)(128)(4,1)}), s8[3670016]{0:T(1024)(128)(4,1)S(1)}, s32[]{:S(2)}) async-start(s8[7864320]{0:T(1024)(128)(4,1)} %bitcast.16), calls=%async_computation.2 | async-start | bytes 7340032
  148.2 3.1 %copy-start.4 = (bf16[128,6144]{1,0:T(8,128)(2,1)S(1)}, bf16[128,6144]{1,0:T(8,128)(2,1)}, u32[]{:S(2)}) copy-start(bf16[128,6144]{1,0:T(8,128)(2,1)} %get-tuple-element.16) | copy-start | bytes 4718596
Sparse Core Ops, SparseCore 0:
  9.4 53.8 all-gather.4

commit v6 on v5

--- a/solution.py
+++ b/solution.py
@@ -20,7 +20,7 @@
 
 
 def patch_kernel(
-    scalar_ref, clean_hbm, noise_hbm, after_ref, own_ref, other_ref, clean_ref, noise_ref, sems
+    time_ref, clean_hbm, noise_hbm, after_ref, own_ref, other_ref, clean_ref, noise_ref, sems
 ):
     del after_ref
     loads = [
@@ -31,7 +31,7 @@
         load.start()
     rows, lanes = clean_ref.shape
     row = lax.broadcasted_iota(jnp.int32, (rows, lanes), 0)
-    steps = jnp.where(row < rows // 2, scalar_ref[1], scalar_ref[2])
+    steps = jnp.where(row < rows // 2, time_ref[0], time_ref[1])
     level = (steps.astype(jnp.float32) + 1.0) / 1000.0
     for load in loads:
         load.wait()
@@ -62,12 +62,12 @@
         result += jnp.dot(pick, jnp.concatenate(shifted, axis=0), preferred_element_type=jnp.float32)
     patches = result.astype(jnp.bfloat16)
     half = patches.shape[1] // 2
-    upper = scalar_ref[0] == 1
+    upper = lax.axis_index("core") == 1
     own_ref[...] = jnp.where(upper, patches[:, half:], patches[:, :half])
     other_ref[...] = jnp.where(upper, patches[:, :half], patches[:, half:])
 
 
-def make_patches(scalars, clean_latents, noise, after):
+def make_patches(timesteps, clean_latents, noise, after):
     flat = clean_latents.shape[-1]
     rows = clean_latents.size // flat
     hbm = pl.BlockSpec(memory_space=pltpu.HBM)
@@ -85,7 +85,7 @@
         ],
         compiler_params=pltpu.CompilerParams(vmem_limit_bytes=8 * 1024 * 1024),
     )(
-        scalars,
+        in_hbm(timesteps),
         in_hbm(clean_latents.reshape(rows, flat)),
         in_hbm(noise.reshape(rows, flat)),
         in_hbm(after),
@@ -102,17 +102,15 @@
 
 
 def attention_kernel(
-    scalar_ref, query_ref, own_ref, kv_hbm, meta_ref, out_ref, kv_ref, kv_sems
+    order_ref, valid_ref, query_ref, own_ref, kv_hbm, meta_ref, out_ref, kv_ref, kv_sems
 ):
-    orders = (scalar_ref[3], scalar_ref[4])
-    valids = (scalar_ref[5], scalar_ref[6])
     tokens = query_ref.shape[0]
     group = query_ref.shape[1] // HD
     span_rows = tokens // 2
     frame_rows = span_rows // 4
+    chunk_blocks = key_chunk // span_rows
+    chunks = kv_ref.shape[0] // chunk_blocks
     kv_copies = []
-    chunk_blocks = key_chunk // tokens
-    chunks = kv_ref.shape[0] // chunk_blocks
     for piece in range(chunks):
         part = pl.ds(piece * chunk_blocks, chunk_blocks)
         kv_copies.append(
@@ -121,59 +119,42 @@
             )
         )
         kv_copies[-1].start()
-    meta = meta_ref[...].astype(jnp.bfloat16)
-    blocks = meta.shape[0]
-    block_row = lax.broadcasted_iota(jnp.int32, (blocks, key_chunk), 0)
-    block_col = lax.broadcasted_iota(jnp.int32, (blocks, key_chunk), 1)
-    key_place = lax.broadcasted_iota(jnp.int32, (1, key_chunk), 1)
-    second = (key_place & span_rows) != 0
-    key_frame = ((key_place & (span_rows - 1)) // frame_rows).astype(jnp.float32)
-    biases = []
-    for piece in range(chunks):
-        pick = block_row == ((block_col + piece * key_chunk) // tokens)
-        spread = lax.dot_general(
-            meta,
-            jnp.where(pick, 1.0, 0.0).astype(jnp.bfloat16),
-            (((0,), (0,)), ((), ())),
-            preferred_element_type=jnp.float32,
-        )
-        key_order = jnp.where(second, spread[1:2], spread[0:1])
-        key_valid = jnp.where(second, spread[3:4], spread[2:3])
-        live = key_frame < key_valid
-        biases.append(
-            [
-                jnp.where(live & (key_order < order.astype(jnp.float32)), 0.0, masked_low)
-                for order in orders
-            ]
-        )
-    queries = query_ref[...]
-    q = jnp.concatenate([queries[:, g * HD : (g + 1) * HD] for g in range(group)], axis=0)
-
-    def scores_of(keys, bias):
-        s = lax.dot_general(q, keys, (((1,), (1,)), ((), ())), preferred_element_type=jnp.float32)
-        s = s.reshape(group, tokens, keys.shape[0]) * score_factor + bias[None]
-        return s.reshape(group * tokens, keys.shape[0])
-
-    row = lax.broadcasted_iota(jnp.int32, (tokens, tokens), 0)
-    col = lax.broadcasted_iota(jnp.int32, (tokens, tokens), 1)
-    valid_col = jnp.where(col < span_rows, valids[0], valids[1])
-    same = (row < span_rows) == (col < span_rows)
-    live_col = lax.rem(col, span_rows) < valid_col * frame_rows
-    own_bias = jnp.where(same & live_col, 0.0, masked_low)
-    s = scores_of(own_ref[:, :HD], own_bias)
-    largest = jnp.max(s, axis=1, keepdims=True)
-    raw = jnp.exp2(s - largest)
-    total = jnp.sum(raw, axis=1, keepdims=True)
-    summed = jnp.dot(raw.astype(jnp.bfloat16), own_ref[:, HD:], preferred_element_type=jnp.float32)
-    first = lax.broadcasted_iota(jnp.int32, (tokens, key_chunk), 0) < span_rows
-    for piece in range(chunks):
-        kv_copies[piece].wait()
-        block = kv_ref[piece * chunk_blocks : (piece + 1) * chunk_blocks]
-        block = block.reshape(key_chunk, 2 * HD)
-        keys = block[:, :HD]
-        values = block[:, HD:]
-        bias = jnp.where(first, biases[piece][0], biases[piece][1])
-        s = scores_of(keys, bias)
+    swap, orders, valids = ordered_spans(order_ref, valid_ref)
+    queries = swap_spans(query_ref[...], swap)
+    own = swap_spans(own_ref[...], swap)
+    q = jnp.concatenate(
+        [
+            queries[slot * span_rows : (slot + 1) * span_rows, g * HD : (g + 1) * HD]
+            for slot in range(2)
+            for g in range(group)
+        ],
+        axis=0,
+    )
+    slot_rows = group * span_rows
+
+    def scores_of(rows, keys):
+        return lax.dot_general(
+            rows, keys, (((1,), (1,)), ((), ())), preferred_element_type=jnp.float32
+        )
+
+    col = lax.broadcasted_iota(jnp.int32, (1, tokens), 1)
+    states = []
+    for slot in range(2):
+        inside = (col >= slot * span_rows) & (
+            col < slot * span_rows + valids[slot] * frame_rows
+        )
+        s = scores_of(q[slot * slot_rows : (slot + 1) * slot_rows], own[:, :HD]) * score_factor
+        s += jnp.where(inside, 0.0, masked_low)
+        largest = jnp.max(s, axis=1, keepdims=True)
+        raw = jnp.exp2(s - largest)
+        total = jnp.sum(raw, axis=1, keepdims=True)
+        summed = jnp.dot(
+            raw.astype(jnp.bfloat16), own[:, HD:], preferred_element_type=jnp.float32
+        )
+        states.append((largest, total, summed))
+
+    def fold(state, s, values):
+        largest, total, summed = state
         new_largest = jnp.maximum(largest, jnp.max(s, axis=1, keepdims=True))
         raw = jnp.exp2(s - new_largest)
         factor = jnp.exp2(largest - new_largest)
@@ -181,17 +162,56 @@
         summed = summed * factor + jnp.dot(
             raw.astype(jnp.bfloat16), values, preferred_element_type=jnp.float32
         )
-        largest = new_largest
-    result = summed / total
-    token = lax.broadcasted_iota(jnp.int32, (tokens, HD), 0)
-    valid_row = jnp.where(token < span_rows, valids[0], valids[1])
-    live_row = lax.rem(token, span_rows) < valid_row * frame_rows
-    for g in range(group):
-        piece = result[g * tokens : (g + 1) * tokens]
-        out_ref[:, g * HD : (g + 1) * HD] = jnp.where(live_row, piece, 0.0).astype(jnp.bfloat16)
-
-
-def attention(scalars, queries, own, kv_all, meta):
+        return (new_largest, total, summed)
+
+    block_row = lax.broadcasted_iota(jnp.int32, (chunk_blocks, key_chunk), 0)
+    block_col = lax.broadcasted_iota(jnp.int32, (chunk_blocks, key_chunk), 1)
+    pick = jnp.where(block_row == block_col // span_rows, 1.0, 0.0).astype(jnp.bfloat16)
+    key_place = lax.broadcasted_iota(jnp.int32, (1, key_chunk), 1)
+    key_frame = ((key_place & (span_rows - 1)) // frame_rows).astype(jnp.float32)
+    limits = [order.astype(jnp.float32) for order in orders]
+    for piece in range(chunks):
+        part = slice(piece * chunk_blocks, (piece + 1) * chunk_blocks)
+        spread = lax.dot_general(
+            meta_ref[part, :].astype(jnp.bfloat16),
+            pick,
+            (((0,), (0,)), ((), ())),
+            preferred_element_type=jnp.float32,
+        )
+        kv_copies[piece].wait()
+        for key_slot in range(2):
+            block = kv_ref[part, key_slot * span_rows : (key_slot + 1) * span_rows, :]
+            block = block.reshape(key_chunk, 2 * HD)
+            key_order = spread[key_slot : key_slot + 1]
+            live = key_frame < spread[2 + key_slot : 3 + key_slot]
+            s = scores_of(q[key_slot * slot_rows :], block[:, :HD]) * score_factor
+            for slot in range(key_slot, 2):
+                bias = jnp.where(live & (key_order < limits[slot]), 0.0, masked_low)
+                begin = (slot - key_slot) * slot_rows
+                states[slot] = fold(
+                    states[slot], s[begin : begin + slot_rows] + bias, block[:, HD:]
+                )
+
+    token = lax.broadcasted_iota(jnp.int32, (span_rows, HD), 0)
+    pieces = []
+    for slot in range(2):
+        largest, total, summed = states[slot]
+        result = summed / total
+        live_row = token < valids[slot] * frame_rows
+        pieces.append(
+            jnp.concatenate(
+                [
+                    jnp.where(live_row, result[g * span_rows : (g + 1) * span_rows], 0.0)
+                    for g in range(group)
+                ],
+                axis=1,
+            )
+        )
+    out_ref[...] = swap_spans(jnp.concatenate(pieces, axis=0), swap).astype(jnp.bfloat16)
+
+
+def attention(order, valid, queries, own, kv_all, meta):
+    smem = pl.BlockSpec(memory_space=pltpu.SMEM)
     vmem = pl.BlockSpec(memory_space=pltpu.VMEM)
     hbm = pl.BlockSpec(memory_space=pltpu.HBM)
     tokens = queries.shape[0]
@@ -199,17 +219,35 @@
     return pl.pallas_call(
         attention_kernel,
         out_shape=jax.ShapeDtypeStruct(queries.shape, jnp.bfloat16),
-        in_specs=[pl.BlockSpec(memory_space=pltpu.SMEM), vmem, vmem, hbm, vmem],
+        in_specs=[smem, smem, vmem, vmem, hbm, vmem],
         out_specs=vmem,
         scratch_shapes=[
             pltpu.VMEM((blocks, tokens, kv_cols), jnp.bfloat16),
-            pltpu.SemaphoreType.DMA((blocks * tokens // key_chunk,)),
+            pltpu.SemaphoreType.DMA((blocks * tokens // (2 * key_chunk),)),
         ],
         compiler_params=pltpu.CompilerParams(vmem_limit_bytes=28 * 1024 * 1024),
-    )(scalars, queries, own, in_hbm(kv_all), meta)
+    )(in_hbm(order), in_hbm(valid), queries, own, in_hbm(kv_all), meta)
+
+
+def ordered_spans(order_ref, valid_ref):
+    swap = order_ref[0] > order_ref[1]
+    orders = (jnp.minimum(order_ref[0], order_ref[1]), jnp.maximum(order_ref[0], order_ref[1]))
+    valids = (
+        jnp.where(swap, valid_ref[1], valid_ref[0]),
+        jnp.where(swap, valid_ref[0], valid_ref[1]),
+    )
+    return swap, orders, valids
+
+
+def swap_spans(values, swap):
+    rows = values.shape[0] // 2
+    turned = jnp.concatenate([values[rows:], values[:rows]], axis=0)
+    return jnp.where(swap, turned, values)
 
 
 def embed_kernel(
+    order_ref,
+    valid_ref,
     own_patch_ref,
     other_patch_ref,
     own_embed_ref,
@@ -263,7 +301,14 @@
     for start in range(0, width, column_chunk):
         cols = slice(start, start + column_chunk)
         wide = embedded_ref[:, cols].astype(jnp.float32)
-        normed = (wide * factor * gain_ref[:, cols].astype(jnp.float32)).astype(jnp.bfloat16)
+        gain = jnp.concatenate(
+            [
+                gain_ref[row : row + 1, :]
+                for row in range(start // 128, (start + column_chunk) // 128)
+            ],
+            axis=1,
+        )
+        normed = (wide * factor * gain.astype(jnp.float32)).astype(jnp.bfloat16)
         embedded_ref[:tokens, cols] = normed[:tokens]
         if (start + column_chunk) % piece_cols == 0:
             piece = start // piece_cols
@@ -276,20 +321,31 @@
             stores[-1].start()
         summed += jnp.dot(normed, weight_ref[cols, :], preferred_element_type=jnp.float32)
     noisy_ref[...] = summed[:tokens].astype(jnp.bfloat16)
-    clean_ref[...] = summed[tokens:].astype(jnp.bfloat16)
+    swap, orders, valids = ordered_spans(order_ref, valid_ref)
+    clean_ref[:tokens, :] = swap_spans(summed[tokens:], swap).astype(jnp.bfloat16)
+    lane = lax.broadcasted_iota(jnp.int32, (meta_rows, summed.shape[1]), 1)
+    first_row = lax.broadcasted_iota(jnp.int32, lane.shape, 0) == 0
+    table = jnp.zeros(lane.shape, jnp.float32)
+    for place, entry in enumerate(orders + valids):
+        table = jnp.where(first_row & (lane == place), entry.astype(jnp.float32), table)
+    clean_ref[tokens:, :] = table.astype(jnp.bfloat16)
     for store in stores:
         store.wait()
 
 
-def embed_tokens(own_patches, other_patches, own_embed, other_embed, position, gain, weight):
+def embed_tokens(
+    order, valid, own_patches, other_patches, own_embed, other_embed, position, gain, weight
+):
     tokens, width = position.shape
     vmem = pl.BlockSpec(memory_space=pltpu.VMEM)
     hbm = pl.BlockSpec(memory_space=pltpu.HBM)
+    smem = pl.BlockSpec(memory_space=pltpu.SMEM)
     kv_shape = jax.ShapeDtypeStruct((tokens, weight.shape[1]), jnp.bfloat16)
+    clean_shape = jax.ShapeDtypeStruct((tokens + meta_rows, weight.shape[1]), jnp.bfloat16)
     return pl.pallas_call(
         embed_kernel,
-        out_shape=(pltpu.HBM((tokens, width), jnp.bfloat16), kv_shape, kv_shape),
-        in_specs=[vmem, vmem, hbm, vmem, hbm, vmem, vmem],
+        out_shape=(pltpu.HBM((tokens, width), jnp.bfloat16), kv_shape, clean_shape),
+        in_specs=[smem, smem, vmem, vmem, hbm, vmem, hbm, vmem, vmem],
         out_specs=(hbm, vmem, vmem),
         scratch_shapes=[
             pltpu.VMEM((2 * tokens, width), jnp.bfloat16),
@@ -300,12 +356,14 @@
         ],
         compiler_params=pltpu.CompilerParams(vmem_limit_bytes=24 * 1024 * 1024),
     )(
+        in_hbm(order),
+        in_hbm(valid),
         own_patches,
         other_patches,
         in_hbm(own_embed),
         other_embed,
         in_hbm(position),
-        gain[None],
+        gain.reshape(-1, 128),
         weight,
     )
 
@@ -322,10 +380,8 @@
     query_weight,
     kv_weight,
 ):
-    slots = clean_latents.shape[0]
     core = lax.axis_index("core")
     half = embed_weight.shape[0] // 2
-    scalars = in_hbm(jnp.concatenate([core[None], timesteps, span_order, valid_frames]))
     own_embed = lax.all_gather(
         lax.dynamic_slice_in_dim(embed_weight, core * half, half, 0), HEAD, axis=1, tiled=True
     )
@@ -339,9 +395,17 @@
     kv_full = gathered[:, q_cols:].astype(jnp.bfloat16)
 
     other_embed = lax.ppermute(own_embed, "core", [(0, 1), (1, 0)])
-    own_patches, other_patches = make_patches(scalars, clean_latents, noise, own_embed)
+    own_patches, other_patches = make_patches(timesteps, clean_latents, noise, own_embed)
     normed_noisy, noisy_kv, clean_kv = embed_tokens(
-        own_patches, other_patches, own_embed, other_embed, position, norm_gain, kv_full
+        span_order,
+        valid_frames,
+        own_patches,
+        other_patches,
+        own_embed,
+        other_embed,
+        position,
+        norm_gain,
+        kv_full,
     )
 
     queries = jnp.dot(
@@ -350,15 +414,15 @@
         preferred_element_type=jnp.float32,
     ).astype(jnp.bfloat16)
 
-    tokens = clean_kv.shape[0]
-    meta = jnp.concatenate([span_order, valid_frames]).astype(jnp.float16)
-    meta_block = jnp.pad(meta[None, :], ((0, meta_rows - 1), (0, kv_cols - 2 * slots)))
-    clean = jnp.concatenate([clean_kv.astype(jnp.float16), meta_block], axis=0)
-    clean_pair = lax.all_gather(clean, "yh", axis=0)
+    slots = span_order.shape[0]
+    rows = clean_kv.shape[0]
+    clean_pair = lax.all_gather(clean_kv.astype(jnp.float16), "yh", axis=0)
     clean_all = lax.all_gather(clean_pair, ("z", "core"), axis=1, tiled=True)
-    clean_all = clean_all.reshape(-1, tokens + meta_rows, kv_cols)
-    meta_all = jnp.sum(clean_all[:, tokens:, : 2 * slots].astype(jnp.float32), axis=1)
-    return attention(scalars, queries, noisy_kv, clean_all.astype(jnp.bfloat16), meta_all)
+    clean_all = clean_all.reshape(-1, rows, kv_cols)
+    meta_all = jnp.sum(clean_all[:, rows - meta_rows :, : 2 * slots].astype(jnp.float32), axis=1)
+    return attention(
+        span_order, valid_frames, queries, noisy_kv, clean_all.astype(jnp.bfloat16), meta_all
+    )
 
 
 def solution(mesh):

time: 169 us -> 166 us (0.982)
    pallas_call x1, Pallas kernels: 9.39 us -> 7.47 us  [attention(): pl.pallas_call(attention_kernel, out_shape=jax.ShapeDtypeStruct(queries.s...]
  transfers between devices with their start and end apart: 2 -> 2, of which waited for: 0 -> 0; matrix products, arithmetic and copies ran while one was open for 3% -> 2% of each run, Pallas kernels for 1% -> 1%
where the time goes in v6:
time: 166 us
  blocking collectives  124 us (75%)
  Pallas kernels  16.8 us (10%)
  between operations  13.5 us (8%)
  other arithmetic  6.37 us (4%)
  starting transfers between devices  2.17 us (1%)
  local copies, waits for them, and re-layouts  1.69 us (1%)
    all_gather x1, blocking collectives, on_device(): gathered = lax.all_gather(weights_pair, ('z', 'core'), axis=1, tiled=True)  66.9 us
    all_gather x1, blocking collectives, on_device(): clean_all = lax.all_gather(clean_pair, ('z', 'core'), axis=1, tiled=True)  45.2 us
    pallas_call x1, Pallas kernels, attention(): pl.pallas_call(attention_kernel, out_shape=jax.ShapeDtypeStruct(queries.s...  7.47 us
    pallas_call x1, Pallas kernels, embed_tokens(): pl.pallas_call(embed_kernel, out_shape=(pltpu.HBM((tokens, width), jnp.bf...  6.88 us
    all_gather x1, blocking collectives, on_device(): weights_pair = lax.all_gather(weights, 'yh', axis=0)  6.67 us
    all_gather x1, blocking collectives, on_device(): clean_pair = lax.all_gather(clean_kv.astype(jnp.float16), 'yh', axis=0)  5.34 us
  transfers between devices with their start and end apart: 2, of which 0 were waited for; matrix products, arithmetic and copies ran while one was open for 2% of the time, Pallas kernels for 1%

profile of v6, /device:TPU:1, one launch (start us, length us, event | category | flops | bytes accessed | tf_op | source)
XLA Modules:
  0.0 165.6 jit_solution(12362653898701197869)
XLA Ops:
  6.5 0.0 copy-start
  6.5 0.0 all-gather.5.cloned.1.call-start
  6.5 1.0 copy-done
  7.5 0.7 constant_dynamic-slice_fusion
  8.2 0.0 all-gather.5.cloned.1.call-update
  8.2 0.9 maximum_convert_fusion
  9.2 6.7 %all_gather.19 = f16[2,96,640]{2,1,0:T(8,128)(2,1)S(1)} all-gather(f16[1,96,640]{2,1,0:T(8,128)(2,1)S(1)} %maximum_convert_fusion), channel_id=1, replica_groups=mesh['yh'=2,'z'=16,'core'=2,'x'=4,'yl'=2] {'yh'}, dimensions={0}, use_global_device_ids=true | all-gather | bytes 368640 | tf_op jit(solution)/shard_map/all_gather | solution.py:391
  15.9 66.9 %all-gather.6 = f16[2,3072,640]{2,1,0:T(8,128)(2,1)} all-gather(f16[2,96,640]{2,1,0:T(8,128)(2,1)S(1)} %all_gather.19), channel_id=1, replica_groups=mesh['yh'=2,'z'=16,'core'=2,'x'=4,'yl'=2] {'z','core'}, dimensions={1}, use_global_device_ids=true | all-gather | bytes 8110080 | tf_op jit(solution)/shard_map/all_gather | solution.py:392
  82.8 0.0 copy-start.1
  82.8 0.0 all-gather.5.cloned.1.call-done.after_ref.own_embed_ref
  82.8 2.2 %collective-permute-start = (bf16[128,6144]{1,0:T(8,128)(2,1)}, bf16[128,6144]{1,0:T(8,128)(2,1)S(1)}, u32[]{:S(2)}, u32[]{:S(2)}) collective-permute-start(bf16[128,6144]{1,0:T(8,128)(2,1)} %all-gather.5.cloned.1.call-done.after_ref.own_embed_ref), channel_id=1, source_target_pairs={{0,8},{8,0},{1,9},{9,1},{2,10},{10,2},{3,11},{11,3},{4,12},{12,4},... | collective-permute-start | bytes 4718600 | tf_op jit(solution)/shard_map/ppermute | solution.py:397
  84.9 2.4 %shard_map.100 = (bf16[256,128]{1,0:T(8,128)(2,1)S(1)}, bf16[256,128]{1,0:T(8,128)(2,1)S(1)}) custom-call(s32[2]{0:T(128)} %time_ref.1, bf16[64,128]{1,0:T(8,128)(2,1)} %bitcast.19, bf16[64,128]{1,0:T(8,128)(2,1)} %bitcast.20, bf16[128,6144]{1,0:T(8,128)(2,1)} %all-gather.5.cloned.1.call-done.after_ref.own_embed_ref), custom_call_target="tpu_custom_call" | custom-call | tf_op jit(solution)/shard_map/pallas_call | solution.py:76
  87.3 2.4 %slice_convert_fusion.2.weight_ref = bf16[6144,256]{1,0:T(8,128)(2,1)S(1)} fusion(f16[6144,640]{1,0:T(8,128)(2,1)} %bitcast.12), kind=kLoop, calls=%fused_computation.2 | loop fusion | flops 1572864 | bytes 6291456 | tf_op jit(solution)/shard_map/convert_element_type | solution.py:395
  89.7 0.0 collective-permute-done.other_embed_ref
  89.7 0.0 copy-done.1
  89.8 0.0 slice-start
  89.8 6.9 %shard_map.101 = (bf16[128,6144]{1,0:T(8,128)(2,1)}, bf16[128,256]{1,0:T(8,128)(2,1)S(1)}, bf16[136,256]{1,0:T(8,128)(2,1)S(1)}) custom-call(s32[2]{0:T(128)} %order_ref.3, s32[2]{0:T(128)} %valid_ref.3, bf16[256,128]{1,0:T(8,128)(2,1)S(1)} %get-tuple-element.13.own_patch_ref, bf16[256,128]{1,0:T(8,128)(2,1)S(1)} %get-tuple-element.14.other_patch_ref, ...), custom_call_target="tpu_custom_call" | custom-call | tf_op jit(solution)/shard_map/pallas_call | solution.py:345
  96.7 5.3 %all-gather = f16[272,256]{1,0:T(8,128)(2,1)S(1)} all-gather(f16[136,256]{1,0:T(8,128)(2,1)S(1)} %convert_element_type.32), channel_id=2, replica_groups=mesh['yh'=2,'z'=16,'core'=2,'x'=4,'yl'=2] {'yh'}, dimensions={0}, use_global_device_ids=true | all-gather | bytes 208896 | tf_op jit(solution)/shard_map/all_gather | solution.py:419
  102.0 0.0 slice-start.1
  102.0 45.2 %all-gather.7 = f16[2,4352,256]{2,1,0:T(8,128)(2,1)S(1)} all-gather(f16[2,136,256]{2,1,0:T(8,128)(2,1)S(1)} %bitcast.16), channel_id=1, replica_groups=mesh['yh'=2,'z'=16,'core'=2,'x'=4,'yl'=2] {'z','core'}, dimensions={1}, use_global_device_ids=true | all-gather | bytes 4595712 | tf_op jit(solution)/shard_map/all_gather | solution.py:420
  147.2 0.1 convert_reduce_fusion.meta_ref
  147.3 0.0 copy-start.2
  147.3 2.9 %convert_element_type.33.kv_hbm = bf16[64,136,256]{2,1,0:T(8,128)(2,1)} convert(f16[64,136,256]{2,1,0:T(8,128)(2,1)S(1)} %bitcast.11) | non-fusion elementwise | flops 2228224 | bytes 8912896 | tf_op jit(solution)/shard_map/convert_element_type | solution.py:424
  150.2 0.0 slice-done
  150.2 0.0 slice-done.1
  150.2 0.0 copy-done.2
  150.3 1.0 fusion.1.query_ref
  151.2 7.5 %shard_map.102 = bf16[128,384]{1,0:T(8,128)(2,1)} custom-call(s32[2]{0:T(128)} %order_ref.3, s32[2]{0:T(128)} %valid_ref.3, bf16[128,384]{1,0:T(8,128)(2,1)S(1)} %fusion.1.query_ref, bf16[128,256]{1,0:T(8,128)(2,1)S(1)} %get-tuple-element.17.own_ref, bf16[64,136,256]{2,1,0:T(8,128)(2,1)} %convert_element_type.33.kv_hbm, f32[64,4]{1,0:T(8,128)S(1)} %convert_reduce_fusion.meta_ref), custom_call_target="tpu_custom_call" | custom-call | tf_op jit(solution)/shard_map/pallas_call | solution.py:219
  (2 shorter events, 0.0 us)
Async XLA Ops:
  6.5 1.0 copy-start
  6.5 76.2 %all-gather.5.cloned.1.call-start = ((), (), s32[]{:S(2)}) async-start(), calls=%async_computation | async-start | bytes 1769472 | tf_op jit(solution)/shard_map/all_gather | solution.py:385
  82.8 7.0 %copy-start.1 = (bf16[6144]{0:T(1024)(128)(2,1)S(1)}, bf16[6144]{0:T(1024)(128)(2,1)}, u32[]{:S(2)}) copy-start(bf16[6144]{0:T(1024)(128)(2,1)} %param.17) | copy-start | bytes 36868
  82.8 7.0 %collective-permute-start = (bf16[128,6144]{1,0:T(8,128)(2,1)}, bf16[128,6144]{1,0:T(8,128)(2,1)S(1)}, u32[]{:S(2)}, u32[]{:S(2)}) collective-permute-start(bf16[128,6144]{1,0:T(8,128)(2,1)} %all-gather.5.cloned.1.call-done.after_ref.own_embed_ref), channel_id=1, source_target_pairs={{0,8},{8,0},{1,9},{9,1},{2,10},{10,2},{3,11},{11,3},{4,12},{12,4},... | collective-permute-start | bytes 4718600 | tf_op jit(solution)/shard_map/ppermute | solution.py:397
  89.8 60.5 %slice-start = ((s8[7864320]{0:T(1024)(128)(4,1)}), s8[4194304]{0:T(1024)(128)(4,1)S(1)}, s32[]{:S(2)}) async-start(s8[7864320]{0:T(1024)(128)(4,1)} %bitcast.13), calls=%async_computation.1 | async-start | bytes 8388608
  102.0 48.2 %slice-start.1 = ((s8[7864320]{0:T(1024)(128)(4,1)}), s8[3670016]{0:T(1024)(128)(4,1)S(1)}, s32[]{:S(2)}) async-start(s8[7864320]{0:T(1024)(128)(4,1)} %bitcast.13), calls=%async_computation.2 | async-start | bytes 7340032
  147.3 3.0 %copy-start.2 = (bf16[128,6144]{1,0:T(8,128)(2,1)S(1)}, bf16[128,6144]{1,0:T(8,128)(2,1)}, u32[]{:S(2)}) copy-start(bf16[128,6144]{1,0:T(8,128)(2,1)} %get-tuple-element.16) | copy-start | bytes 4718596
Sparse Core Ops, SparseCore 0:
  9.4 54.2 all-gather.4

commit v7 on v6

--- a/solution.py
+++ b/solution.py
@@ -19,8 +19,35 @@
     return pltpu.with_memory_space_constraint(array, pltpu.HBM)
 
 
+def ordered_spans(order_ref, valid_ref):
+    swap = order_ref[0] > order_ref[1]
+    orders = (jnp.minimum(order_ref[0], order_ref[1]), jnp.maximum(order_ref[0], order_ref[1]))
+    valids = (
+        jnp.where(swap, valid_ref[1], valid_ref[0]),
+        jnp.where(swap, valid_ref[0], valid_ref[1]),
+    )
+    return swap, orders, valids
+
+
+def swap_spans(values, swap):
+    rows = values.shape[0] // 2
+    turned = jnp.concatenate([values[rows:], values[:rows]], axis=0)
+    return jnp.where(swap, turned, values)
+
+
 def patch_kernel(
-    time_ref, clean_hbm, noise_hbm, after_ref, own_ref, other_ref, clean_ref, noise_ref, sems
+    time_ref,
+    order_ref,
+    valid_ref,
+    clean_hbm,
+    noise_hbm,
+    after_ref,
+    own_ref,
+    other_ref,
+    plan_ref,
+    clean_ref,
+    noise_ref,
+    sems,
 ):
     del after_ref
     loads = [
@@ -65,9 +92,17 @@
     upper = lax.axis_index("core") == 1
     own_ref[...] = jnp.where(upper, patches[:, half:], patches[:, :half])
     other_ref[...] = jnp.where(upper, patches[:, :half], patches[:, half:])
-
-
-def make_patches(timesteps, clean_latents, noise, after):
+    swap, orders, valids = ordered_spans(order_ref, valid_ref)
+    lane = lax.broadcasted_iota(jnp.int32, plan_ref.shape, 1)
+    plan_row = lax.broadcasted_iota(jnp.int32, plan_ref.shape, 0)
+    plan = jnp.where(plan_row == 1, jnp.where(swap, 1.0, 0.0), 0.0)
+    for place, entry in enumerate(orders + valids):
+        plan = jnp.where((plan_row == 0) & (lane == place), entry.astype(jnp.float32), plan)
+    plan_ref[...] = plan
+
+
+def make_patches(timesteps, order, valid, clean_latents, noise, after):
+    smem = pl.BlockSpec(memory_space=pltpu.SMEM)
     flat = clean_latents.shape[-1]
     rows = clean_latents.size // flat
     hbm = pl.BlockSpec(memory_space=pltpu.HBM)
@@ -75,9 +110,9 @@
     shape = jax.ShapeDtypeStruct((256, 128), jnp.bfloat16)
     return pl.pallas_call(
         patch_kernel,
-        out_shape=(shape, shape),
-        in_specs=[pl.BlockSpec(memory_space=pltpu.SMEM), hbm, hbm, hbm],
-        out_specs=(vmem, vmem),
+        out_shape=(shape, shape, jax.ShapeDtypeStruct((meta_rows, 256), jnp.float32)),
+        in_specs=[smem, smem, smem, hbm, hbm, hbm],
+        out_specs=(vmem, vmem, vmem),
         scratch_shapes=[
             pltpu.VMEM((rows, flat), jnp.bfloat16),
             pltpu.VMEM((rows, flat), jnp.bfloat16),
@@ -86,6 +121,8 @@
         compiler_params=pltpu.CompilerParams(vmem_limit_bytes=8 * 1024 * 1024),
     )(
         in_hbm(timesteps),
+        in_hbm(order),
+        in_hbm(valid),
         in_hbm(clean_latents.reshape(rows, flat)),
         in_hbm(noise.reshape(rows, flat)),
         in_hbm(after),
@@ -102,7 +139,7 @@
 
 
 def attention_kernel(
-    order_ref, valid_ref, query_ref, own_ref, kv_hbm, meta_ref, out_ref, kv_ref, kv_sems
+    order_ref, valid_ref, query_ref, own_ref, kv_ref, meta_ref, out_ref
 ):
     tokens = query_ref.shape[0]
     group = query_ref.shape[1] // HD
@@ -110,15 +147,6 @@
     frame_rows = span_rows // 4
     chunk_blocks = key_chunk // span_rows
     chunks = kv_ref.shape[0] // chunk_blocks
-    kv_copies = []
-    for piece in range(chunks):
-        part = pl.ds(piece * chunk_blocks, chunk_blocks)
-        kv_copies.append(
-            pltpu.make_async_copy(
-                kv_hbm.at[part, pl.ds(0, tokens)], kv_ref.at[part], kv_sems.at[piece]
-            )
-        )
-        kv_copies[-1].start()
     swap, orders, valids = ordered_spans(order_ref, valid_ref)
     queries = swap_spans(query_ref[...], swap)
     own = swap_spans(own_ref[...], swap)
@@ -178,7 +206,6 @@
             (((0,), (0,)), ((), ())),
             preferred_element_type=jnp.float32,
         )
-        kv_copies[piece].wait()
         for key_slot in range(2):
             block = kv_ref[part, key_slot * span_rows : (key_slot + 1) * span_rows, :]
             block = block.reshape(key_chunk, 2 * HD)
@@ -213,41 +240,17 @@
 def attention(order, valid, queries, own, kv_all, meta):
     smem = pl.BlockSpec(memory_space=pltpu.SMEM)
     vmem = pl.BlockSpec(memory_space=pltpu.VMEM)
-    hbm = pl.BlockSpec(memory_space=pltpu.HBM)
-    tokens = queries.shape[0]
-    blocks, unused, kv_cols = kv_all.shape
     return pl.pallas_call(
         attention_kernel,
         out_shape=jax.ShapeDtypeStruct(queries.shape, jnp.bfloat16),
-        in_specs=[smem, smem, vmem, vmem, hbm, vmem],
+        in_specs=[smem, smem, vmem, vmem, vmem, vmem],
         out_specs=vmem,
-        scratch_shapes=[
-            pltpu.VMEM((blocks, tokens, kv_cols), jnp.bfloat16),
-            pltpu.SemaphoreType.DMA((blocks * tokens // (2 * key_chunk),)),
-        ],
-        compiler_params=pltpu.CompilerParams(vmem_limit_bytes=28 * 1024 * 1024),
-    )(in_hbm(order), in_hbm(valid), queries, own, in_hbm(kv_all), meta)
-
-
-def ordered_spans(order_ref, valid_ref):
-    swap = order_ref[0] > order_ref[1]
-    orders = (jnp.minimum(order_ref[0], order_ref[1]), jnp.maximum(order_ref[0], order_ref[1]))
-    valids = (
-        jnp.where(swap, valid_ref[1], valid_ref[0]),
-        jnp.where(swap, valid_ref[0], valid_ref[1]),
-    )
-    return swap, orders, valids
-
-
-def swap_spans(values, swap):
-    rows = values.shape[0] // 2
-    turned = jnp.concatenate([values[rows:], values[:rows]], axis=0)
-    return jnp.where(swap, turned, values)
+        compiler_params=pltpu.CompilerParams(vmem_limit_bytes=16 * 1024 * 1024),
+    )(in_hbm(order), in_hbm(valid), queries, own, kv_all, meta)
 
 
 def embed_kernel(
-    order_ref,
-    valid_ref,
+    plan_ref,
     own_patch_ref,
     other_patch_ref,
     own_embed_ref,
@@ -321,31 +324,26 @@
             stores[-1].start()
         summed += jnp.dot(normed, weight_ref[cols, :], preferred_element_type=jnp.float32)
     noisy_ref[...] = summed[:tokens].astype(jnp.bfloat16)
-    swap, orders, valids = ordered_spans(order_ref, valid_ref)
+    swap = plan_ref[1:2, :] > 0.5
     clean_ref[:tokens, :] = swap_spans(summed[tokens:], swap).astype(jnp.bfloat16)
-    lane = lax.broadcasted_iota(jnp.int32, (meta_rows, summed.shape[1]), 1)
-    first_row = lax.broadcasted_iota(jnp.int32, lane.shape, 0) == 0
-    table = jnp.zeros(lane.shape, jnp.float32)
-    for place, entry in enumerate(orders + valids):
-        table = jnp.where(first_row & (lane == place), entry.astype(jnp.float32), table)
-    clean_ref[tokens:, :] = table.astype(jnp.bfloat16)
+    first_row = lax.broadcasted_iota(jnp.int32, plan_ref.shape, 0) == 0
+    clean_ref[tokens:, :] = jnp.where(first_row, plan_ref[...], 0.0).astype(jnp.bfloat16)
     for store in stores:
         store.wait()
 
 
 def embed_tokens(
-    order, valid, own_patches, other_patches, own_embed, other_embed, position, gain, weight
+    plan, own_patches, other_patches, own_embed, other_embed, position, gain, weight
 ):
     tokens, width = position.shape
     vmem = pl.BlockSpec(memory_space=pltpu.VMEM)
     hbm = pl.BlockSpec(memory_space=pltpu.HBM)
-    smem = pl.BlockSpec(memory_space=pltpu.SMEM)
     kv_shape = jax.ShapeDtypeStruct((tokens, weight.shape[1]), jnp.bfloat16)
     clean_shape = jax.ShapeDtypeStruct((tokens + meta_rows, weight.shape[1]), jnp.bfloat16)
     return pl.pallas_call(
         embed_kernel,
         out_shape=(pltpu.HBM((tokens, width), jnp.bfloat16), kv_shape, clean_shape),
-        in_specs=[smem, smem, vmem, vmem, hbm, vmem, hbm, vmem, vmem],
+        in_specs=[vmem, vmem, vmem, hbm, vmem, hbm, vmem, vmem],
         out_specs=(hbm, vmem, vmem),
         scratch_shapes=[
             pltpu.VMEM((2 * tokens, width), jnp.bfloat16),
@@ -356,8 +354,7 @@
         ],
         compiler_params=pltpu.CompilerParams(vmem_limit_bytes=24 * 1024 * 1024),
     )(
-        in_hbm(order),
-        in_hbm(valid),
+        plan,
         own_patches,
         other_patches,
         in_hbm(own_embed),
@@ -395,10 +392,11 @@
     kv_full = gathered[:, q_cols:].astype(jnp.bfloat16)
 
     other_embed = lax.ppermute(own_embed, "core", [(0, 1), (1, 0)])
-    own_patches, other_patches = make_patches(timesteps, clean_latents, noise, own_embed)
+    own_patches, other_patches, plan = make_patches(
+        timesteps, span_order, valid_frames, clean_latents, noise, own_embed
+    )
     normed_noisy, noisy_kv, clean_kv = embed_tokens(
-        span_order,
-        valid_frames,
+        plan,
         own_patches,
         other_patches,
         own_embed,

time: 166 us -> 162 us (0.976)
  other arithmetic: 6.37 us -> 4.3 us
  Pallas kernels: 16.8 us -> 14.8 us
    convert_element_type x1, other arithmetic: 2.94 us -> 0.87 us  [on_device(): clean_all.astype(jnp.bfloat16)]
where the time goes in v7:
time: 162 us
  blocking collectives  124 us (77%)
  Pallas kernels  14.8 us (9%)
  between operations  13.5 us (8%)
  other arithmetic  4.3 us (3%)
  local copies, waits for them, and re-layouts  2.19 us (1%)
  starting transfers between devices  2.17 us (1%)
    all_gather x1, blocking collectives, on_device(): gathered = lax.all_gather(weights_pair, ('z', 'core'), axis=1, tiled=True)  66.9 us
    all_gather x1, blocking collectives, on_device(): clean_all = lax.all_gather(clean_pair, ('z', 'core'), axis=1, tiled=True)  45.2 us
    all_gather x1, blocking collectives, on_device(): weights_pair = lax.all_gather(weights, 'yh', axis=0)  6.67 us
    pallas_call x1, Pallas kernels, attention(): pl.pallas_call(attention_kernel, out_shape=jax.ShapeDtypeStruct(queries.s...  6.54 us
    pallas_call x1, Pallas kernels, embed_tokens(): pl.pallas_call(embed_kernel, out_shape=(pltpu.HBM((tokens, width), jnp.bf...  5.86 us
    all_gather x1, blocking collectives, on_device(): clean_pair = lax.all_gather(clean_kv.astype(jnp.float16), 'yh', axis=0)  5.34 us
  transfers between devices with their start and end apart: 2, of which 0 were waited for; matrix products, arithmetic and copies ran while one was open for 2% of the time, Pallas kernels for 1%

profile of v7, /device:TPU:1, one launch (start us, length us, event | category | flops | bytes accessed | tf_op | source)
XLA Modules:
  0.0 162.1 jit_solution(1203813321343360294)
XLA Ops:
  6.5 0.0 copy-start
  6.5 0.0 all-gather.5.cloned.1.call-start
  6.5 1.0 copy-done
  7.5 0.7 constant_dynamic-slice_fusion
  8.2 0.0 all-gather.5.cloned.1.call-update
  8.2 0.9 maximum_convert_fusion
  9.2 6.7 %all_gather.19 = f16[2,96,640]{2,1,0:T(8,128)(2,1)S(1)} all-gather(f16[1,96,640]{2,1,0:T(8,128)(2,1)S(1)} %maximum_convert_fusion), channel_id=1, replica_groups=mesh['yh'=2,'z'=16,'core'=2,'x'=4,'yl'=2] {'yh'}, dimensions={0}, use_global_device_ids=true | all-gather | bytes 368640 | tf_op jit(solution)/shard_map/all_gather | solution.py:388
  15.9 66.9 %all-gather.6 = f16[2,3072,640]{2,1,0:T(8,128)(2,1)} all-gather(f16[2,96,640]{2,1,0:T(8,128)(2,1)S(1)} %all_gather.19), channel_id=1, replica_groups=mesh['yh'=2,'z'=16,'core'=2,'x'=4,'yl'=2] {'z','core'}, dimensions={1}, use_global_device_ids=true | all-gather | bytes 8110080 | tf_op jit(solution)/shard_map/all_gather | solution.py:389
  82.8 0.0 copy-start.1
  82.8 0.0 all-gather.5.cloned.1.call-done.after_ref.own_embed_ref
  82.8 2.2 %collective-permute-start = (bf16[128,6144]{1,0:T(8,128)(2,1)}, bf16[128,6144]{1,0:T(8,128)(2,1)S(1)}, u32[]{:S(2)}, u32[]{:S(2)}) collective-permute-start(bf16[128,6144]{1,0:T(8,128)(2,1)} %all-gather.5.cloned.1.call-done.after_ref.own_embed_ref), channel_id=1, source_target_pairs={{0,8},{8,0},{1,9},{9,1},{2,10},{10,2},{3,11},{11,3},{4,12},{12,4},... | collective-permute-start | bytes 4718600 | tf_op jit(solution)/shard_map/ppermute | solution.py:394
  84.9 2.4 %shard_map.100 = (bf16[256,128]{1,0:T(8,128)(2,1)S(1)}, bf16[256,128]{1,0:T(8,128)(2,1)S(1)}, f32[8,256]{1,0:T(8,128)S(1)}) custom-call(s32[2]{0:T(128)} %time_ref.1, s32[2]{0:T(128)} %order_ref.3, s32[2]{0:T(128)} %valid_ref.3, bf16[64,128]{1,0:T(8,128)(2,1)} %bitcast.19, bf16[64,128]{1,0:T(8,128)(2,1)} %bitcast.20, ...), custom_call_target="tpu_custom_call" | custom-call | tf_op jit(solution)/shard_map/pallas_call | solution.py:111
  87.4 2.4 %slice_convert_fusion.2.weight_ref = bf16[6144,256]{1,0:T(8,128)(2,1)S(1)} fusion(f16[6144,640]{1,0:T(8,128)(2,1)} %bitcast.12), kind=kLoop, calls=%fused_computation.2 | loop fusion | flops 1572864 | bytes 6291456 | tf_op jit(solution)/shard_map/convert_element_type | solution.py:392
  89.8 0.0 collective-permute-done.other_embed_ref
  89.8 0.0 copy-done.1
  89.8 0.0 slice-start
  89.8 5.9 %shard_map.101 = (bf16[128,6144]{1,0:T(8,128)(2,1)}, bf16[128,256]{1,0:T(8,128)(2,1)S(1)}, bf16[136,256]{1,0:T(8,128)(2,1)S(1)}) custom-call(f32[8,256]{1,0:T(8,128)S(1)} %get-tuple-element.14.plan_ref, bf16[256,128]{1,0:T(8,128)(2,1)S(1)} %get-tuple-element.15.own_patch_ref, bf16[256,128]{1,0:T(8,128)(2,1)S(1)} %get-tuple-element.16.other_patch_ref, ...), custom_call_target="tpu_custom_call" | custom-call | tf_op jit(solution)/shard_map/pallas_call | solution.py:343
  95.7 5.3 %all-gather = f16[272,256]{1,0:T(8,128)(2,1)S(1)} all-gather(f16[136,256]{1,0:T(8,128)(2,1)S(1)} %convert_element_type.32), channel_id=2, replica_groups=mesh['yh'=2,'z'=16,'core'=2,'x'=4,'yl'=2] {'yh'}, dimensions={0}, use_global_device_ids=true | all-gather | bytes 208896 | tf_op jit(solution)/shard_map/all_gather | solution.py:417
  101.0 0.0 slice-start.1
  101.0 45.2 %all-gather.7 = f16[2,4352,256]{2,1,0:T(8,128)(2,1)S(1)} all-gather(f16[2,136,256]{2,1,0:T(8,128)(2,1)S(1)} %bitcast.16), channel_id=1, replica_groups=mesh['yh'=2,'z'=16,'core'=2,'x'=4,'yl'=2] {'z','core'}, dimensions={1}, use_global_device_ids=true | all-gather | bytes 4595712 | tf_op jit(solution)/shard_map/all_gather | solution.py:418
  146.2 0.1 convert_reduce_fusion.meta_ref
  146.3 0.0 copy-start.2
  146.3 0.9 convert_element_type.33.kv_ref
  147.2 0.0 slice-done
  147.2 0.0 slice-done.1
  147.2 0.5 copy-done.2
  147.7 1.0 fusion.1.query_ref
  148.7 6.5 %shard_map.102 = bf16[128,384]{1,0:T(8,128)(2,1)} custom-call(s32[2]{0:T(128)} %order_ref.3, s32[2]{0:T(128)} %valid_ref.3, bf16[128,384]{1,0:T(8,128)(2,1)S(1)} %fusion.1.query_ref, bf16[128,256]{1,0:T(8,128)(2,1)S(1)} %get-tuple-element.19.own_ref, bf16[64,136,256]{2,1,0:T(8,128)(2,1)S(1)} %convert_element_type.33.kv_ref, ...), custom_call_target="tpu_custom_call" | custom-call | tf_op jit(solution)/shard_map/pallas_call | solution.py:243
  (2 shorter events, 0.0 us)
Async XLA Ops:
  6.5 1.0 copy-start
  6.5 76.2 %all-gather.5.cloned.1.call-start = ((), (), s32[]{:S(2)}) async-start(), calls=%async_computation | async-start | bytes 1769472 | tf_op jit(solution)/shard_map/all_gather | solution.py:382
  82.8 7.0 %copy-start.1 = (bf16[6144]{0:T(1024)(128)(2,1)S(1)}, bf16[6144]{0:T(1024)(128)(2,1)}, u32[]{:S(2)}) copy-start(bf16[6144]{0:T(1024)(128)(2,1)} %param.17) | copy-start | bytes 36868
  82.8 7.0 %collective-permute-start = (bf16[128,6144]{1,0:T(8,128)(2,1)}, bf16[128,6144]{1,0:T(8,128)(2,1)S(1)}, u32[]{:S(2)}, u32[]{:S(2)}) collective-permute-start(bf16[128,6144]{1,0:T(8,128)(2,1)} %all-gather.5.cloned.1.call-done.after_ref.own_embed_ref), channel_id=1, source_target_pairs={{0,8},{8,0},{1,9},{9,1},{2,10},{10,2},{3,11},{11,3},{4,12},{12,4},... | collective-permute-start | bytes 4718600 | tf_op jit(solution)/shard_map/ppermute | solution.py:394
  89.8 57.4 %slice-start = ((s8[7864320]{0:T(1024)(128)(4,1)}), s8[4194304]{0:T(1024)(128)(4,1)S(1)}, s32[]{:S(2)}) async-start(s8[7864320]{0:T(1024)(128)(4,1)} %bitcast.13), calls=%async_computation.1 | async-start | bytes 8388608
  101.0 46.2 %slice-start.1 = ((s8[7864320]{0:T(1024)(128)(4,1)}), s8[3670016]{0:T(1024)(128)(4,1)S(1)}, s32[]{:S(2)}) async-start(s8[7864320]{0:T(1024)(128)(4,1)} %bitcast.13), calls=%async_computation.2 | async-start | bytes 7340032
  146.3 1.4 copy-start.2
Sparse Core Ops, SparseCore 0:
  9.4 54.2 all-gather.4

commit v8 on v7

--- a/solution.py
+++ b/solution.py
@@ -133,7 +133,7 @@
 HEAD = ("x", "yl")
 meta_rows = 8
 score_factor = HD ** (-0.5) * math.log2(math.e)
-key_chunk = 1024
+key_chunk = 2048
 column_chunk = 768
 embed_pieces = 4
 

time: 162 us -> 162 us (level)
  transfers between devices with their start and end apart: 2 -> 2, of which waited for: 0 -> 0; matrix products, arithmetic and copies ran while one was open for 2% -> 2% of each run, Pallas kernels for 1% -> 2%
where the time goes in v8:
time: 162 us; the launch traced here: 161 us
  blocking collectives  124 us (77%)
  Pallas kernels  14.1 us (9%)
  between operations  13.5 us (8%)
  other arithmetic  4.3 us (3%)
  local copies, waits for them, and re-layouts  2.19 us (1%)
  starting transfers between devices  2.17 us (1%)
    all_gather x1, blocking collectives, on_device(): gathered = lax.all_gather(weights_pair, ('z', 'core'), axis=1, tiled=True)  66.9 us
    all_gather x1, blocking collectives, on_device(): clean_all = lax.all_gather(clean_pair, ('z', 'core'), axis=1, tiled=True)  45.2 us
    all_gather x1, blocking collectives, on_device(): weights_pair = lax.all_gather(weights, 'yh', axis=0)  6.67 us
    pallas_call x1, Pallas kernels, embed_tokens(): pl.pallas_call(embed_kernel, out_shape=(pltpu.HBM((tokens, width), jnp.bf...  5.86 us
    pallas_call x1, Pallas kernels, attention(): pl.pallas_call(attention_kernel, out_shape=jax.ShapeDtypeStruct(queries.s...  5.81 us
    all_gather x1, blocking collectives, on_device(): clean_pair = lax.all_gather(clean_kv.astype(jnp.float16), 'yh', axis=0)  5.34 us
  transfers between devices with their start and end apart: 2, of which 0 were waited for; matrix products, arithmetic and copies ran while one was open for 2% of the time, Pallas kernels for 2%

profile of v8, /device:TPU:1, one launch (start us, length us, event | category | flops | bytes accessed | tf_op | source)
XLA Modules:
  0.0 161.3 jit_solution(6006931992405906742)
XLA Ops:
  6.5 0.0 copy-start
  6.5 0.0 all-gather.5.cloned.1.call-start
  6.5 1.0 copy-done
  7.5 0.7 constant_dynamic-slice_fusion
  8.2 0.0 all-gather.5.cloned.1.call-update
  8.2 0.9 maximum_convert_fusion
  9.2 6.7 %all_gather.19 = f16[2,96,640]{2,1,0:T(8,128)(2,1)S(1)} all-gather(f16[1,96,640]{2,1,0:T(8,128)(2,1)S(1)} %maximum_convert_fusion), channel_id=1, replica_groups=mesh['yh'=2,'z'=16,'core'=2,'x'=4,'yl'=2] {'yh'}, dimensions={0}, use_global_device_ids=true | all-gather | bytes 368640 | tf_op jit(solution)/shard_map/all_gather | solution.py:388
  15.9 66.9 %all-gather.6 = f16[2,3072,640]{2,1,0:T(8,128)(2,1)} all-gather(f16[2,96,640]{2,1,0:T(8,128)(2,1)S(1)} %all_gather.19), channel_id=1, replica_groups=mesh['yh'=2,'z'=16,'core'=2,'x'=4,'yl'=2] {'z','core'}, dimensions={1}, use_global_device_ids=true | all-gather | bytes 8110080 | tf_op jit(solution)/shard_map/all_gather | solution.py:389
  82.8 0.0 copy-start.1
  82.8 0.0 all-gather.5.cloned.1.call-done.after_ref.own_embed_ref
  82.8 2.2 %collective-permute-start = (bf16[128,6144]{1,0:T(8,128)(2,1)}, bf16[128,6144]{1,0:T(8,128)(2,1)S(1)}, u32[]{:S(2)}, u32[]{:S(2)}) collective-permute-start(bf16[128,6144]{1,0:T(8,128)(2,1)} %all-gather.5.cloned.1.call-done.after_ref.own_embed_ref), channel_id=1, source_target_pairs={{0,8},{8,0},{1,9},{9,1},{2,10},{10,2},{3,11},{11,3},{4,12},{12,4},... | collective-permute-start | bytes 4718600 | tf_op jit(solution)/shard_map/ppermute | solution.py:394
  84.9 2.4 %shard_map.100 = (bf16[256,128]{1,0:T(8,128)(2,1)S(1)}, bf16[256,128]{1,0:T(8,128)(2,1)S(1)}, f32[8,256]{1,0:T(8,128)S(1)}) custom-call(s32[2]{0:T(128)} %time_ref.1, s32[2]{0:T(128)} %order_ref.3, s32[2]{0:T(128)} %valid_ref.3, bf16[64,128]{1,0:T(8,128)(2,1)} %bitcast.19, bf16[64,128]{1,0:T(8,128)(2,1)} %bitcast.20, ...), custom_call_target="tpu_custom_call" | custom-call | tf_op jit(solution)/shard_map/pallas_call | solution.py:111
  87.4 2.4 %slice_convert_fusion.2.weight_ref = bf16[6144,256]{1,0:T(8,128)(2,1)S(1)} fusion(f16[6144,640]{1,0:T(8,128)(2,1)} %bitcast.12), kind=kLoop, calls=%fused_computation.2 | loop fusion | flops 1572864 | bytes 6291456 | tf_op jit(solution)/shard_map/convert_element_type | solution.py:392
  89.8 0.0 collective-permute-done.other_embed_ref
  89.8 0.0 copy-done.1
  89.8 0.0 slice-start
  89.8 5.9 %shard_map.101 = (bf16[128,6144]{1,0:T(8,128)(2,1)}, bf16[128,256]{1,0:T(8,128)(2,1)S(1)}, bf16[136,256]{1,0:T(8,128)(2,1)S(1)}) custom-call(f32[8,256]{1,0:T(8,128)S(1)} %get-tuple-element.14.plan_ref, bf16[256,128]{1,0:T(8,128)(2,1)S(1)} %get-tuple-element.15.own_patch_ref, bf16[256,128]{1,0:T(8,128)(2,1)S(1)} %get-tuple-element.16.other_patch_ref, ...), custom_call_target="tpu_custom_call" | custom-call | tf_op jit(solution)/shard_map/pallas_call | solution.py:343
  95.7 5.3 %all-gather = f16[272,256]{1,0:T(8,128)(2,1)S(1)} all-gather(f16[136,256]{1,0:T(8,128)(2,1)S(1)} %convert_element_type.32), channel_id=2, replica_groups=mesh['yh'=2,'z'=16,'core'=2,'x'=4,'yl'=2] {'yh'}, dimensions={0}, use_global_device_ids=true | all-gather | bytes 208896 | tf_op jit(solution)/shard_map/all_gather | solution.py:417
  101.0 0.0 slice-start.1
  101.0 45.2 %all-gather.7 = f16[2,4352,256]{2,1,0:T(8,128)(2,1)S(1)} all-gather(f16[2,136,256]{2,1,0:T(8,128)(2,1)S(1)} %bitcast.16), channel_id=1, replica_groups=mesh['yh'=2,'z'=16,'core'=2,'x'=4,'yl'=2] {'z','core'}, dimensions={1}, use_global_device_ids=true | all-gather | bytes 4595712 | tf_op jit(solution)/shard_map/all_gather | solution.py:418
  146.2 0.1 convert_reduce_fusion.meta_ref
  146.3 0.0 copy-start.2
  146.3 0.9 convert_element_type.33.kv_ref
  147.2 0.0 slice-done
  147.2 0.0 slice-done.1
  147.2 0.5 copy-done.2
  147.7 1.0 fusion.1.query_ref
  148.7 5.8 %shard_map.102 = bf16[128,384]{1,0:T(8,128)(2,1)} custom-call(s32[2]{0:T(128)} %order_ref.3, s32[2]{0:T(128)} %valid_ref.3, bf16[128,384]{1,0:T(8,128)(2,1)S(1)} %fusion.1.query_ref, bf16[128,256]{1,0:T(8,128)(2,1)S(1)} %get-tuple-element.19.own_ref, bf16[64,136,256]{2,1,0:T(8,128)(2,1)S(1)} %convert_element_type.33.kv_ref, ...), custom_call_target="tpu_custom_call" | custom-call | tf_op jit(solution)/shard_map/pallas_call | solution.py:243
  (2 shorter events, 0.0 us)
Async XLA Ops:
  6.5 1.0 copy-start
  6.5 76.2 %all-gather.5.cloned.1.call-start = ((), (), s32[]{:S(2)}) async-start(), calls=%async_computation | async-start | bytes 1769472 | tf_op jit(solution)/shard_map/all_gather | solution.py:382
  82.8 7.0 %copy-start.1 = (bf16[6144]{0:T(1024)(128)(2,1)S(1)}, bf16[6144]{0:T(1024)(128)(2,1)}, u32[]{:S(2)}) copy-start(bf16[6144]{0:T(1024)(128)(2,1)} %param.17) | copy-start | bytes 36868
  82.8 7.0 %collective-permute-start = (bf16[128,6144]{1,0:T(8,128)(2,1)}, bf16[128,6144]{1,0:T(8,128)(2,1)S(1)}, u32[]{:S(2)}, u32[]{:S(2)}) collective-permute-start(bf16[128,6144]{1,0:T(8,128)(2,1)} %all-gather.5.cloned.1.call-done.after_ref.own_embed_ref), channel_id=1, source_target_pairs={{0,8},{8,0},{1,9},{9,1},{2,10},{10,2},{3,11},{11,3},{4,12},{12,4},... | collective-permute-start | bytes 4718600 | tf_op jit(solution)/shard_map/ppermute | solution.py:394
  89.8 57.4 %slice-start = ((s8[7864320]{0:T(1024)(128)(4,1)}), s8[4194304]{0:T(1024)(128)(4,1)S(1)}, s32[]{:S(2)}) async-start(s8[7864320]{0:T(1024)(128)(4,1)} %bitcast.13), calls=%async_computation.1 | async-start | bytes 8388608
  101.0 46.2 %slice-start.1 = ((s8[7864320]{0:T(1024)(128)(4,1)}), s8[3670016]{0:T(1024)(128)(4,1)S(1)}, s32[]{:S(2)}) async-start(s8[7864320]{0:T(1024)(128)(4,1)} %bitcast.13), calls=%async_computation.2 | async-start | bytes 7340032
  146.3 1.4 copy-start.2
Sparse Core Ops, SparseCore 0:
  9.4 54.2 all-gather.4

commit v9 on v8

--- a/solution.py
+++ b/solution.py
@@ -134,7 +134,7 @@
 meta_rows = 8
 score_factor = HD ** (-0.5) * math.log2(math.e)
 key_chunk = 2048
-column_chunk = 768
+column_chunk = 1536
 embed_pieces = 4
 
 

time: 162 us -> 162 us (level)
  no operation moved by 1% of the time
where the time goes in v9:
time: 162 us; the launch traced here: 161 us
  blocking collectives  124 us (77%)
  Pallas kernels  14.1 us (9%)
  between operations  13.5 us (8%)
  other arithmetic  4.3 us (3%)
  local copies, waits for them, and re-layouts  2.19 us (1%)
  starting transfers between devices  2.17 us (1%)
    all_gather x1, blocking collectives, on_device(): gathered = lax.all_gather(weights_pair, ('z', 'core'), axis=1, tiled=True)  66.9 us
    all_gather x1, blocking collectives, on_device(): clean_all = lax.all_gather(clean_pair, ('z', 'core'), axis=1, tiled=True)  45.2 us
    all_gather x1, blocking collectives, on_device(): weights_pair = lax.all_gather(weights, 'yh', axis=0)  6.67 us
    pallas_call x1, Pallas kernels, embed_tokens(): pl.pallas_call(embed_kernel, out_shape=(pltpu.HBM((tokens, width), jnp.bf...  5.91 us
    pallas_call x1, Pallas kernels, attention(): pl.pallas_call(attention_kernel, out_shape=jax.ShapeDtypeStruct(queries.s...  5.81 us
    all_gather x1, blocking collectives, on_device(): clean_pair = lax.all_gather(clean_kv.astype(jnp.float16), 'yh', axis=0)  5.34 us
  transfers between devices with their start and end apart: 2, of which 0 were waited for; matrix products, arithmetic and copies ran while one was open for 2% of the time, Pallas kernels for 2%

profile of v9, /device:TPU:1, one launch (start us, length us, event | category | flops | bytes accessed | tf_op | source)
XLA Modules:
  0.0 161.4 jit_solution(16639817553701951375)
XLA Ops:
  6.5 0.0 copy-start
  6.5 0.0 all-gather.5.cloned.1.call-start
  6.5 1.0 copy-done
  7.5 0.7 constant_dynamic-slice_fusion
  8.2 0.0 all-gather.5.cloned.1.call-update
  8.2 0.9 maximum_convert_fusion
  9.2 6.7 %all_gather.19 = f16[2,96,640]{2,1,0:T(8,128)(2,1)S(1)} all-gather(f16[1,96,640]{2,1,0:T(8,128)(2,1)S(1)} %maximum_convert_fusion), channel_id=1, replica_groups=mesh['yh'=2,'z'=16,'core'=2,'x'=4,'yl'=2] {'yh'}, dimensions={0}, use_global_device_ids=true | all-gather | bytes 368640 | tf_op jit(solution)/shard_map/all_gather | solution.py:388
  15.9 66.9 %all-gather.6 = f16[2,3072,640]{2,1,0:T(8,128)(2,1)} all-gather(f16[2,96,640]{2,1,0:T(8,128)(2,1)S(1)} %all_gather.19), channel_id=1, replica_groups=mesh['yh'=2,'z'=16,'core'=2,'x'=4,'yl'=2] {'z','core'}, dimensions={1}, use_global_device_ids=true | all-gather | bytes 8110080 | tf_op jit(solution)/shard_map/all_gather | solution.py:389
  82.8 0.0 copy-start.1
  82.8 0.0 all-gather.5.cloned.1.call-done.after_ref.own_embed_ref
  82.8 2.2 %collective-permute-start = (bf16[128,6144]{1,0:T(8,128)(2,1)}, bf16[128,6144]{1,0:T(8,128)(2,1)S(1)}, u32[]{:S(2)}, u32[]{:S(2)}) collective-permute-start(bf16[128,6144]{1,0:T(8,128)(2,1)} %all-gather.5.cloned.1.call-done.after_ref.own_embed_ref), channel_id=1, source_target_pairs={{0,8},{8,0},{1,9},{9,1},{2,10},{10,2},{3,11},{11,3},{4,12},{12,4},... | collective-permute-start | bytes 4718600 | tf_op jit(solution)/shard_map/ppermute | solution.py:394
  84.9 2.4 %shard_map.100 = (bf16[256,128]{1,0:T(8,128)(2,1)S(1)}, bf16[256,128]{1,0:T(8,128)(2,1)S(1)}, f32[8,256]{1,0:T(8,128)S(1)}) custom-call(s32[2]{0:T(128)} %time_ref.1, s32[2]{0:T(128)} %order_ref.3, s32[2]{0:T(128)} %valid_ref.3, bf16[64,128]{1,0:T(8,128)(2,1)} %bitcast.19, bf16[64,128]{1,0:T(8,128)(2,1)} %bitcast.20, ...), custom_call_target="tpu_custom_call" | custom-call | tf_op jit(solution)/shard_map/pallas_call | solution.py:111
  87.4 2.4 %slice_convert_fusion.2.weight_ref = bf16[6144,256]{1,0:T(8,128)(2,1)S(1)} fusion(f16[6144,640]{1,0:T(8,128)(2,1)} %bitcast.12), kind=kLoop, calls=%fused_computation.2 | loop fusion | flops 1572864 | bytes 6291456 | tf_op jit(solution)/shard_map/convert_element_type | solution.py:392
  89.8 0.0 collective-permute-done.other_embed_ref
  89.8 0.0 copy-done.1
  89.8 0.0 slice-start
  89.8 5.9 %shard_map.101 = (bf16[128,6144]{1,0:T(8,128)(2,1)}, bf16[128,256]{1,0:T(8,128)(2,1)S(1)}, bf16[136,256]{1,0:T(8,128)(2,1)S(1)}) custom-call(f32[8,256]{1,0:T(8,128)S(1)} %get-tuple-element.14.plan_ref, bf16[256,128]{1,0:T(8,128)(2,1)S(1)} %get-tuple-element.15.own_patch_ref, bf16[256,128]{1,0:T(8,128)(2,1)S(1)} %get-tuple-element.16.other_patch_ref, ...), custom_call_target="tpu_custom_call" | custom-call | tf_op jit(solution)/shard_map/pallas_call | solution.py:343
  95.7 5.3 %all-gather = f16[272,256]{1,0:T(8,128)(2,1)S(1)} all-gather(f16[136,256]{1,0:T(8,128)(2,1)S(1)} %convert_element_type.32), channel_id=2, replica_groups=mesh['yh'=2,'z'=16,'core'=2,'x'=4,'yl'=2] {'yh'}, dimensions={0}, use_global_device_ids=true | all-gather | bytes 208896 | tf_op jit(solution)/shard_map/all_gather | solution.py:417
  101.1 0.0 slice-start.1
  101.1 45.2 %all-gather.7 = f16[2,4352,256]{2,1,0:T(8,128)(2,1)S(1)} all-gather(f16[2,136,256]{2,1,0:T(8,128)(2,1)S(1)} %bitcast.16), channel_id=1, replica_groups=mesh['yh'=2,'z'=16,'core'=2,'x'=4,'yl'=2] {'z','core'}, dimensions={1}, use_global_device_ids=true | all-gather | bytes 4595712 | tf_op jit(solution)/shard_map/all_gather | solution.py:418
  146.2 0.1 convert_reduce_fusion.meta_ref
  146.3 0.0 copy-start.2
  146.3 0.9 convert_element_type.33.kv_ref
  147.2 0.0 slice-done
  147.2 0.0 slice-done.1
  147.2 0.5 copy-done.2
  147.7 1.0 fusion.1.query_ref
  148.7 5.8 %shard_map.102 = bf16[128,384]{1,0:T(8,128)(2,1)} custom-call(s32[2]{0:T(128)} %order_ref.3, s32[2]{0:T(128)} %valid_ref.3, bf16[128,384]{1,0:T(8,128)(2,1)S(1)} %fusion.1.query_ref, bf16[128,256]{1,0:T(8,128)(2,1)S(1)} %get-tuple-element.19.own_ref, bf16[64,136,256]{2,1,0:T(8,128)(2,1)S(1)} %convert_element_type.33.kv_ref, ...), custom_call_target="tpu_custom_call" | custom-call | tf_op jit(solution)/shard_map/pallas_call | solution.py:243
  (2 shorter events, 0.0 us)
Async XLA Ops:
  6.5 1.0 copy-start
  6.5 76.2 %all-gather.5.cloned.1.call-start = ((), (), s32[]{:S(2)}) async-start(), calls=%async_computation | async-start | bytes 1769472 | tf_op jit(solution)/shard_map/all_gather | solution.py:382
  82.8 7.0 %copy-start.1 = (bf16[6144]{0:T(1024)(128)(2,1)S(1)}, bf16[6144]{0:T(1024)(128)(2,1)}, u32[]{:S(2)}) copy-start(bf16[6144]{0:T(1024)(128)(2,1)} %param.17) | copy-start | bytes 36868
  82.8 7.0 %collective-permute-start = (bf16[128,6144]{1,0:T(8,128)(2,1)}, bf16[128,6144]{1,0:T(8,128)(2,1)S(1)}, u32[]{:S(2)}, u32[]{:S(2)}) collective-permute-start(bf16[128,6144]{1,0:T(8,128)(2,1)} %all-gather.5.cloned.1.call-done.after_ref.own_embed_ref), channel_id=1, source_target_pairs={{0,8},{8,0},{1,9},{9,1},{2,10},{10,2},{3,11},{11,3},{4,12},{12,4},... | collective-permute-start | bytes 4718600 | tf_op jit(solution)/shard_map/ppermute | solution.py:394
  89.8 57.4 %slice-start = ((s8[7864320]{0:T(1024)(128)(4,1)}), s8[4194304]{0:T(1024)(128)(4,1)S(1)}, s32[]{:S(2)}) async-start(s8[7864320]{0:T(1024)(128)(4,1)} %bitcast.13), calls=%async_computation.1 | async-start | bytes 8388608
  101.1 46.2 %slice-start.1 = ((s8[7864320]{0:T(1024)(128)(4,1)}), s8[3670016]{0:T(1024)(128)(4,1)S(1)}, s32[]{:S(2)}) async-start(s8[7864320]{0:T(1024)(128)(4,1)} %bitcast.13), calls=%async_computation.2 | async-start | bytes 7340032
  146.3 1.4 copy-start.2
Sparse Core Ops, SparseCore 0:
  9.4 54.2 all-gather.4
